TPU v7x, 32 devices: a whole 2x2x4 slice. The times are simulated.
32 devices in a mesh: groups: 2 (over x), tile: 16 (over z, y, core).
Axes of the slice: x: 2, y: 2, z: 4, core: 2. Of those that a mesh axis runs over, the one named last changes fastest.
Arguments:
- data_halves: bfloat16 [2, 4, 256, 32, 512], P(None, None, ('groups', 'tile')), parts along dimension 2, may hold values from 0.1 to 20, as said below
- psf_taps: float32 [4, 3, 9], replicated, may hold values from 0.05 to 1
- cycle_map: int32 [32, 32, 512], P(('groups', 'tile')), parts along dimension 0, may hold values from 0 to 255, as said below
- cutoff: int32 [2], P('groups'), parts along dimension 0, may hold values from 64 to 255
Outputs:
- joined: float32 [256, 32, 512], P(('groups', 'tile')), parts along dimension 0
There are 2 independent parts, one for each index of `groups`. A program takes and returns all parts, laid end to end along the dimension named above; an argument that names none is the same for every part. Nothing has to cross between parts.
Inputs may be any that keep to these rules, and one draw needn't show every extreme that they name: `data_halves`: positive photon counts. cycle_map[b, k, l] is the cycle of frequency (k, l) in block b: with fk = min(k, 32 - k), fl = min(l, 512 - l) and a whole stretch s_b of 1 to 4 drawn for each block, the largest r with r * r <= (s_b fk)^2 + fl^2, capped at 255.
All inputs are finite; a program needn't handle non-finite values.
Results may differ from a plain program's by a relative error of at most 0.00095.
The roundings to bfloat16 on the way count: a program that leaves them out, or rounds other values in their place, can miss the bound.
Values may be sent and summed in bfloat16 or wider, within the bound.
No kernel may reach another device: no remote copies, remote signals or barrier semaphores. Data moves between devices by JAX's collectives and lax.ppermute only.
A program may use at most 64 MiB of HBM per device.

v0:
```python
import jax
import jax.numpy as jnp
import numpy as np
from jax import lax
from jax.experimental import pallas as pl
from jax.experimental.pallas import tpu as pltpu
from jax.sharding import PartitionSpec as P

CYCLES = 256
BF = jnp.bfloat16
F32 = jnp.float32
VMEM_LIMIT = 32 * 1024 * 1024


def dot(a, b):
    return lax.dot_general(a, b, (((1,), (0,)), ((), ())), preferred_element_type=F32)


def iota(shape, dim):
    return lax.broadcasted_iota(jnp.int32, shape, dim)


def lookup(index, values):
    total = jnp.zeros(index.shape, F32)
    for place, value in values:
        total = jnp.where(index == place, value, total)
    return total


def shift_rows(x, by):
    count = x.shape[0]
    if by == 0:
        return x
    pad = jnp.zeros((abs(by), x.shape[1]), x.dtype)
    if by > 0:
        return jnp.concatenate([x[by:], pad], axis=0)
    return jnp.concatenate([pad, x[: count + by]], axis=0)


def prep_kernel(views, taps, slab, depth, lateral):
    radius = taps // 2
    group = 128 // depth
    ext = slab + 2 * radius
    rows = slab * depth
    scale = 1.0 / views

    def kernel(kern, place, a_ref, b_ref, t_ref, c_ref, tt_ref, ct_ref, base_ref, off_ref, row_ref, w_ref, one0_ref, one1_ref):
        first, rows_total = place[0], place[1]

        def tap(v, axis, t):
            return kern[(v * 3 + axis) * taps + t]

        def ones(v, axis, index, count, flip):
            summed = jnp.zeros(index.shape, F32)
            for t in range(taps):
                source = index + t - radius
                ok = (source >= 0) & (source < count)
                summed = summed + jnp.where(ok, tap(v, axis, taps - 1 - t if flip else t), 0.0)
            return summed

        row = iota((depth, 128), 0)
        lane = iota((depth, 128), 1)
        cell = lax.rem(lane, depth)
        slot = lane // depth
        gap_z = cell - row + radius
        gap_zt = row - cell + radius
        gap = iota((128, 128), 0) - iota((128, 128), 1) + radius
        upper_gap = gap[120:128] - 128
        lower_gap = gap[0:8] + 128
        zero = jnp.zeros((depth, 128), BF)
        flat = jnp.zeros((128, 128), BF)
        tail = jnp.zeros((120, 128), F32)
        gains = []
        for v in range(views):
            band_z = lookup(gap_z, [(t, tap(v, 1, t)) for t in range(taps)])
            band_zt = lookup(gap_zt, [(t, tap(v, 1, t)) for t in range(taps)])

            def lane_taps(shift, sign, v=v):
                pairs = [(j, shift + sign * j) for j in range(group)]
                pairs = [(j, tap(v, 0, t)) for j, t in pairs if 0 <= t < taps]
                return lookup(slot, pairs) if pairs else None

            blocks = {}
            for i in range(slab):
                for g in range(ext * depth // 128):
                    d = group * g - i
                    if d not in blocks:
                        weight = lane_taps(d, 1)
                        blocks[d] = zero if weight is None else (weight * band_z).astype(BF)
                    a_ref[pl.ds((v * slab + i) * depth, depth), pl.ds(g * 128, 128)] = blocks[d]
            blocks = {}
            for i in range(ext):
                for g in range(rows // 128):
                    d = i - group * g
                    if d not in blocks:
                        weight = lane_taps(d, -1)
                        blocks[d] = zero if weight is None else (weight * band_zt).astype(BF)
                    b_ref[pl.ds(i * depth, depth), pl.ds(v * rows + g * 128, 128)] = blocks[d]

            for flip, band_ref, cross_ref in ((False, t_ref, c_ref), (True, tt_ref, ct_ref)):
                pairs = [(t, tap(v, 2, taps - 1 - t if flip else t)) for t in range(taps)]
                middle = lookup(gap, pairs).astype(BF)
                upper = jnp.concatenate([tail, lookup(upper_gap, pairs[:radius])], axis=0).astype(BF)
                lower = jnp.concatenate([lookup(lower_gap, pairs[radius + 1 :]), tail], axis=0).astype(BF)
                for at, block in ((0, middle), (1, upper), (2, lower), (3, middle)):
                    at_rows, at_cols = pl.ds(at // 2 * 128, 128), pl.ds(at % 2 * 128, 128)
                    band_ref[v, at_rows, at_cols] = block
                    cross_ref[v, at_rows, at_cols] = flat if at in (0, 3) else block

            mid = depth // 2
            sum_xz = jnp.sum(
                a_ref[pl.ds(v * rows, depth), :].astype(F32)[mid : mid + 1], axis=1, keepdims=True
            )
            sum_y = jnp.sum(t_ref[v, 0:128, :].astype(F32)[64:65], axis=1, keepdims=True)
            gains.append(1.0 / (sum_xz * sum_y))

        def blur_z(v, x, flip):
            total = None
            for t in range(taps):
                term = shift_rows(x, t - radius) * tap(v, 1, taps - 1 - t if flip else t)
                total = term if total is None else total + term
            return total

        field0 = [ones(v, 1, row, depth, False) for v in range(views)]
        back0 = [blur_z(v, 1.0 / field0[v], True) for v in range(views)]
        shape = back0[0]
        for v in range(1, views):
            shape = shape + back0[v]
        shape = shape * scale
        w_ref[...] = shape
        field1 = [blur_z(v, shape, False) for v in range(views)]
        back1 = [blur_z(v, 1.0 / field1[v], True) for v in range(views)]

        x_out = iota((slab, 128), 0) + first
        x_ext = iota((ext, 128), 0) + (first - radius)
        y_row = iota((8, lateral), 1)
        edges = []
        for v in range(views):
            part_x = ones(v, 0, x_out, rows_total, False)
            for n, field in enumerate((field0, field1)):
                for i in range(slab):
                    at = pl.ds((v * slab + i) * depth, depth)
                    base_ref[n, at, :] = field[v] * part_x[i : i + 1]
                off_ref[n, v] = gains[v] / field[v]
            row_ref[v, 0] = ones(v, 2, y_row, lateral, False)
            row_ref[v, 1] = jnp.broadcast_to(gains[v], (8, lateral))
            edges.append((ones(v, 0, x_ext, rows_total, True) * scale, ones(v, 2, y_row, lateral, True)))
        for n, back, one_ref, low, high in (
            (0, back0, one0_ref, 0, ext),
            (1, back1, one1_ref, radius, radius + slab),
        ):
            for e in range(low, high):
                terms = [back[v] * edges[v][0][e : e + 1] for v in range(views)]
                for j in range(lateral // 128):
                    total = None
                    for v in range(views):
                        term = terms[v]
                        if j in (0, lateral // 128 - 1):
                            term = term * edges[v][1][0:1, j * 128 : (j + 1) * 128]
                        total = term if total is None else total + term
                    one_ref[pl.ds((e - low) * depth, depth), pl.ds(j * 128, 128)] = total

    return kernel


def y_blur(x, band, cross):
    left = dot(x[:, 0:256], band)
    right = dot(x[:, 256:512], band)
    mid = dot(x[:, 128:384], cross)
    left = jnp.concatenate([left[:, 0:128], left[:, 128:256] + mid[:, 0:128]], axis=1)
    right = jnp.concatenate([right[:, 0:128] + mid[:, 128:256], right[:, 128:256]], axis=1)
    return jnp.concatenate([left, right], axis=1)


def mean_views(data_ref, views):
    total = data_ref[0, 0].astype(F32)
    for v in range(1, views):
        total = total + data_ref[0, v].astype(F32)
    return total * (1.0 / views)


def level_of(x):
    total = jnp.sum(jnp.sum(x, axis=0, keepdims=True), axis=1, keepdims=True)
    return (total * (1.0 / x.size)).astype(BF).astype(F32)


def across(x, lateral):
    return jnp.concatenate([x] * (lateral // 128), axis=1)


def blur_back(n, views, slab, rows, level, data_ref, ext, mats, held):
    a_ref, b_ref, t_ref, c_ref, tt_ref, ct_ref, base_ref, off_ref, row_ref = mats
    lateral = ext.shape[1]
    for v in range(views):
        part = dot(a_ref[pl.ds(v * rows, rows), :], ext).astype(BF)
        base = across(base_ref[n, pl.ds(v * rows, rows), :], lateral) * (row_ref[v, 0, 0:1, :] * level)
        predicted = y_blur(part, t_ref[v], c_ref[v]) + base
        scaled = data_ref[0, v].astype(F32) * row_ref[v, 1, 0:1, :]
        offset = across(jnp.concatenate([off_ref[n, v]] * slab, axis=0), lateral)
        quotient = (scaled / predicted - offset).astype(BF)
        held[pl.ds(v * rows, rows), :] = y_blur(quotient, tt_ref[v], ct_ref[v]).astype(BF)
    return dot(b_ref[...], held[...])


def pick(even, from_pair, from_other):
    pair = from_pair[0].astype(F32)
    other = from_other[0].astype(F32)
    return jnp.where(even, other, pair), jnp.where(even, pair, other)


def put(even, low, high, to_pair, to_other):
    @pl.when(even)
    def _():
        to_pair[0] = high
        to_other[0] = low

    @pl.when(jnp.logical_not(even))
    def _():
        to_pair[0] = low
        to_other[0] = high


def first_kernel(views, slab, rows, edge):
    def kernel(place, data_ref, pair_ref, other_ref, *refs):
        mats, (own_ref, to_pair, to_other, held) = refs[:9], refs[9:]
        even = place[2] == 0
        lo, hi = pick(even, pair_ref, other_ref)
        has_lo = jnp.where(place[0] > 0, 1.0, 0.0)
        has_hi = jnp.where(place[0] + slab < place[1], 1.0, 0.0)
        estimate = mean_views(data_ref, views)
        level = level_of(estimate)
        ext = jnp.concatenate([lo - level * has_lo, estimate - level, hi - level * has_hi], axis=0)
        part = blur_back(0, views, slab, rows, level, data_ref, ext.astype(BF), mats, held)
        own_ref[0] = part[edge : edge + rows]
        put(even, part[0 : 2 * edge].astype(BF), part[rows:].astype(BF), to_pair, to_other)

    return kernel


def second_kernel(views, slab, rows, edge, lateral):
    scale = 1.0 / views

    def kernel(
        place, data_ref, pair0_ref, other0_ref, own_ref, sent_pair, sent_other, pair_ref, other_ref, w_ref, one_ref, *refs
    ):
        mats, (est_ref, part_ref, to_pair, to_other, held) = refs[:9], refs[9:]
        even = place[2] == 0
        has_lo = jnp.where(place[0] > 0, 1.0, 0.0)
        has_hi = jnp.where(place[0] + slab < place[1], 1.0, 0.0)
        lo, hi = pick(even, pair0_ref, other0_ref)
        got_lo, got_hi = pick(even, pair_ref, other_ref)
        sent_lo, sent_hi = pick(even, sent_pair, sent_other)
        lo = lo * (one_ref[0:edge] + scale * (sent_lo[0:edge] + got_lo[0:edge]))
        hi = hi * (one_ref[edge + rows :] + scale * (sent_hi[edge:] + got_hi[edge:]))
        got = jnp.concatenate([got_lo[edge:], got_hi[0:edge]], axis=0)
        before = mean_views(data_ref, views)
        level = level_of(before)
        estimate = before * (one_ref[pl.ds(edge, rows)] + scale * (own_ref[0] + got))
        est_ref[0] = estimate
        shape = across(w_ref[...], lateral) * level
        shapes = jnp.concatenate([shape] * (edge // shape.shape[0]), axis=0)
        ext = jnp.concatenate(
            [
                lo - shapes * has_lo,
                estimate - jnp.concatenate([shape] * slab, axis=0),
                hi - shapes * has_hi,
            ],
            axis=0,
        )
        part = blur_back(1, views, slab, rows, level, data_ref, ext.astype(BF), mats, held)
        part_ref[0] = part[edge : edge + rows]
        put(even, part[0:edge].astype(BF), part[edge + rows :].astype(BF), to_pair, to_other)

    return kernel


def table_kernel(slab, depth, lateral):
    half = lateral // 2

    def kernel(quarter_ref, wave_ref, _, waves_ref, back_ref, high_ref, low_ref):
        steps = [jnp.broadcast_to(quarter_ref[0:1, :], (8, 128)), jnp.broadcast_to(quarter_ref[1:2, :], (8, 128))]
        for j in range(half // 128):
            lane = iota((8, 128), 1) + j * 128
            phase = (iota((8, 128), 0) * lane) & (lateral - 1)
            for i in range(lateral // 16):
                pair = []
                for _ in range(2):
                    near, turn = phase & 127, phase // 128
                    g0 = jnp.take_along_axis(steps[0], near, axis=1)
                    g1 = jnp.take_along_axis(steps[1], near, axis=1)
                    odd = (turn & 1) == 1
                    cos = jnp.where(odd, g1, g0) * jnp.where(turn >= 2, -1.0, 1.0)
                    sin = jnp.where(odd, g0, g1) * jnp.where((turn == 0) | (turn == 3), -1.0, 1.0)
                    if j == 0:
                        flip = jnp.where((iota((8, 128), 0) & 1) == 1, -1.0, 1.0)
                        sin = jnp.where(lane == 0, flip, sin)
                    pair.append((cos, sin))
                    phase = (phase + lane * 8) & (lateral - 1)
                at = pl.ds(i * 16, 16)
                waves_ref[at, pl.ds(j * 128, 128)] = jnp.concatenate([pair[0][0], pair[1][0]], axis=0).astype(BF)
                waves_ref[at, pl.ds(half + j * 128, 128)] = jnp.concatenate(
                    [pair[0][1], pair[1][1]], axis=0
                ).astype(BF)
        for j in range(lateral // 128):
            lane = iota((8, 128), 1) + j * 128
            phase = (iota((8, 128), 0) * lane) & (lateral - 1)
            for i in range(half // 16):
                pair = []
                for s in range(2):
                    near, turn = phase & 127, phase // 128
                    g0 = jnp.take_along_axis(steps[0], near, axis=1)
                    g1 = jnp.take_along_axis(steps[1], near, axis=1)
                    odd = (turn & 1) == 1
                    cos = jnp.where(odd, g1, g0) * jnp.where(turn >= 2, -1.0, 1.0)
                    sin = jnp.where(odd, g0, g1) * jnp.where((turn == 0) | (turn == 3), 1.0, -1.0)
                    if i == 0 and s == 0:
                        flip = jnp.where((lane & 1) == 1, -1.0, 1.0)
                        sin = jnp.where(iota((8, 128), 0) == 0, flip, sin)
                    pair.append((cos, sin))
                    phase = (phase + lane * 8) & (lateral - 1)
                at = pl.ds(j * 128, 128)
                back_ref[pl.ds(i * 16, 16), at] = jnp.concatenate([pair[0][0], pair[1][0]], axis=0).astype(BF)
                back_ref[pl.ds(half + i * 16, 16), at] = jnp.concatenate([pair[0][1], pair[1][1]], axis=0).astype(BF)
        slot = iota((depth, 128), 1) // depth
        group = 128 // depth
        for kind in range(2):
            wave = wave_ref[kind]
            high = wave.astype(BF).astype(F32)
            for i in range(slab):
                for g in range(slab * depth // 128):
                    at = (pl.ds((kind * slab + i) * depth, depth), pl.ds(g * 128, 128))
                    here = slot == i - group * g
                    high_ref[at] = jnp.where(here, high, 0.0).astype(BF)
                    low_ref[at] = jnp.where(here, wave - high, 0.0).astype(BF)

    return kernel


def split_dot(table_hi, table_lo, x):
    x_hi = x.astype(BF)
    x_lo = (x - x_hi.astype(F32)).astype(BF)
    return dot(table_hi, x_hi) + dot(table_hi, x_lo) + dot(table_lo, x_hi)


def spectrum(even, scale, rows, half, est_ref, part_ref, pair_ref, other_ref, one_ref, waves_ref, high_ref, low_ref):
    got_lo, got_hi = pick(even, pair_ref, other_ref)
    got = jnp.concatenate([got_lo, got_hi], axis=0)
    estimate = est_ref[0] * (one_ref[...] + scale * (part_ref[0] + got))
    row = dot(estimate.astype(BF), waves_ref[...])
    from_cos = split_dot(high_ref[...], low_ref[...], row[:, :half])
    from_sin = split_dot(high_ref[...], low_ref[...], row[:, half:])
    first = iota((rows, half), 1) == 0
    sin_cos = from_sin[:rows]
    sin_sin = from_sin[rows:]
    real = from_cos[:rows] - jnp.where(first, 0.0, sin_sin)
    imag = -from_cos[rows:] - jnp.where(first, 0.0, sin_cos)
    top = iota((rows, 128), 1) == 0
    top_real = jnp.where(top, sin_cos[:, :128], 0.0)
    top_imag = jnp.where(top, -sin_sin[:, :128], 0.0)
    return real, imag, top_real, top_imag


def spectrum_kernel(views, slab, depth, lateral):
    rows, half = slab * depth, lateral // 2

    def kernel(place, est_ref, part_ref, pair_ref, other_ref, one_ref, waves_ref, high_ref, low_ref, *outs):
        even = place[2] == 0
        args = (est_ref, part_ref, pair_ref, other_ref, one_ref, waves_ref, high_ref, low_ref)
        for ref, value in zip(outs, spectrum(even, 1.0 / views, rows, half, *args)):
            ref[...] = value

    return kernel


def power_kernel(views, slab, depth, lateral, count):
    rows, half = slab * depth, lateral // 2

    def kernel(
        place,
        est_ref,
        part_ref,
        pair_ref,
        other_ref,
        one_ref,
        waves_ref,
        high_ref,
        low_ref,
        map_ref,
        re_ref,
        im_ref,
        tre_ref,
        tim_ref,
        mre_ref,
        mim_ref,
        mtre_ref,
        mtim_ref,
        sum_ref,
    ):
        even = place[2] == 0
        args = (est_ref, part_ref, pair_ref, other_ref, one_ref, waves_ref, high_ref, low_ref)
        re1, im1, tre1, tim1 = spectrum(even, 1.0 / views, rows, half, *args)
        re0, im0, tre0, tim0 = re_ref[...], im_ref[...], tre_ref[...], tim_ref[...]
        mre_ref[...] = 0.5 * (re0 + re1)
        mim_ref[...] = 0.5 * (im0 + im1)
        mtre_ref[...] = 0.5 * (tre0 + tre1)
        mtim_ref[...] = 0.5 * (tim0 + tim1)

        def over_slab(x):
            total = x[0:depth]
            for s in range(1, slab):
                total = total + x[s * depth : (s + 1) * depth]
            return total

        twice = jnp.where(iota((depth, half), 1) == 0, 1.0, 2.0)
        powers, tops = [], []
        for a, b, c, d in (
            (re0, re1, im0, im1),
            (re0, re0, im0, im0),
            (re1, re1, im1, im1),
        ):
            powers.append(over_slab(a * b + c * d) * twice)
        for a, b, c, d in (
            (tre0, tre1, tim0, tim1),
            (tre0, tre0, tim0, tim0),
            (tre1, tre1, tim1, tim1),
        ):
            tops.append(jnp.sum(over_slab(a * b + c * d), axis=0, keepdims=True))
        top = jnp.sum(jnp.concatenate(tops, axis=0), axis=1, keepdims=True)
        total = jnp.zeros((9, CYCLES), F32)
        cycle = iota((CYCLES, half), 0)
        for k in range(depth // 2 + 1):
            other = depth - k
            terms = [p[k : k + 1] + p[other : other + 1] if 0 < k < other else p[k : k + 1] for p in powers]
            term = jnp.concatenate(terms, axis=0)
            high = term.astype(BF).astype(F32)
            middle = (term - high).astype(BF).astype(F32)
            low = term - high - middle
            term = jnp.concatenate([high, middle, low], axis=0).astype(BF)
            onehot = (map_ref[0, k : k + 1, 0:half] == cycle).astype(F32).astype(BF)
            total = total + lax.dot_general(
                term, onehot, (((1,), (1,)), ((), ())), preferred_element_type=F32
            )
        last = jnp.where(iota((3, CYCLES), 1) == CYCLES - 1, top, 0.0)
        total = total[0:3] + total[3:6] + total[6:9] + last
        for i in range(count):
            sum_ref[i] = total

    return kernel


def inverse_kernel(slab, depth, lateral, count):
    rows, half = slab * depth, lateral // 2

    def kernel(cut_ref, sum_ref, map_ref, mre_ref, mim_ref, mtre_ref, mtim_ref, back_ref, high_ref, low_ref, out_ref):
        total = sum_ref[0]
        for i in range(1, count):
            total = total + sum_ref[i]
        cross, power0, power1 = total[0:1], total[1:2], total[2:3]
        corr = cross / (jnp.sqrt(power0) * jnp.sqrt(power1))
        weight = jnp.where(iota((1, CYCLES), 1) <= cut_ref[0], corr, 0.0)
        low = jnp.broadcast_to(weight[:, 0:128], (depth, 128))
        high = jnp.broadcast_to(weight[:, 128:256], (depth, 128))
        pieces = []
        for j in range(half // 128):
            cell = map_ref[0, :, pl.ds(j * 128, 128)]
            near = cell & 127
            found = jnp.where(
                cell < 128,
                jnp.take_along_axis(low, near, axis=1),
                jnp.take_along_axis(high, near, axis=1),
            )
            twice = jnp.where(iota((depth, 128), 1) + j * 128 == 0, 1.0, 2.0)
            pieces.append(found * twice)
        cells = jnp.concatenate(pieces, axis=1)
        cells = jnp.concatenate([cells] * slab, axis=0)
        last = weight[:, CYCLES - 1 : CYCLES]
        re = mre_ref[...] * cells
        im = mim_ref[...] * cells
        re = jnp.concatenate([re[:, :128] - mtim_ref[...] * last, re[:, 128:]], axis=1)
        im = jnp.concatenate([im[:, :128] + mtre_ref[...] * last, im[:, 128:]], axis=1)
        from_re = split_dot(high_ref[...], low_ref[...], re)
        from_im = split_dot(high_ref[...], low_ref[...], im)
        inner_re = (from_re[:rows] - from_im[rows:]).astype(BF)
        inner_im = (from_re[rows:] + from_im[:rows]).astype(BF)
        joined = dot(inner_re, back_ref[0:half]) + dot(inner_im, back_ref[half:lateral])
        out_ref[...] = joined * (1.0 / (depth * lateral))

    return kernel


def body(data_halves, psf_taps, cycle_map, cutoff):
    _, views, slab, depth, lateral = data_halves.shape
    taps = psf_taps.shape[-1]
    radius = taps // 2
    rows, edge = slab * depth, radius * depth
    ext_rows = rows + 2 * edge
    half = lateral // 2
    count = lax.axis_size("tile")
    index = lax.axis_index("tile")
    pairs = [(i, i ^ 1) for i in range(count)]
    others = [(i, i + 1) for i in range(1, count - 1, 2)]
    others = others + [(b, a) for a, b in others]

    def exchange(to_pair, to_other):
        other = lax.ppermute(to_other, "tile", others)
        return lax.ppermute(to_pair, "tile", pairs), other

    def whole(array):
        return pl.BlockSpec(array.shape, lambda i: (0,) * len(array.shape))

    def half_of(array, h, size=None, at=0):
        shape = (1,) + array.shape[1:] if size is None else (1, size) + array.shape[2:]
        return pl.BlockSpec(shape, lambda i: (h, at) + (0,) * (len(shape) - 2))

    def call(kernel, inputs, outputs, name, scratch=(), flops=0):
        arrays = [x[0] if isinstance(x, tuple) else x for x in inputs]
        specs = []
        for x in inputs:
            if isinstance(x, tuple):
                specs.append(x[1])
            else:
                specs.append(whole(x))
        bytes_moved = sum(int(np.prod(s.shape)) * s.dtype.itemsize for s in outputs)
        return pl.pallas_call(
            kernel,
            grid=(1,),
            in_specs=specs,
            out_specs=tuple(whole(s) for s in outputs),
            out_shape=tuple(outputs),
            scratch_shapes=list(scratch),
            cost_estimate=pl.CostEstimate(flops=flops, bytes_accessed=2 * bytes_moved, transcendentals=0),
            compiler_params=pltpu.CompilerParams(vmem_limit_bytes=VMEM_LIMIT),
            name=name,
        )(*arrays)

    def shaped(*shape, dtype=F32):
        return jax.ShapeDtypeStruct(shape, dtype)

    scalars = pl.BlockSpec(memory_space=pltpu.SMEM)
    data = data_halves.reshape(2, views, rows, lateral)
    start = jnp.mean(data.astype(F32), axis=1).astype(BF)
    even = index % 2 == 0
    low, high = start[:, :edge], start[:, rows - edge :]
    pair0, other0 = exchange(jnp.where(even, high, low), jnp.where(even, low, high))

    kernels = psf_taps / jnp.sum(psf_taps, axis=-1, keepdims=True)
    place = (jnp.stack([index * slab, jnp.int32(count * slab), index % 2]), scalars)
    band = shaped(views, 256, 256, dtype=BF)
    *mats, shape, one0, one1 = call(
        prep_kernel(views, taps, slab, depth, lateral),
        [(kernels.reshape(-1), scalars), place],
        [
            shaped(views * rows, ext_rows, dtype=BF),
            shaped(ext_rows, views * rows, dtype=BF),
            band,
            band,
            band,
            band,
            shaped(2, views * rows, 128),
            shaped(2, views, depth, 128),
            shaped(views, 2, 8, lateral),
            shaped(depth, 128),
            shaped(ext_rows, lateral),
            shaped(rows, lateral),
        ],
        "prep",
        flops=4 * 10**9,
    )

    held = [pltpu.VMEM((views * rows, lateral), BF)]
    firsts = []
    for h in range(2):
        own, to_pair, to_other = call(
            first_kernel(views, slab, rows, edge),
            [place, (data, half_of(data, h)), (pair0, half_of(pair0, h)), (other0, half_of(other0, h))] + mats,
            [shaped(1, rows, lateral)] + [shaped(1, 2 * edge, lateral, dtype=BF)] * 2,
            f"first{h}",
            held,
            flops=4 * 10**9,
        )
        firsts.append((own, to_pair, to_other) + exchange(to_pair, to_other))

    angle = 2.0 * np.pi / lateral * np.arange(256)
    quarter = jnp.asarray(np.cos(angle).astype(np.float32).reshape(2, 128))
    grid_z = np.arange(depth)[:, None] * np.arange(depth)[None, :] % depth * (2.0 * np.pi / depth)
    wave = np.stack([np.cos(grid_z), np.sin(grid_z)]).astype(np.float32)
    wave = jnp.asarray(np.tile(wave, (1, 1, 128 // depth)))
    table = shaped(2 * rows, rows, dtype=BF)
    waves, back, table_hi, table_lo = call(
        table_kernel(slab, depth, lateral),
        [quarter, wave, (firsts[1][0], pl.BlockSpec((1, 8, 128), lambda i: (0, 0, 0)))],
        [shaped(lateral, lateral, dtype=BF), shaped(lateral, lateral, dtype=BF), table, table],
        "tables",
        flops=2 * 10**9,
    )

    seconds = []
    for h in range(2):
        own, to_pair, to_other, pair, other = firsts[h]
        est, part, to_pair, to_other = call(
            second_kernel(views, slab, rows, edge, lateral),
            [place, (data, half_of(data, h)), (pair0, half_of(pair0, h)), (other0, half_of(other0, h))]
            + [own, to_pair, to_other, pair, other, shape, one0]
            + mats,
            [shaped(1, rows, lateral)] * 2 + [shaped(1, edge, lateral, dtype=BF)] * 2,
            f"second{h}",
            held,
            flops=4 * 10**9,
        )
        seconds.append((est, part) + exchange(to_pair, to_other))

    plane, top = shaped(rows, half), shaped(rows, 128)
    tables = [one1, waves, table_hi, table_lo]
    spectra = call(
        spectrum_kernel(views, slab, depth, lateral),
        [place, *seconds[0]] + tables,
        [plane, plane, top, top],
        "spectrum0",
        flops=10**9,
    )
    *mixed, sums = call(
        power_kernel(views, slab, depth, lateral, count),
        [place, *seconds[1]] + tables + [cycle_map, *spectra],
        [plane, plane, top, top, shaped(count, 3, CYCLES)],
        "spectrum1",
        flops=2 * 10**9,
    )
    sums = lax.all_to_all(sums, "tile", 0, 0)
    (joined,) = call(
        inverse_kernel(slab, depth, lateral, count),
        [(cutoff, scalars), sums, cycle_map, *mixed, back, table_hi, table_lo],
        [shaped(rows, lateral)],
        "inverse",
        flops=10**9,
    )
    return joined.reshape(slab, depth, lateral)


def solution(mesh):
    in_specs = (
        P(None, None, ("groups", "tile"), None, None),
        P(),
        P(("groups", "tile"), None, None),
        P("groups"),
    )
    out_specs = P(("groups", "tile"), None, None)
    return jax.shard_map(body, mesh=mesh, in_specs=in_specs, out_specs=out_specs, check_vma=False)
```

profile of v0, /device:TPU:0, one launch (start us, length us, event | category | flops | bytes accessed | tf_op | source)
XLA Modules:
  0.0 65.8 jit_solution(4323638417073215052)
XLA Ops:
  0.0 2.1 %convert_reduce_fusion = f32[2,8,32,512]{3,2,1,0:T(8,128)S(1)} fusion(bf16[2,4,8,32,512]{4,3,2,1,0:T(8,128)(2,1)} %param.6), kind=kLoop, calls=%fused_computation | loop fusion | flops 1835008 | bytes 3145728 | tf_op jit(solution)/shard_map/reduce_sum | solution.py:541
  2.1 0.0 copy-start.4
  2.2 0.1 multiply_convert_fusion
  2.3 0.7 %collective-permute-start.1 = (bf16[2,128,512]{2,1,0:T(8,128)(2,1)S(1)}, bf16[2,128,512]{2,1,0:T(8,128)(2,1)S(1)}, u32[]{:S(2)}, u32[]{:S(2)}) collective-permute-start(bf16[2,128,512]{2,1,0:T(8,128)(2,1)S(1)} %get-tuple-element.83), channel_id=1, source_target_pairs={{1,2},{3,4},{5,6},{7,8},{9,10},{11,12},{13,14},{2,1},{4,3},{6,5},{... | collective-permute-start | bytes 786440 | tf_op jit(solution)/shard_map/ppermute | solution.py:505
  3.0 4.4 %collective-permute-start = (bf16[2,128,512]{2,1,0:T(8,128)(2,1)S(1)}, bf16[2,128,512]{2,1,0:T(8,128)(2,1)S(1)}, u32[]{:S(2)}, u32[]{:S(2)}) collective-permute-start(bf16[2,128,512]{2,1,0:T(8,128)(2,1)S(1)} %get-tuple-element.84), channel_id=1, source_target_pairs={{0,1},{1,0},{2,3},{3,2},{4,5},{5,4},{6,7},{7,6},{8,9},{9,8},{10,11... | collective-permute-start | bytes 786440 | tf_op jit(solution)/shard_map/ppermute | solution.py:506
  7.4 0.1 reduce_sum.19
  7.5 0.1 broadcast_divide_fusion
  7.6 0.1 reshape.15.kern
  7.7 0.1 pad_add_fusion.place
  7.8 2.2 %prep.1 = (bf16[1024,512]{1,0:T(8,128)(2,1)S(1)}, bf16[512,1024]{1,0:T(8,128)(2,1)S(1)}, bf16[4,256,256]{2,1,0:T(8,128)(2,1)S(1)}, bf16[4,256,256]{2,1,0:T(8,128...) custom-call(f32[108]{0:T(128)S(1)} %reshape.15.kern, ...), custom_call_target="tpu_custom_call" | custom-call | flops 4000000000 | bytes 14188544 | tf_op jit(solution)/shard_map/prep/pallas_call | solution.py:524
  10.0 0.0 collective-permute-done.1.other_ref.other0_ref
  10.1 3.7 %first0.1 = (f32[1,256,512]{2,1,0:T(8,128)S(1)}, bf16[1,256,512]{2,1,0:T(8,128)(2,1)S(1)}, bf16[1,256,512]{2,1,0:T(8,128)(2,1)S(1)}) custom-call(s32[3]{0:T(128)S(1)} %pad_add_fusion.place, bf16[2,4,256,512]{3,2,1,0:T(8,128)(2,1)S(1)} %bitcast.5, bf16[2,128,512]{2,1,0:T(8,128)(2,1)S(1)} %collective-permute-done.pair_ref.pair0_ref, ...), custom_call_target="tpu_custom_call" | custom-call | flops 4000000000 | bytes 2097152 | tf_op jit(solution)/shard_map/first0/pallas_call | solution.py:524
  13.8 3.5 %collective-permute-start.6 = (bf16[1,256,512]{2,1,0:T(8,128)(2,1)S(1)}, bf16[1,256,512]{2,1,0:T(8,128)(2,1)S(1)}, u32[]{:S(2)}, u32[]{:S(2)}) collective-permute-start(bf16[1,256,512]{2,1,0:T(8,128)(2,1)S(1)} %get-tuple-element.67.sent_pair), channel_id=1, source_target_pairs={{0,1},{1,0},{2,3},{3,2},{4,5},{5,4},{6,7},{7,6},{8,9},{9,8},{10,11... | collective-permute-start | bytes 786440 | tf_op jit(solution)/shard_map/ppermute | solution.py:506
  17.3 0.7 %collective-permute-start.7 = (bf16[1,256,512]{2,1,0:T(8,128)(2,1)S(1)}, bf16[1,256,512]{2,1,0:T(8,128)(2,1)S(1)}, u32[]{:S(2)}, u32[]{:S(2)}) collective-permute-start(bf16[1,256,512]{2,1,0:T(8,128)(2,1)S(1)} %get-tuple-element.68.sent_other), channel_id=1, source_target_pairs={{1,2},{3,4},{5,6},{7,8},{9,10},{11,12},{13,14},{2,1},{4,3},{6,5},{... | collective-permute-start | bytes 786440 | tf_op jit(solution)/shard_map/ppermute | solution.py:505
  18.0 3.7 %first1.1 = (f32[1,256,512]{2,1,0:T(8,128)S(1)}, bf16[1,256,512]{2,1,0:T(8,128)(2,1)S(1)}, bf16[1,256,512]{2,1,0:T(8,128)(2,1)S(1)}) custom-call(s32[3]{0:T(128)S(1)} %pad_add_fusion.place, bf16[2,4,256,512]{3,2,1,0:T(8,128)(2,1)S(1)} %bitcast.6, bf16[2,128,512]{2,1,0:T(8,128)(2,1)S(1)} %collective-permute-done.pair_ref.pair0_ref, ...), custom_call_target="tpu_custom_call" | custom-call | flops 4000000000 | bytes 2097152 | tf_op jit(solution)/shard_map/first1/pallas_call | solution.py:524
  21.7 3.8 %collective-permute-start.2 = (bf16[1,256,512]{2,1,0:T(8,128)(2,1)S(1)}, bf16[1,256,512]{2,1,0:T(8,128)(2,1)S(1)}, u32[]{:S(2)}, u32[]{:S(2)}) collective-permute-start(bf16[1,256,512]{2,1,0:T(8,128)(2,1)S(1)} %get-tuple-element.54.sent_pair), channel_id=1, source_target_pairs={{0,1},{1,0},{2,3},{3,2},{4,5},{5,4},{6,7},{7,6},{8,9},{9,8},{10,11... | collective-permute-start | bytes 786440 | tf_op jit(solution)/shard_map/ppermute | solution.py:506
  25.5 0.7 %collective-permute-start.3 = (bf16[1,256,512]{2,1,0:T(8,128)(2,1)S(1)}, bf16[1,256,512]{2,1,0:T(8,128)(2,1)S(1)}, u32[]{:S(2)}, u32[]{:S(2)}) collective-permute-start(bf16[1,256,512]{2,1,0:T(8,128)(2,1)S(1)} %get-tuple-element.55.sent_other), channel_id=1, source_target_pairs={{1,2},{3,4},{5,6},{7,8},{9,10},{11,12},{13,14},{2,1},{4,3},{6,5},{... | collective-permute-start | bytes 786440 | tf_op jit(solution)/shard_map/ppermute | solution.py:505
  26.2 4.0 %second0.1 = (f32[1,256,512]{2,1,0:T(8,128)S(1)}, f32[1,256,512]{2,1,0:T(8,128)S(1)}, bf16[1,128,512]{2,1,0:T(8,128)(2,1)S(1)}, bf16[1,128,512]{2,1,0:T(8,128)(2,1)S(1)}) custom-call(s32[3]{0:T(128)S(1)} %pad_add_fusion.place, bf16[2,4,256,512]{3,2,1,0:T(8,128)(2,1)S(1)} %bitcast.7, bf16[2,128,512]{2,1,0:T(8,128)(2,1)S(1)} %collective-permute-done.pair_ref.pair0_ref, ...), custom_call_target="tpu_custom_call" | custom-call | flops 4000000000 | bytes 2621440 | tf_op jit(solution)/shard_map/second0/pallas_call | solution.py:524
  30.2 2.8 %collective-permute-start.8 = (bf16[1,128,512]{2,1,0:T(8,128)(2,1)S(1)}, bf16[1,128,512]{2,1,0:T(8,128)(2,1)S(1)}, u32[]{:S(2)}, u32[]{:S(2)}) collective-permute-start(bf16[1,128,512]{2,1,0:T(8,128)(2,1)S(1)} %get-tuple-element.71), channel_id=1, source_target_pairs={{0,1},{1,0},{2,3},{3,2},{4,5},{5,4},{6,7},{7,6},{8,9},{9,8},{10,11... | collective-permute-start | bytes 393224 | tf_op jit(solution)/shard_map/ppermute | solution.py:506
  33.1 0.8 %collective-permute-start.9 = (bf16[1,128,512]{2,1,0:T(8,128)(2,1)S(1)}, bf16[1,128,512]{2,1,0:T(8,128)(2,1)S(1)}, u32[]{:S(2)}, u32[]{:S(2)}) collective-permute-start(bf16[1,128,512]{2,1,0:T(8,128)(2,1)S(1)} %get-tuple-element.72), channel_id=1, source_target_pairs={{1,2},{3,4},{5,6},{7,8},{9,10},{11,12},{13,14},{2,1},{4,3},{6,5},{... | collective-permute-start | bytes 393224 | tf_op jit(solution)/shard_map/ppermute | solution.py:505
  33.9 0.0 copy-start.2
  33.9 0.0 copy-start.3
  33.9 4.0 %second1.1 = (f32[1,256,512]{2,1,0:T(8,128)S(1)}, f32[1,256,512]{2,1,0:T(8,128)S(1)}, bf16[1,128,512]{2,1,0:T(8,128)(2,1)S(1)}, bf16[1,128,512]{2,1,0:T(8,128)(2,1)S(1)}) custom-call(s32[3]{0:T(128)S(1)} %pad_add_fusion.place, bf16[2,4,256,512]{3,2,1,0:T(8,128)(2,1)S(1)} %bitcast.8, bf16[2,128,512]{2,1,0:T(8,128)(2,1)S(1)} %collective-permute-done.pair_ref.pair0_ref, ...), custom_call_target="tpu_custom_call" | custom-call | flops 4000000000 | bytes 2621440 | tf_op jit(solution)/shard_map/second1/pallas_call | solution.py:524
  38.0 3.1 %collective-permute-start.4 = (bf16[1,128,512]{2,1,0:T(8,128)(2,1)S(1)}, bf16[1,128,512]{2,1,0:T(8,128)(2,1)S(1)}, u32[]{:S(2)}, u32[]{:S(2)}) collective-permute-start(bf16[1,128,512]{2,1,0:T(8,128)(2,1)S(1)} %get-tuple-element.60), channel_id=1, source_target_pairs={{0,1},{1,0},{2,3},{3,2},{4,5},{5,4},{6,7},{7,6},{8,9},{9,8},{10,11... | collective-permute-start | bytes 393224 | tf_op jit(solution)/shard_map/ppermute | solution.py:506
  41.0 0.7 collective-permute-start.5
  41.7 1.1 %tables.1 = (bf16[512,512]{1,0:T(8,128)(2,1)S(1)}, bf16[512,512]{1,0:T(8,128)(2,1)S(1)}, bf16[512,256]{1,0:T(8,128)(2,1)S(1)}, bf16[512,256]{1,0:T(8,128)(2,1)S(1)}) custom-call(f32[2,128]{1,0:T(2,128)S(1)} %copy-done.3, f32[2,32,128]{2,1,0:T(8,128)S(1)} %copy-done.2, f32[1,256,512]{2,1,0:T(8,128)S(1)} %get-tuple-element.53.own_ref._), custom_call_target="tpu_custom_call" | custom-call | flops 2000000000 | bytes 3145728 | tf_op jit(solution)/shard_map/tables/pallas_call | solution.py:524
  42.8 0.0 copy-start.1
  42.8 1.4 %spectrum0.1 = (f32[256,256]{1,0:T(8,128)S(1)}, f32[256,256]{1,0:T(8,128)S(1)}, f32[256,128]{1,0:T(8,128)S(1)}, f32[256,128]{1,0:T(8,128)S(1)}) custom-call(s32[3]{0:T(128)S(1)} %pad_add_fusion.place, f32[1,256,512]{2,1,0:T(8,128)S(1)} %get-tuple-element.69.est_ref, f32[1,256,512]{2,1,0:T(8,128)S(1)} %get-tuple-element.70.part_ref, ...), custom_call_target="tpu_custom_call" | custom-call | flops 1000000000 | bytes 1572864 | tf_op jit(solution)/shard_map/spectrum0/pallas_call | solution.py:524
  44.3 3.8 %spectrum1.1 = (f32[256,256]{1,0:T(8,128)S(1)}, f32[256,256]{1,0:T(8,128)S(1)}, f32[256,128]{1,0:T(8,128)S(1)}, f32[256,128]{1,0:T(8,128)S(1)}, f32[16,3,256]{2,1,0:T(4,128)}) custom-call(s32[3]{0:T(128)S(1)} %pad_add_fusion.place, f32[1,256,512]{2,1,0:T(8,128)S(1)} %get-tuple-element.58.est_ref, f32[1,256,512]{2,1,0:T(8,128)S(1)} %get-tuple-element.59.part_ref, ...), custom_call_target="tpu_custom_call" | custom-call | flops 2000000000 | bytes 1671168 | tf_op jit(solution)/shard_map/spectrum1/pallas_call | solution.py:524
  48.0 9.0 %all-to-all-start = ((f32[16,3,256]{2,1,0:T(4,128)}), f32[16,3,256]{2,1,0:T(4,128)S(1)}, u32[]{:S(2)}, u32[]{:S(2)}) async-start(f32[16,3,256]{2,1,0:T(4,128)} %get-tuple-element.77), calls=%async_computation | async-start | bytes 131072 | tf_op jit(solution)/shard_map/all_to_all | solution.py:628
  57.6 6.2 %all-to-all-done.sum_ref = f32[16,3,256]{2,1,0:T(4,128)S(1)} async-done(((f32[16,3,256]{2,1,0:T(4,128)}), f32[16,3,256]{2,1,0:T(4,128)S(1)}, u32[]{:S(2)}, u32[]{:S(2)}) %all-to-all-start) | async-done | bytes 49184 | tf_op jit(solution)/shard_map/all_to_all | solution.py:628
  63.9 1.9 %inverse.1 = f32[256,512]{1,0:T(8,128)} custom-call(s32[1]{0:T(128)S(6)} %copy.9.cut_ref, f32[16,3,256]{2,1,0:T(4,128)S(1)} %all-to-all-done.sum_ref, s32[1,32,512]{2,1,0:T(8,128)S(1)} %copy-done.1, f32[256,256]{1,0:T(8,128)S(1)} %get-tuple-element.78.mre_ref, f32[256,256]{1,0:T(8,128)S(1)} %get-tuple-element.79.mim_ref, ...), custom_call_target="tpu_custom_call" | custom-call | flops 1000000000 | bytes 1048576 | tf_op jit(solution)/shard_map/inverse/pallas_call | solution.py:524
  (17 shorter events, 0.1 us)
Async XLA Ops:
  2.1 5.3 %copy-start.4 = (f32[4,3,9]{2,0,1:T(4,128)S(1)}, f32[4,3,9]{2,0,1:T(4,128)}, u32[]{:S(2)}) copy-start(f32[4,3,9]{2,0,1:T(4,128)} %param.7) | copy-start | bytes 1300
  2.3 7.7 %collective-permute-start.1 = (bf16[2,128,512]{2,1,0:T(8,128)(2,1)S(1)}, bf16[2,128,512]{2,1,0:T(8,128)(2,1)S(1)}, u32[]{:S(2)}, u32[]{:S(2)}) collective-permute-start(bf16[2,128,512]{2,1,0:T(8,128)(2,1)S(1)} %get-tuple-element.83), channel_id=1, source_target_pairs={{1,2},{3,4},{5,6},{7,8},{9,10},{11,12},{13,14},{2,1},{4,3},{6,5},{... | collective-permute-start | bytes 786440 | tf_op jit(solution)/shard_map/ppermute | solution.py:505
  3.0 7.0 %collective-permute-start = (bf16[2,128,512]{2,1,0:T(8,128)(2,1)S(1)}, bf16[2,128,512]{2,1,0:T(8,128)(2,1)S(1)}, u32[]{:S(2)}, u32[]{:S(2)}) collective-permute-start(bf16[2,128,512]{2,1,0:T(8,128)(2,1)S(1)} %get-tuple-element.84), channel_id=1, source_target_pairs={{0,1},{1,0},{2,3},{3,2},{4,5},{5,4},{6,7},{7,6},{8,9},{9,8},{10,11... | collective-permute-start | bytes 786440 | tf_op jit(solution)/shard_map/ppermute | solution.py:506
  7.8 2.3 %copy-start = (bf16[2,4,8,32,512]{4,3,2,1,0:T(8,128)(2,1)S(1)}, bf16[2,4,8,32,512]{4,3,2,1,0:T(8,128)(2,1)}, u32[]{:S(2)}) copy-start(bf16[2,4,8,32,512]{4,3,2,1,0:T(8,128)(2,1)} %param.6) | copy-start | bytes 6291460
  13.8 12.4 %collective-permute-start.6 = (bf16[1,256,512]{2,1,0:T(8,128)(2,1)S(1)}, bf16[1,256,512]{2,1,0:T(8,128)(2,1)S(1)}, u32[]{:S(2)}, u32[]{:S(2)}) collective-permute-start(bf16[1,256,512]{2,1,0:T(8,128)(2,1)S(1)} %get-tuple-element.67.sent_pair), channel_id=1, source_target_pairs={{0,1},{1,0},{2,3},{3,2},{4,5},{5,4},{6,7},{7,6},{8,9},{9,8},{10,11... | collective-permute-start | bytes 786440 | tf_op jit(solution)/shard_map/ppermute | solution.py:506
  17.3 8.9 %collective-permute-start.7 = (bf16[1,256,512]{2,1,0:T(8,128)(2,1)S(1)}, bf16[1,256,512]{2,1,0:T(8,128)(2,1)S(1)}, u32[]{:S(2)}, u32[]{:S(2)}) collective-permute-start(bf16[1,256,512]{2,1,0:T(8,128)(2,1)S(1)} %get-tuple-element.68.sent_other), channel_id=1, source_target_pairs={{1,2},{3,4},{5,6},{7,8},{9,10},{11,12},{13,14},{2,1},{4,3},{6,5},{... | collective-permute-start | bytes 786440 | tf_op jit(solution)/shard_map/ppermute | solution.py:505
  21.7 12.2 %collective-permute-start.2 = (bf16[1,256,512]{2,1,0:T(8,128)(2,1)S(1)}, bf16[1,256,512]{2,1,0:T(8,128)(2,1)S(1)}, u32[]{:S(2)}, u32[]{:S(2)}) collective-permute-start(bf16[1,256,512]{2,1,0:T(8,128)(2,1)S(1)} %get-tuple-element.54.sent_pair), channel_id=1, source_target_pairs={{0,1},{1,0},{2,3},{3,2},{4,5},{5,4},{6,7},{7,6},{8,9},{9,8},{10,11... | collective-permute-start | bytes 786440 | tf_op jit(solution)/shard_map/ppermute | solution.py:506
  25.5 8.4 %collective-permute-start.3 = (bf16[1,256,512]{2,1,0:T(8,128)(2,1)S(1)}, bf16[1,256,512]{2,1,0:T(8,128)(2,1)S(1)}, u32[]{:S(2)}, u32[]{:S(2)}) collective-permute-start(bf16[1,256,512]{2,1,0:T(8,128)(2,1)S(1)} %get-tuple-element.55.sent_other), channel_id=1, source_target_pairs={{1,2},{3,4},{5,6},{7,8},{9,10},{11,12},{13,14},{2,1},{4,3},{6,5},{... | collective-permute-start | bytes 786440 | tf_op jit(solution)/shard_map/ppermute | solution.py:505
  30.2 12.6 %collective-permute-start.8 = (bf16[1,128,512]{2,1,0:T(8,128)(2,1)S(1)}, bf16[1,128,512]{2,1,0:T(8,128)(2,1)S(1)}, u32[]{:S(2)}, u32[]{:S(2)}) collective-permute-start(bf16[1,128,512]{2,1,0:T(8,128)(2,1)S(1)} %get-tuple-element.71), channel_id=1, source_target_pairs={{0,1},{1,0},{2,3},{3,2},{4,5},{5,4},{6,7},{7,6},{8,9},{9,8},{10,11... | collective-permute-start | bytes 393224 | tf_op jit(solution)/shard_map/ppermute | solution.py:506
  33.1 9.8 %collective-permute-start.9 = (bf16[1,128,512]{2,1,0:T(8,128)(2,1)S(1)}, bf16[1,128,512]{2,1,0:T(8,128)(2,1)S(1)}, u32[]{:S(2)}, u32[]{:S(2)}) collective-permute-start(bf16[1,128,512]{2,1,0:T(8,128)(2,1)S(1)} %get-tuple-element.72), channel_id=1, source_target_pairs={{1,2},{3,4},{5,6},{7,8},{9,10},{11,12},{13,14},{2,1},{4,3},{6,5},{... | collective-permute-start | bytes 393224 | tf_op jit(solution)/shard_map/ppermute | solution.py:505
  33.9 7.8 %copy-start.2 = (f32[2,32,128]{2,1,0:T(8,128)S(1)}, f32[2,32,128]{2,1,0:T(8,128)}, u32[]{:S(2)}) copy-start(f32[2,32,128]{2,1,0:T(8,128)} %constant.34.clone.wave_ref) | copy-start | bytes 98308
  33.9 7.8 %copy-start.3 = (f32[2,128]{1,0:T(2,128)S(1)}, f32[2,128]{1,0:T(2,128)}, u32[]{:S(2)}) copy-start(f32[2,128]{1,0:T(2,128)} %constant.33.clone.quarter_ref) | copy-start | bytes 3076
  38.0 6.3 %collective-permute-start.4 = (bf16[1,128,512]{2,1,0:T(8,128)(2,1)S(1)}, bf16[1,128,512]{2,1,0:T(8,128)(2,1)S(1)}, u32[]{:S(2)}, u32[]{:S(2)}) collective-permute-start(bf16[1,128,512]{2,1,0:T(8,128)(2,1)S(1)} %get-tuple-element.60), channel_id=1, source_target_pairs={{0,1},{1,0},{2,3},{3,2},{4,5},{5,4},{6,7},{7,6},{8,9},{9,8},{10,11... | collective-permute-start | bytes 393224 | tf_op jit(solution)/shard_map/ppermute | solution.py:506
  41.0 3.2 %collective-permute-start.5 = (bf16[1,128,512]{2,1,0:T(8,128)(2,1)S(1)}, bf16[1,128,512]{2,1,0:T(8,128)(2,1)S(1)}, u32[]{:S(2)}, u32[]{:S(2)}) collective-permute-start(bf16[1,128,512]{2,1,0:T(8,128)(2,1)S(1)} %get-tuple-element.61), channel_id=1, source_target_pairs={{1,2},{3,4},{5,6},{7,8},{9,10},{11,12},{13,14},{2,1},{4,3},{6,5},{... | collective-permute-start | bytes 393224 | tf_op jit(solution)/shard_map/ppermute | solution.py:505
  42.8 1.5 %copy-start.1 = (s32[1,32,512]{2,1,0:T(8,128)S(1)}, s32[1,32,512]{2,1,0:T(8,128)}, u32[]{:S(2)}) copy-start(s32[1,32,512]{2,1,0:T(8,128)} %map_ref.3) | copy-start | bytes 196612
  48.0 15.9 %all-to-all-start = ((f32[16,3,256]{2,1,0:T(4,128)}), f32[16,3,256]{2,1,0:T(4,128)S(1)}, u32[]{:S(2)}, u32[]{:S(2)}) async-start(f32[16,3,256]{2,1,0:T(4,128)} %get-tuple-element.77), calls=%async_computation | async-start | bytes 131072 | tf_op jit(solution)/shard_map/all_to_all | solution.py:628
where the time goes:
time: 66.1 us; the launch traced here: 65.8 us
  starting transfers between devices  30 us (45%)
  Pallas kernels  25.9 us (39%)
  waiting for transfers between devices  6.28 us (10%)
  other arithmetic  2.54 us (4%)
  between operations  0.93 us (1%)
    pallas_call x9, Pallas kernels, call(): pl.pallas_call(kernel, grid=(1,), in_specs=specs, out_specs=tuple((whole(...  25.9 us
    ppermute x5, starting transfers between devices, exchange(): return (lax.ppermute(to_pair, 'tile', pairs), other)  17.6 us
    all_to_all x1, starting transfers between devices, body(): sums = lax.all_to_all(sums, 'tile', 0, 0)  8.96 us
    all_to_all x1, waiting for transfers between devices, body(): sums = lax.all_to_all(sums, 'tile', 0, 0)  6.25 us
    ppermute x5, starting transfers between devices, exchange(): other = lax.ppermute(to_other, 'tile', others)  3.5 us
    reduce_sum x1, other arithmetic, body(): start = jnp.mean(data.astype(F32), axis=1).astype(BF)  2.13 us
  transfers between devices with their start and end apart: 11, of which 1 were waited for; matrix products, arithmetic and copies ran while one was open for 1% of the time, Pallas kernels for 25%

commit v1 on v0

--- a/solution.py
+++ b/solution.py
@@ -44,8 +44,9 @@
     rows = slab * depth
     scale = 1.0 / views
 
-    def kernel(kern, place, a_ref, b_ref, t_ref, c_ref, tt_ref, ct_ref, base_ref, off_ref, row_ref, w_ref, one0_ref, one1_ref):
-        first, rows_total = place[0], place[1]
+    def kernel(kern, a_ref, b_ref, t_ref, tt_ref, base_ref, off_ref, row_ref, w_ref, one0_ref, one1_ref):
+        first = lax.axis_index("tile") * slab
+        rows_total = lax.axis_size("tile") * slab
 
         def tap(v, axis, t):
             return kern[(v * 3 + axis) * taps + t]
@@ -68,7 +69,6 @@
         upper_gap = gap[120:128] - 128
         lower_gap = gap[0:8] + 128
         zero = jnp.zeros((depth, 128), BF)
-        flat = jnp.zeros((128, 128), BF)
         tail = jnp.zeros((120, 128), F32)
         gains = []
         for v in range(views):
@@ -97,7 +97,7 @@
                         blocks[d] = zero if weight is None else (weight * band_zt).astype(BF)
                     b_ref[pl.ds(i * depth, depth), pl.ds(v * rows + g * 128, 128)] = blocks[d]
 
-            for flip, band_ref, cross_ref in ((False, t_ref, c_ref), (True, tt_ref, ct_ref)):
+            for flip, band_ref in ((False, t_ref), (True, tt_ref)):
                 pairs = [(t, tap(v, 2, taps - 1 - t if flip else t)) for t in range(taps)]
                 middle = lookup(gap, pairs).astype(BF)
                 upper = jnp.concatenate([tail, lookup(upper_gap, pairs[:radius])], axis=0).astype(BF)
@@ -105,7 +105,6 @@
                 for at, block in ((0, middle), (1, upper), (2, lower), (3, middle)):
                     at_rows, at_cols = pl.ds(at // 2 * 128, 128), pl.ds(at % 2 * 128, 128)
                     band_ref[v, at_rows, at_cols] = block
-                    cross_ref[v, at_rows, at_cols] = flat if at in (0, 3) else block
 
             mid = depth // 2
             sum_xz = jnp.sum(
@@ -163,19 +162,27 @@
     return kernel
 
 
-def y_blur(x, band, cross):
-    left = dot(x[:, 0:256], band)
-    right = dot(x[:, 256:512], band)
-    mid = dot(x[:, 128:384], cross)
-    left = jnp.concatenate([left[:, 0:128], left[:, 128:256] + mid[:, 0:128]], axis=1)
-    right = jnp.concatenate([right[:, 0:128] + mid[:, 128:256], right[:, 128:256]], axis=1)
-    return jnp.concatenate([left, right], axis=1)
-
-
-def mean_views(data_ref, views):
-    total = data_ref[0, 0].astype(F32)
+def y_blur(x, band):
+    rows = x.shape[0]
+    stacked = jnp.concatenate([x[:, 0:256], x[:, 128:384], x[:, 256:512]], axis=0)
+    wide = dot(stacked, band)
+    left, mid, right = wide[:rows], wide[rows : 2 * rows], wide[2 * rows :]
+    low = iota((rows, 128), 1) < 64
+    return jnp.concatenate(
+        [
+            left[:, :128],
+            jnp.where(low, left[:, 128:], mid[:, :128]),
+            jnp.where(low, mid[:, 128:], right[:, :128]),
+            right[:, 128:],
+        ],
+        axis=1,
+    )
+
+
+def mean_views(h, data_ref, views):
+    total = data_ref[h, 0].astype(F32)
     for v in range(1, views):
-        total = total + data_ref[0, v].astype(F32)
+        total = total + data_ref[h, v].astype(F32)
     return total * (1.0 / views)
 
 
@@ -188,72 +195,99 @@
     return jnp.concatenate([x] * (lateral // 128), axis=1)
 
 
-def blur_back(n, views, slab, rows, level, data_ref, ext, mats, held):
-    a_ref, b_ref, t_ref, c_ref, tt_ref, ct_ref, base_ref, off_ref, row_ref = mats
+def blur_back(n, h, views, slab, rows, level, data_ref, ext, mats, held):
+    a_ref, b_ref, t_ref, tt_ref, base_ref, off_ref, row_ref = mats
     lateral = ext.shape[1]
+    held[...] = dot(a_ref[...], ext).astype(BF)
     for v in range(views):
-        part = dot(a_ref[pl.ds(v * rows, rows), :], ext).astype(BF)
+        part = held[pl.ds(v * rows, rows), :]
         base = across(base_ref[n, pl.ds(v * rows, rows), :], lateral) * (row_ref[v, 0, 0:1, :] * level)
-        predicted = y_blur(part, t_ref[v], c_ref[v]) + base
-        scaled = data_ref[0, v].astype(F32) * row_ref[v, 1, 0:1, :]
+        predicted = y_blur(part, t_ref[v]) + base
+        scaled = data_ref[h, v].astype(F32) * row_ref[v, 1, 0:1, :]
         offset = across(jnp.concatenate([off_ref[n, v]] * slab, axis=0), lateral)
         quotient = (scaled / predicted - offset).astype(BF)
-        held[pl.ds(v * rows, rows), :] = y_blur(quotient, tt_ref[v], ct_ref[v]).astype(BF)
+        held[pl.ds(v * rows, rows), :] = y_blur(quotient, tt_ref[v]).astype(BF)
     return dot(b_ref[...], held[...])
 
 
-def pick(even, from_pair, from_other):
-    pair = from_pair[0].astype(F32)
-    other = from_other[0].astype(F32)
+def pick(even, from_pair, from_other, h=0):
+    pair = from_pair[h].astype(F32)
+    other = from_other[h].astype(F32)
     return jnp.where(even, other, pair), jnp.where(even, pair, other)
 
 
-def put(even, low, high, to_pair, to_other):
+def put(even, low, high, to_pair, to_other, h=0):
     @pl.when(even)
     def _():
-        to_pair[0] = high
-        to_other[0] = low
+        to_pair[h] = high
+        to_other[h] = low
 
     @pl.when(jnp.logical_not(even))
     def _():
-        to_pair[0] = low
-        to_other[0] = high
-
-
-def first_kernel(views, slab, rows, edge):
-    def kernel(place, data_ref, pair_ref, other_ref, *refs):
-        mats, (own_ref, to_pair, to_other, held) = refs[:9], refs[9:]
-        even = place[2] == 0
-        lo, hi = pick(even, pair_ref, other_ref)
-        has_lo = jnp.where(place[0] > 0, 1.0, 0.0)
-        has_hi = jnp.where(place[0] + slab < place[1], 1.0, 0.0)
-        estimate = mean_views(data_ref, views)
+        to_pair[h] = low
+        to_other[h] = high
+
+
+def is_even():
+    return (lax.axis_index("tile") & 1) == 0
+
+
+def has_sides():
+    index = lax.axis_index("tile")
+    return jnp.where(index > 0, 1.0, 0.0), jnp.where(index + 1 < lax.axis_size("tile"), 1.0, 0.0)
+
+
+def edge_kernel(views, rows, edge):
+    def kernel(data_hbm, data_ref, to_pair, to_other, sems):
+        copies = {}
+        for h in range(2):
+            for v in range(views):
+                copies[h, v] = pltpu.make_async_copy(
+                    data_hbm.at[h, v], data_ref.at[h, v], sems.at[h * views + v]
+                )
+                copies[h, v].start()
+        even = is_even()
+        for h in range(2):
+            for v in range(views):
+                copies[h, v].wait()
+            start = mean_views(h, data_ref, views).astype(BF)
+            put(even, start[:edge], start[rows - edge :], to_pair, to_other, h)
+
+    return kernel
+
+
+def first_kernel(h, views, slab, rows, edge):
+    def kernel(data_ref, pair_ref, other_ref, *refs):
+        mats, (own_ref, to_pair, to_other, held) = refs[:7], refs[7:]
+        even = is_even()
+        lo, hi = pick(even, pair_ref, other_ref, h)
+        has_lo, has_hi = has_sides()
+        estimate = mean_views(h, data_ref, views)
         level = level_of(estimate)
         ext = jnp.concatenate([lo - level * has_lo, estimate - level, hi - level * has_hi], axis=0)
-        part = blur_back(0, views, slab, rows, level, data_ref, ext.astype(BF), mats, held)
+        part = blur_back(0, h, views, slab, rows, level, data_ref, ext.astype(BF), mats, held)
         own_ref[0] = part[edge : edge + rows]
         put(even, part[0 : 2 * edge].astype(BF), part[rows:].astype(BF), to_pair, to_other)
 
     return kernel
 
 
-def second_kernel(views, slab, rows, edge, lateral):
+def second_kernel(h, views, slab, rows, edge, lateral):
     scale = 1.0 / views
 
     def kernel(
-        place, data_ref, pair0_ref, other0_ref, own_ref, sent_pair, sent_other, pair_ref, other_ref, w_ref, one_ref, *refs
+        data_ref, pair0_ref, other0_ref, own_ref, sent_pair, sent_other, pair_ref, other_ref, w_ref, one_ref, *refs
     ):
-        mats, (est_ref, part_ref, to_pair, to_other, held) = refs[:9], refs[9:]
-        even = place[2] == 0
-        has_lo = jnp.where(place[0] > 0, 1.0, 0.0)
-        has_hi = jnp.where(place[0] + slab < place[1], 1.0, 0.0)
-        lo, hi = pick(even, pair0_ref, other0_ref)
+        mats, (est_ref, part_ref, to_pair, to_other, held) = refs[:7], refs[7:]
+        even = is_even()
+        has_lo, has_hi = has_sides()
+        lo, hi = pick(even, pair0_ref, other0_ref, h)
         got_lo, got_hi = pick(even, pair_ref, other_ref)
         sent_lo, sent_hi = pick(even, sent_pair, sent_other)
         lo = lo * (one_ref[0:edge] + scale * (sent_lo[0:edge] + got_lo[0:edge]))
         hi = hi * (one_ref[edge + rows :] + scale * (sent_hi[edge:] + got_hi[edge:]))
         got = jnp.concatenate([got_lo[edge:], got_hi[0:edge]], axis=0)
-        before = mean_views(data_ref, views)
+        before = mean_views(h, data_ref, views)
         level = level_of(before)
         estimate = before * (one_ref[pl.ds(edge, rows)] + scale * (own_ref[0] + got))
         est_ref[0] = estimate
@@ -267,7 +301,7 @@
             ],
             axis=0,
         )
-        part = blur_back(1, views, slab, rows, level, data_ref, ext.astype(BF), mats, held)
+        part = blur_back(1, h, views, slab, rows, level, data_ref, ext.astype(BF), mats, held)
         part_ref[0] = part[edge : edge + rows]
         put(even, part[0:edge].astype(BF), part[edge + rows :].astype(BF), to_pair, to_other)
 
@@ -363,8 +397,8 @@
 def spectrum_kernel(views, slab, depth, lateral):
     rows, half = slab * depth, lateral // 2
 
-    def kernel(place, est_ref, part_ref, pair_ref, other_ref, one_ref, waves_ref, high_ref, low_ref, *outs):
-        even = place[2] == 0
+    def kernel(est_ref, part_ref, pair_ref, other_ref, one_ref, waves_ref, high_ref, low_ref, *outs):
+        even = is_even()
         args = (est_ref, part_ref, pair_ref, other_ref, one_ref, waves_ref, high_ref, low_ref)
         for ref, value in zip(outs, spectrum(even, 1.0 / views, rows, half, *args)):
             ref[...] = value
@@ -372,11 +406,21 @@
     return kernel
 
 
+def cycle_kernel(depth, half):
+    def kernel(map_ref, cycle_ref):
+        columns = jnp.transpose(map_ref[0, :, 0:half].astype(F32))
+        cycle = iota((half, CYCLES), 1).astype(F32)
+        for k in range(depth // 2 + 1):
+            here = columns[:, k : k + 1] == cycle
+            cycle_ref[pl.ds(k * half, half), :] = jnp.where(here, 1.0, 0.0).astype(BF)
+
+    return kernel
+
+
 def power_kernel(views, slab, depth, lateral, count):
     rows, half = slab * depth, lateral // 2
 
     def kernel(
-        place,
         est_ref,
         part_ref,
         pair_ref,
@@ -385,7 +429,7 @@
         waves_ref,
         high_ref,
         low_ref,
-        map_ref,
+        cycle_ref,
         re_ref,
         im_ref,
         tre_ref,
@@ -396,7 +440,7 @@
         mtim_ref,
         sum_ref,
     ):
-        even = place[2] == 0
+        even = is_even()
         args = (est_ref, part_ref, pair_ref, other_ref, one_ref, waves_ref, high_ref, low_ref)
         re1, im1, tre1, tim1 = spectrum(even, 1.0 / views, rows, half, *args)
         re0, im0, tre0, tim0 = re_ref[...], im_ref[...], tre_ref[...], tim_ref[...]
@@ -426,20 +470,16 @@
         ):
             tops.append(jnp.sum(over_slab(a * b + c * d), axis=0, keepdims=True))
         top = jnp.sum(jnp.concatenate(tops, axis=0), axis=1, keepdims=True)
-        total = jnp.zeros((9, CYCLES), F32)
-        cycle = iota((CYCLES, half), 0)
+        terms = []
         for k in range(depth // 2 + 1):
             other = depth - k
-            terms = [p[k : k + 1] + p[other : other + 1] if 0 < k < other else p[k : k + 1] for p in powers]
-            term = jnp.concatenate(terms, axis=0)
-            high = term.astype(BF).astype(F32)
-            middle = (term - high).astype(BF).astype(F32)
-            low = term - high - middle
-            term = jnp.concatenate([high, middle, low], axis=0).astype(BF)
-            onehot = (map_ref[0, k : k + 1, 0:half] == cycle).astype(F32).astype(BF)
-            total = total + lax.dot_general(
-                term, onehot, (((1,), (1,)), ((), ())), preferred_element_type=F32
-            )
+            fold = [p[k : k + 1] + p[other : other + 1] if 0 < k < other else p[k : k + 1] for p in powers]
+            terms.append(jnp.concatenate(fold, axis=0))
+        term = jnp.concatenate(terms, axis=1)
+        high = term.astype(BF).astype(F32)
+        middle = (term - high).astype(BF).astype(F32)
+        low = term - high - middle
+        total = dot(jnp.concatenate([high, middle, low], axis=0).astype(BF), cycle_ref[...])
         last = jnp.where(iota((3, CYCLES), 1) == CYCLES - 1, top, 0.0)
         total = total[0:3] + total[3:6] + total[6:9] + last
         for i in range(count):
@@ -496,7 +536,6 @@
     ext_rows = rows + 2 * edge
     half = lateral // 2
     count = lax.axis_size("tile")
-    index = lax.axis_index("tile")
     pairs = [(i, i ^ 1) for i in range(count)]
     others = [(i, i + 1) for i in range(1, count - 1, 2)]
     others = others + [(b, a) for a, b in others]
@@ -505,55 +544,49 @@
         other = lax.ppermute(to_other, "tile", others)
         return lax.ppermute(to_pair, "tile", pairs), other
 
-    def whole(array):
-        return pl.BlockSpec(array.shape, lambda i: (0,) * len(array.shape))
-
-    def half_of(array, h, size=None, at=0):
-        shape = (1,) + array.shape[1:] if size is None else (1, size) + array.shape[2:]
-        return pl.BlockSpec(shape, lambda i: (h, at) + (0,) * (len(shape) - 2))
+    vmem = pl.BlockSpec(memory_space=pltpu.VMEM)
+    scalars = pl.BlockSpec(memory_space=pltpu.SMEM)
 
     def call(kernel, inputs, outputs, name, scratch=(), flops=0):
-        arrays = [x[0] if isinstance(x, tuple) else x for x in inputs]
-        specs = []
-        for x in inputs:
-            if isinstance(x, tuple):
-                specs.append(x[1])
-            else:
-                specs.append(whole(x))
         bytes_moved = sum(int(np.prod(s.shape)) * s.dtype.itemsize for s in outputs)
         return pl.pallas_call(
             kernel,
-            grid=(1,),
-            in_specs=specs,
-            out_specs=tuple(whole(s) for s in outputs),
+            in_specs=[scalars if isinstance(x, tuple) else vmem for x in inputs],
+            out_specs=tuple(vmem for _ in outputs),
             out_shape=tuple(outputs),
             scratch_shapes=list(scratch),
             cost_estimate=pl.CostEstimate(flops=flops, bytes_accessed=2 * bytes_moved, transcendentals=0),
             compiler_params=pltpu.CompilerParams(vmem_limit_bytes=VMEM_LIMIT),
             name=name,
-        )(*arrays)
+        )(*[x[0] if isinstance(x, tuple) else x for x in inputs])
 
     def shaped(*shape, dtype=F32):
         return jax.ShapeDtypeStruct(shape, dtype)
 
-    scalars = pl.BlockSpec(memory_space=pltpu.SMEM)
     data = data_halves.reshape(2, views, rows, lateral)
-    start = jnp.mean(data.astype(F32), axis=1).astype(BF)
-    even = index % 2 == 0
-    low, high = start[:, :edge], start[:, rows - edge :]
-    pair0, other0 = exchange(jnp.where(even, high, low), jnp.where(even, low, high))
+    data, to_pair, to_other = pl.pallas_call(
+        edge_kernel(views, rows, edge),
+        in_specs=[pl.BlockSpec(memory_space=pltpu.HBM)],
+        out_specs=(vmem, vmem, vmem),
+        out_shape=(
+            shaped(2, views, rows, lateral, dtype=BF),
+            shaped(2, edge, lateral, dtype=BF),
+            shaped(2, edge, lateral, dtype=BF),
+        ),
+        scratch_shapes=[pltpu.SemaphoreType.DMA((2 * views,))],
+        compiler_params=pltpu.CompilerParams(vmem_limit_bytes=VMEM_LIMIT),
+        name="edges",
+    )(data)
+    pair0, other0 = exchange(to_pair, to_other)
 
     kernels = psf_taps / jnp.sum(psf_taps, axis=-1, keepdims=True)
-    place = (jnp.stack([index * slab, jnp.int32(count * slab), index % 2]), scalars)
     band = shaped(views, 256, 256, dtype=BF)
     *mats, shape, one0, one1 = call(
         prep_kernel(views, taps, slab, depth, lateral),
-        [(kernels.reshape(-1), scalars), place],
+        [(kernels.reshape(-1),)],
         [
             shaped(views * rows, ext_rows, dtype=BF),
             shaped(ext_rows, views * rows, dtype=BF),
-            band,
-            band,
             band,
             band,
             shaped(2, views * rows, 128),
@@ -567,12 +600,20 @@
         flops=4 * 10**9,
     )
 
+    (cycles,) = call(
+        cycle_kernel(depth, half),
+        [cycle_map],
+        [shaped((depth // 2 + 1) * half, CYCLES, dtype=BF)],
+        "cycles",
+        flops=10**9,
+    )
+
     held = [pltpu.VMEM((views * rows, lateral), BF)]
     firsts = []
     for h in range(2):
         own, to_pair, to_other = call(
-            first_kernel(views, slab, rows, edge),
-            [place, (data, half_of(data, h)), (pair0, half_of(pair0, h)), (other0, half_of(other0, h))] + mats,
+            first_kernel(h, views, slab, rows, edge),
+            [data, pair0, other0] + mats,
             [shaped(1, rows, lateral)] + [shaped(1, 2 * edge, lateral, dtype=BF)] * 2,
             f"first{h}",
             held,
@@ -588,7 +629,7 @@
     table = shaped(2 * rows, rows, dtype=BF)
     waves, back, table_hi, table_lo = call(
         table_kernel(slab, depth, lateral),
-        [quarter, wave, (firsts[1][0], pl.BlockSpec((1, 8, 128), lambda i: (0, 0, 0)))],
+        [quarter, wave, firsts[1][0]],
         [shaped(lateral, lateral, dtype=BF), shaped(lateral, lateral, dtype=BF), table, table],
         "tables",
         flops=2 * 10**9,
@@ -598,8 +639,8 @@
     for h in range(2):
         own, to_pair, to_other, pair, other = firsts[h]
         est, part, to_pair, to_other = call(
-            second_kernel(views, slab, rows, edge, lateral),
-            [place, (data, half_of(data, h)), (pair0, half_of(pair0, h)), (other0, half_of(other0, h))]
+            second_kernel(h, views, slab, rows, edge, lateral),
+            [data, pair0, other0]
             + [own, to_pair, to_other, pair, other, shape, one0]
             + mats,
             [shaped(1, rows, lateral)] * 2 + [shaped(1, edge, lateral, dtype=BF)] * 2,
@@ -613,14 +654,14 @@
     tables = [one1, waves, table_hi, table_lo]
     spectra = call(
         spectrum_kernel(views, slab, depth, lateral),
-        [place, *seconds[0]] + tables,
+        [*seconds[0]] + tables,
         [plane, plane, top, top],
         "spectrum0",
         flops=10**9,
     )
     *mixed, sums = call(
         power_kernel(views, slab, depth, lateral, count),
-        [place, *seconds[1]] + tables + [cycle_map, *spectra],
+        [*seconds[1]] + tables + [cycles, *spectra],
         [plane, plane, top, top, shaped(count, 3, CYCLES)],
         "spectrum1",
         flops=2 * 10**9,
@@ -628,7 +669,7 @@
     sums = lax.all_to_all(sums, "tile", 0, 0)
     (joined,) = call(
         inverse_kernel(slab, depth, lateral, count),
-        [(cutoff, scalars), sums, cycle_map, *mixed, back, table_hi, table_lo],
+        [(cutoff,), sums, cycle_map, *mixed, back, table_hi, table_lo],
         [shaped(rows, lateral)],
         "inverse",
         flops=10**9,

time: 66.1 us -> 62.2 us (0.941)
  Pallas kernels: 25.9 us -> 21.3 us
  other arithmetic: 2.54 us -> 0.17 us
  local copies, waits for them, and re-layouts: 0.12 us -> 1.71 us
  starting transfers between devices: 30 us -> 31.5 us
    pallas_call x9 -> x11, Pallas kernels: 25.9 us -> 21.3 us  [the longest x10 20.6 us: call(): pl.pallas_call(kernel, in_specs=[scalars if isinstance(x, tuple) else vme...]
    reduce_sum x1 -> x0, other arithmetic: 2.13 us -> none  [body(): start = jnp.mean(data.astype(F32), axis=1).astype(BF)]
    unnamed x10, local copies, waits for them, and re-layouts: 0.03 us -> 1.61 us
    all_to_all x1, starting transfers between devices: 8.96 us -> 10.4 us  [body(): sums = lax.all_to_all(sums, 'tile', 0, 0)]
  transfers between devices with their start and end apart: 11 -> 11, of which waited for: 1 -> 1; matrix products, arithmetic and copies ran while one was open for 1% -> 0% of each run, Pallas kernels for 25% -> 22%
where the time goes in v1:
time: 62.2 us; the launch traced here: 61.9 us
  starting transfers between devices  31.5 us (51%)
  Pallas kernels  21.3 us (34%)
  waiting for transfers between devices  6.28 us (10%)
  local copies, waits for them, and re-layouts  1.71 us (3%)
  between operations  0.9 us (1%)
    pallas_call x10, Pallas kernels, call(): pl.pallas_call(kernel, in_specs=[scalars if isinstance(x, tuple) else vme...  20.6 us
    ppermute x5, starting transfers between devices, exchange(): return (lax.ppermute(to_pair, 'tile', pairs), other)  17.7 us
    all_to_all x1, starting transfers between devices, body(): sums = lax.all_to_all(sums, 'tile', 0, 0)  10.4 us
    all_to_all x1, waiting for transfers between devices, body(): sums = lax.all_to_all(sums, 'tile', 0, 0)  6.25 us
    ppermute x5, starting transfers between devices, exchange(): other = lax.ppermute(to_other, 'tile', others)  3.49 us
    unnamed x10, local copies, waits for them, and re-layouts  1.61 us
  transfers between devices with their start and end apart: 11, of which 1 were waited for; matrix products, arithmetic and copies ran while one was open for 0% of the time, Pallas kernels for 22%

profile of v1, /device:TPU:0, one launch (start us, length us, event | category | flops | bytes accessed | tf_op | source)
XLA Modules:
  0.0 61.9 jit_solution(14155208548695683072)
XLA Ops:
  0.0 1.6 %copy-done = bf16[2,4,8,32,512]{4,3,2,1,0:T(8,128)(2,1)S(1)} copy-done((bf16[2,4,8,32,512]{4,3,2,1,0:T(8,128)(2,1)S(1)}, bf16[2,4,8,32,512]{4,3,2,1,0:T(8,128)(2,1)}, u32[]{:S(2)}) %copy-start) | copy-done | bytes 2097176
  1.6 0.7 %edges.1 = (bf16[2,4,256,512]{3,2,1,0:T(8,128)(2,1)S(1)}, bf16[2,128,512]{2,1,0:T(8,128)(2,1)S(1)}, bf16[2,128,512]{2,1,0:T(8,128)(2,1)S(1)}) custom-call(bf16[2,4,256,512]{3,2,1,0:T(8,128)(2,1)S(1)} %bitcast.2), custom_call_target="tpu_custom_call" | custom-call | tf_op jit(solution)/shard_map/edges/pallas_call | solution.py:567
  2.3 0.6 collective-permute-start
  2.9 0.7 %collective-permute-start.1 = (bf16[2,128,512]{2,1,0:T(8,128)(2,1)S(1)}, bf16[2,128,512]{2,1,0:T(8,128)(2,1)S(1)}, u32[]{:S(2)}, u32[]{:S(2)}) collective-permute-start(bf16[2,128,512]{2,1,0:T(8,128)(2,1)S(1)} %get-tuple-element.47), channel_id=1, source_target_pairs={{1,2},{3,4},{5,6},{7,8},{9,10},{11,12},{13,14},{2,1},{4,3},{6,5},{... | collective-permute-start | bytes 786440 | tf_op jit(solution)/shard_map/ppermute | solution.py:544
  3.5 0.1 reduce_sum.9
  3.6 0.1 broadcast_divide_fusion
  3.7 0.1 reshape.11.kern
  3.8 0.7 %cycles.1.cycle_ref = bf16[4352,256]{1,0:T(8,128)(2,1)S(1)} custom-call(s32[1,32,512]{2,1,0:T(8,128)S(1)} %copy-done.1), custom_call_target="tpu_custom_call" | custom-call | flops 1000000000 | bytes 4456448 | tf_op jit(solution)/shard_map/cycles/pallas_call | solution.py:552
  4.6 2.1 %prep.1 = (bf16[1024,512]{1,0:T(8,128)(2,1)S(1)}, bf16[512,1024]{1,0:T(8,128)(2,1)S(1)}, bf16[4,256,256]{2,1,0:T(8,128)(2,1)S(1)}, bf16[4,256,256]{2,1,0:T(8,128...) custom-call(f32[108]{0:T(128)S(1)} %reshape.11.kern), custom_call_target="tpu_custom_call" | custom-call | flops 4000000000 | bytes 12091392 | tf_op jit(solution)/shard_map/prep/pallas_call | solution.py:552
  6.7 2.7 %first0.1 = (f32[1,256,512]{2,1,0:T(8,128)S(1)}, bf16[1,256,512]{2,1,0:T(8,128)(2,1)S(1)}, bf16[1,256,512]{2,1,0:T(8,128)(2,1)S(1)}) custom-call(bf16[2,4,256,512]{3,2,1,0:T(8,128)(2,1)S(1)} %get-tuple-element.45.data_ref, bf16[2,128,512]{2,1,0:T(8,128)(2,1)S(1)} %collective-permute-done.pair_ref.pair0_ref, ...), custom_call_target="tpu_custom_call" | custom-call | flops 4000000000 | bytes 2097152 | tf_op jit(solution)/shard_map/first0/pallas_call | solution.py:552
  9.5 6.9 %collective-permute-start.6 = (bf16[1,256,512]{2,1,0:T(8,128)(2,1)S(1)}, bf16[1,256,512]{2,1,0:T(8,128)(2,1)S(1)}, u32[]{:S(2)}, u32[]{:S(2)}) collective-permute-start(bf16[1,256,512]{2,1,0:T(8,128)(2,1)S(1)} %get-tuple-element.69.sent_pair), channel_id=1, source_target_pairs={{0,1},{1,0},{2,3},{3,2},{4,5},{5,4},{6,7},{7,6},{8,9},{9,8},{10,11... | collective-permute-start | bytes 786440 | tf_op jit(solution)/shard_map/ppermute | solution.py:545
  16.3 0.7 %collective-permute-start.7 = (bf16[1,256,512]{2,1,0:T(8,128)(2,1)S(1)}, bf16[1,256,512]{2,1,0:T(8,128)(2,1)S(1)}, u32[]{:S(2)}, u32[]{:S(2)}) collective-permute-start(bf16[1,256,512]{2,1,0:T(8,128)(2,1)S(1)} %get-tuple-element.70.sent_other), channel_id=1, source_target_pairs={{1,2},{3,4},{5,6},{7,8},{9,10},{11,12},{13,14},{2,1},{4,3},{6,5},{... | collective-permute-start | bytes 786440 | tf_op jit(solution)/shard_map/ppermute | solution.py:544
  17.0 2.7 %first1.1 = (f32[1,256,512]{2,1,0:T(8,128)S(1)}, bf16[1,256,512]{2,1,0:T(8,128)(2,1)S(1)}, bf16[1,256,512]{2,1,0:T(8,128)(2,1)S(1)}) custom-call(bf16[2,4,256,512]{3,2,1,0:T(8,128)(2,1)S(1)} %get-tuple-element.45.data_ref, bf16[2,128,512]{2,1,0:T(8,128)(2,1)S(1)} %collective-permute-done.pair_ref.pair0_ref, ...), custom_call_target="tpu_custom_call" | custom-call | flops 4000000000 | bytes 2097152 | tf_op jit(solution)/shard_map/first1/pallas_call | solution.py:552
  19.8 3.8 %collective-permute-start.2 = (bf16[1,256,512]{2,1,0:T(8,128)(2,1)S(1)}, bf16[1,256,512]{2,1,0:T(8,128)(2,1)S(1)}, u32[]{:S(2)}, u32[]{:S(2)}) collective-permute-start(bf16[1,256,512]{2,1,0:T(8,128)(2,1)S(1)} %get-tuple-element.56.sent_pair), channel_id=1, source_target_pairs={{0,1},{1,0},{2,3},{3,2},{4,5},{5,4},{6,7},{7,6},{8,9},{9,8},{10,11... | collective-permute-start | bytes 786440 | tf_op jit(solution)/shard_map/ppermute | solution.py:545
  23.6 0.7 %collective-permute-start.3 = (bf16[1,256,512]{2,1,0:T(8,128)(2,1)S(1)}, bf16[1,256,512]{2,1,0:T(8,128)(2,1)S(1)}, u32[]{:S(2)}, u32[]{:S(2)}) collective-permute-start(bf16[1,256,512]{2,1,0:T(8,128)(2,1)S(1)} %get-tuple-element.57.sent_other), channel_id=1, source_target_pairs={{1,2},{3,4},{5,6},{7,8},{9,10},{11,12},{13,14},{2,1},{4,3},{6,5},{... | collective-permute-start | bytes 786440 | tf_op jit(solution)/shard_map/ppermute | solution.py:544
  24.2 0.0 collective-permute-done.6.pair_ref
  24.3 2.9 %second0.1 = (f32[1,256,512]{2,1,0:T(8,128)S(1)}, f32[1,256,512]{2,1,0:T(8,128)S(1)}, bf16[1,128,512]{2,1,0:T(8,128)(2,1)S(1)}, bf16[1,128,512]{2,1,0:T(8,128)(2,1)S(1)}) custom-call(bf16[2,4,256,512]{3,2,1,0:T(8,128)(2,1)S(1)} %get-tuple-element.45.data_ref, bf16[2,128,512]{2,1,0:T(8,128)(2,1)S(1)} %collective-permute-done.pair_ref.pair0_ref, ...), custom_call_target="tpu_custom_call" | custom-call | flops 4000000000 | bytes 2621440 | tf_op jit(solution)/shard_map/second0/pallas_call | solution.py:552
  27.2 3.4 %collective-permute-start.8 = (bf16[1,128,512]{2,1,0:T(8,128)(2,1)S(1)}, bf16[1,128,512]{2,1,0:T(8,128)(2,1)S(1)}, u32[]{:S(2)}, u32[]{:S(2)}) collective-permute-start(bf16[1,128,512]{2,1,0:T(8,128)(2,1)S(1)} %get-tuple-element.73), channel_id=1, source_target_pairs={{0,1},{1,0},{2,3},{3,2},{4,5},{5,4},{6,7},{7,6},{8,9},{9,8},{10,11... | collective-permute-start | bytes 393224 | tf_op jit(solution)/shard_map/ppermute | solution.py:545
  30.6 0.8 %collective-permute-start.9 = (bf16[1,128,512]{2,1,0:T(8,128)(2,1)S(1)}, bf16[1,128,512]{2,1,0:T(8,128)(2,1)S(1)}, u32[]{:S(2)}, u32[]{:S(2)}) collective-permute-start(bf16[1,128,512]{2,1,0:T(8,128)(2,1)S(1)} %get-tuple-element.74), channel_id=1, source_target_pairs={{1,2},{3,4},{5,6},{7,8},{9,10},{11,12},{13,14},{2,1},{4,3},{6,5},{... | collective-permute-start | bytes 393224 | tf_op jit(solution)/shard_map/ppermute | solution.py:544
  31.4 0.0 collective-permute-done.3.other_ref
  31.4 0.0 copy-start.2
  31.5 0.0 copy-start.3
  31.5 2.9 %second1.1 = (f32[1,256,512]{2,1,0:T(8,128)S(1)}, f32[1,256,512]{2,1,0:T(8,128)S(1)}, bf16[1,128,512]{2,1,0:T(8,128)(2,1)S(1)}, bf16[1,128,512]{2,1,0:T(8,128)(2,1)S(1)}) custom-call(bf16[2,4,256,512]{3,2,1,0:T(8,128)(2,1)S(1)} %get-tuple-element.45.data_ref, bf16[2,128,512]{2,1,0:T(8,128)(2,1)S(1)} %collective-permute-done.pair_ref.pair0_ref, ...), custom_call_target="tpu_custom_call" | custom-call | flops 4000000000 | bytes 2621440 | tf_op jit(solution)/shard_map/second1/pallas_call | solution.py:552
  34.4 3.1 %collective-permute-start.4 = (bf16[1,128,512]{2,1,0:T(8,128)(2,1)S(1)}, bf16[1,128,512]{2,1,0:T(8,128)(2,1)S(1)}, u32[]{:S(2)}, u32[]{:S(2)}) collective-permute-start(bf16[1,128,512]{2,1,0:T(8,128)(2,1)S(1)} %get-tuple-element.62), channel_id=1, source_target_pairs={{0,1},{1,0},{2,3},{3,2},{4,5},{5,4},{6,7},{7,6},{8,9},{9,8},{10,11... | collective-permute-start | bytes 393224 | tf_op jit(solution)/shard_map/ppermute | solution.py:545
  37.5 0.7 %collective-permute-start.5 = (bf16[1,128,512]{2,1,0:T(8,128)(2,1)S(1)}, bf16[1,128,512]{2,1,0:T(8,128)(2,1)S(1)}, u32[]{:S(2)}, u32[]{:S(2)}) collective-permute-start(bf16[1,128,512]{2,1,0:T(8,128)(2,1)S(1)} %get-tuple-element.63), channel_id=1, source_target_pairs={{1,2},{3,4},{5,6},{7,8},{9,10},{11,12},{13,14},{2,1},{4,3},{6,5},{... | collective-permute-start | bytes 393224 | tf_op jit(solution)/shard_map/ppermute | solution.py:544
  38.1 1.1 %tables.1 = (bf16[512,512]{1,0:T(8,128)(2,1)S(1)}, bf16[512,512]{1,0:T(8,128)(2,1)S(1)}, bf16[512,256]{1,0:T(8,128)(2,1)S(1)}, bf16[512,256]{1,0:T(8,128)(2,1)S(1)}) custom-call(f32[2,128]{1,0:T(2,128)S(1)} %copy-done.3, f32[2,32,128]{2,1,0:T(8,128)S(1)} %copy-done.2, f32[1,256,512]{2,1,0:T(8,128)S(1)} %get-tuple-element.55.own_ref._), custom_call_target="tpu_custom_call" | custom-call | flops 2000000000 | bytes 3145728 | tf_op jit(solution)/shard_map/tables/pallas_call | solution.py:552
  39.2 0.0 collective-permute-done.8.pair_ref
  39.3 0.9 %spectrum0.1 = (f32[256,256]{1,0:T(8,128)S(1)}, f32[256,256]{1,0:T(8,128)S(1)}, f32[256,128]{1,0:T(8,128)S(1)}, f32[256,128]{1,0:T(8,128)S(1)}) custom-call(f32[1,256,512]{2,1,0:T(8,128)S(1)} %get-tuple-element.71.est_ref, f32[1,256,512]{2,1,0:T(8,128)S(1)} %get-tuple-element.72.part_ref, bf16[1,128,512]{2,1,0:T(8,128)(2,1)S(1)} %collective-permute-done.8.pair_ref, ...), custom_call_target="tpu_custom_call" | custom-call | flops 1000000000 | bytes 1572864 | tf_op jit(solution)/shard_map/spectrum0/pallas_call | solution.py:552
  40.2 2.6 %spectrum1.1 = (f32[256,256]{1,0:T(8,128)S(1)}, f32[256,256]{1,0:T(8,128)S(1)}, f32[256,128]{1,0:T(8,128)S(1)}, f32[256,128]{1,0:T(8,128)S(1)}, f32[16,3,256]{2,1,0:T(4,128)}) custom-call(f32[1,256,512]{2,1,0:T(8,128)S(1)} %get-tuple-element.60.est_ref, f32[1,256,512]{2,1,0:T(8,128)S(1)} %get-tuple-element.61.part_ref, ...), custom_call_target="tpu_custom_call" | custom-call | flops 2000000000 | bytes 1671168 | tf_op jit(solution)/shard_map/spectrum1/pallas_call | solution.py:552
  42.7 10.4 %all-to-all-start = ((f32[16,3,256]{2,1,0:T(4,128)}), f32[16,3,256]{2,1,0:T(4,128)S(1)}, u32[]{:S(2)}, u32[]{:S(2)}) async-start(f32[16,3,256]{2,1,0:T(4,128)} %get-tuple-element.79), calls=%async_computation | async-start | bytes 131072 | tf_op jit(solution)/shard_map/all_to_all | solution.py:669
  53.7 6.2 %all-to-all-done.sum_ref = f32[16,3,256]{2,1,0:T(4,128)S(1)} async-done(((f32[16,3,256]{2,1,0:T(4,128)}), f32[16,3,256]{2,1,0:T(4,128)S(1)}, u32[]{:S(2)}, u32[]{:S(2)}) %all-to-all-start) | async-done | bytes 49184 | tf_op jit(solution)/shard_map/all_to_all | solution.py:669
  60.0 1.9 %inverse.1 = f32[256,512]{1,0:T(8,128)} custom-call(s32[1]{0:T(128)S(6)} %copy.9.cut_ref, f32[16,3,256]{2,1,0:T(4,128)S(1)} %all-to-all-done.sum_ref, s32[1,32,512]{2,1,0:T(8,128)S(1)} %copy-done.1, f32[256,256]{1,0:T(8,128)S(1)} %get-tuple-element.80.mre_ref, f32[256,256]{1,0:T(8,128)S(1)} %get-tuple-element.81.mim_ref, ...), custom_call_target="tpu_custom_call" | custom-call | flops 1000000000 | bytes 1048576 | tf_op jit(solution)/shard_map/inverse/pallas_call | solution.py:552
  (15 shorter events, 0.0 us)
Async XLA Ops:
  0.0 1.6 %copy-start = (bf16[2,4,8,32,512]{4,3,2,1,0:T(8,128)(2,1)S(1)}, bf16[2,4,8,32,512]{4,3,2,1,0:T(8,128)(2,1)}, u32[]{:S(2)}) copy-start(bf16[2,4,8,32,512]{4,3,2,1,0:T(8,128)(2,1)} %param.6) | copy-start | bytes 6291460
  1.6 1.9 %copy-start.4 = (f32[4,3,9]{2,0,1:T(4,128)S(1)}, f32[4,3,9]{2,0,1:T(4,128)}, u32[]{:S(2)}) copy-start(f32[4,3,9]{2,0,1:T(4,128)} %param.7) | copy-start | bytes 1300
  1.6 2.2 %copy-start.1 = (s32[1,32,512]{2,1,0:T(8,128)S(1)}, s32[1,32,512]{2,1,0:T(8,128)}, u32[]{:S(2)}) copy-start(s32[1,32,512]{2,1,0:T(8,128)} %map_ref.3) | copy-start | bytes 196612
  2.3 4.4 %collective-permute-start = (bf16[2,128,512]{2,1,0:T(8,128)(2,1)S(1)}, bf16[2,128,512]{2,1,0:T(8,128)(2,1)S(1)}, u32[]{:S(2)}, u32[]{:S(2)}) collective-permute-start(bf16[2,128,512]{2,1,0:T(8,128)(2,1)S(1)} %get-tuple-element.46), channel_id=1, source_target_pairs={{0,1},{1,0},{2,3},{3,2},{4,5},{5,4},{6,7},{7,6},{8,9},{9,8},{10,11... | collective-permute-start | bytes 786440 | tf_op jit(solution)/shard_map/ppermute | solution.py:545
  2.9 3.8 %collective-permute-start.1 = (bf16[2,128,512]{2,1,0:T(8,128)(2,1)S(1)}, bf16[2,128,512]{2,1,0:T(8,128)(2,1)S(1)}, u32[]{:S(2)}, u32[]{:S(2)}) collective-permute-start(bf16[2,128,512]{2,1,0:T(8,128)(2,1)S(1)} %get-tuple-element.47), channel_id=1, source_target_pairs={{1,2},{3,4},{5,6},{7,8},{9,10},{11,12},{13,14},{2,1},{4,3},{6,5},{... | collective-permute-start | bytes 786440 | tf_op jit(solution)/shard_map/ppermute | solution.py:544
  9.5 14.8 %collective-permute-start.6 = (bf16[1,256,512]{2,1,0:T(8,128)(2,1)S(1)}, bf16[1,256,512]{2,1,0:T(8,128)(2,1)S(1)}, u32[]{:S(2)}, u32[]{:S(2)}) collective-permute-start(bf16[1,256,512]{2,1,0:T(8,128)(2,1)S(1)} %get-tuple-element.69.sent_pair), channel_id=1, source_target_pairs={{0,1},{1,0},{2,3},{3,2},{4,5},{5,4},{6,7},{7,6},{8,9},{9,8},{10,11... | collective-permute-start | bytes 786440 | tf_op jit(solution)/shard_map/ppermute | solution.py:545
  16.3 7.9 %collective-permute-start.7 = (bf16[1,256,512]{2,1,0:T(8,128)(2,1)S(1)}, bf16[1,256,512]{2,1,0:T(8,128)(2,1)S(1)}, u32[]{:S(2)}, u32[]{:S(2)}) collective-permute-start(bf16[1,256,512]{2,1,0:T(8,128)(2,1)S(1)} %get-tuple-element.70.sent_other), channel_id=1, source_target_pairs={{1,2},{3,4},{5,6},{7,8},{9,10},{11,12},{13,14},{2,1},{4,3},{6,5},{... | collective-permute-start | bytes 786440 | tf_op jit(solution)/shard_map/ppermute | solution.py:544
  19.8 11.7 %collective-permute-start.2 = (bf16[1,256,512]{2,1,0:T(8,128)(2,1)S(1)}, bf16[1,256,512]{2,1,0:T(8,128)(2,1)S(1)}, u32[]{:S(2)}, u32[]{:S(2)}) collective-permute-start(bf16[1,256,512]{2,1,0:T(8,128)(2,1)S(1)} %get-tuple-element.56.sent_pair), channel_id=1, source_target_pairs={{0,1},{1,0},{2,3},{3,2},{4,5},{5,4},{6,7},{7,6},{8,9},{9,8},{10,11... | collective-permute-start | bytes 786440 | tf_op jit(solution)/shard_map/ppermute | solution.py:545
  23.6 7.9 %collective-permute-start.3 = (bf16[1,256,512]{2,1,0:T(8,128)(2,1)S(1)}, bf16[1,256,512]{2,1,0:T(8,128)(2,1)S(1)}, u32[]{:S(2)}, u32[]{:S(2)}) collective-permute-start(bf16[1,256,512]{2,1,0:T(8,128)(2,1)S(1)} %get-tuple-element.57.sent_other), channel_id=1, source_target_pairs={{1,2},{3,4},{5,6},{7,8},{9,10},{11,12},{13,14},{2,1},{4,3},{6,5},{... | collective-permute-start | bytes 786440 | tf_op jit(solution)/shard_map/ppermute | solution.py:544
  27.2 12.1 %collective-permute-start.8 = (bf16[1,128,512]{2,1,0:T(8,128)(2,1)S(1)}, bf16[1,128,512]{2,1,0:T(8,128)(2,1)S(1)}, u32[]{:S(2)}, u32[]{:S(2)}) collective-permute-start(bf16[1,128,512]{2,1,0:T(8,128)(2,1)S(1)} %get-tuple-element.73), channel_id=1, source_target_pairs={{0,1},{1,0},{2,3},{3,2},{4,5},{5,4},{6,7},{7,6},{8,9},{9,8},{10,11... | collective-permute-start | bytes 393224 | tf_op jit(solution)/shard_map/ppermute | solution.py:545
  30.6 8.7 %collective-permute-start.9 = (bf16[1,128,512]{2,1,0:T(8,128)(2,1)S(1)}, bf16[1,128,512]{2,1,0:T(8,128)(2,1)S(1)}, u32[]{:S(2)}, u32[]{:S(2)}) collective-permute-start(bf16[1,128,512]{2,1,0:T(8,128)(2,1)S(1)} %get-tuple-element.74), channel_id=1, source_target_pairs={{1,2},{3,4},{5,6},{7,8},{9,10},{11,12},{13,14},{2,1},{4,3},{6,5},{... | collective-permute-start | bytes 393224 | tf_op jit(solution)/shard_map/ppermute | solution.py:544
  31.4 6.7 %copy-start.2 = (f32[2,32,128]{2,1,0:T(8,128)S(1)}, f32[2,32,128]{2,1,0:T(8,128)}, u32[]{:S(2)}) copy-start(f32[2,32,128]{2,1,0:T(8,128)} %constant.7.clone.wave_ref) | copy-start | bytes 98308
  31.5 6.7 %copy-start.3 = (f32[2,128]{1,0:T(2,128)S(1)}, f32[2,128]{1,0:T(2,128)}, u32[]{:S(2)}) copy-start(f32[2,128]{1,0:T(2,128)} %constant.6.clone.quarter_ref) | copy-start | bytes 3076
  34.4 5.7 %collective-permute-start.4 = (bf16[1,128,512]{2,1,0:T(8,128)(2,1)S(1)}, bf16[1,128,512]{2,1,0:T(8,128)(2,1)S(1)}, u32[]{:S(2)}, u32[]{:S(2)}) collective-permute-start(bf16[1,128,512]{2,1,0:T(8,128)(2,1)S(1)} %get-tuple-element.62), channel_id=1, source_target_pairs={{0,1},{1,0},{2,3},{3,2},{4,5},{5,4},{6,7},{7,6},{8,9},{9,8},{10,11... | collective-permute-start | bytes 393224 | tf_op jit(solution)/shard_map/ppermute | solution.py:545
  37.5 2.7 %collective-permute-start.5 = (bf16[1,128,512]{2,1,0:T(8,128)(2,1)S(1)}, bf16[1,128,512]{2,1,0:T(8,128)(2,1)S(1)}, u32[]{:S(2)}, u32[]{:S(2)}) collective-permute-start(bf16[1,128,512]{2,1,0:T(8,128)(2,1)S(1)} %get-tuple-element.63), channel_id=1, source_target_pairs={{1,2},{3,4},{5,6},{7,8},{9,10},{11,12},{13,14},{2,1},{4,3},{6,5},{... | collective-permute-start | bytes 393224 | tf_op jit(solution)/shard_map/ppermute | solution.py:544
  42.7 17.3 %all-to-all-start = ((f32[16,3,256]{2,1,0:T(4,128)}), f32[16,3,256]{2,1,0:T(4,128)S(1)}, u32[]{:S(2)}, u32[]{:S(2)}) async-start(f32[16,3,256]{2,1,0:T(4,128)} %get-tuple-element.79), calls=%async_computation | async-start | bytes 131072 | tf_op jit(solution)/shard_map/all_to_all | solution.py:669

commit v2 on v1

--- a/solution.py
+++ b/solution.py
@@ -5,6 +5,7 @@
 from jax.experimental import pallas as pl
 from jax.experimental.pallas import tpu as pltpu
 from jax.sharding import PartitionSpec as P
+
 
 CYCLES = 256
 BF = jnp.bfloat16
@@ -48,8 +49,13 @@
         first = lax.axis_index("tile") * slab
         rows_total = lax.axis_size("tile") * slab
 
+        all_taps = kern[...]
+
         def tap(v, axis, t):
-            return kern[(v * 3 + axis) * taps + t]
+            return all_taps[v * 3 + axis : v * 3 + axis + 1, t : t + 1]
+
+        def spread(x):
+            return jnp.concatenate([x] * (depth // 8), axis=0)
 
         def ones(v, axis, index, count, flip):
             summed = jnp.zeros(index.shape, F32)
@@ -62,12 +68,11 @@
         row = iota((depth, 128), 0)
         lane = iota((depth, 128), 1)
         cell = lax.rem(lane, depth)
-        slot = lane // depth
+        slot8 = iota((8, 128), 1) // depth
         gap_z = cell - row + radius
         gap_zt = row - cell + radius
-        gap = iota((128, 128), 0) - iota((128, 128), 1) + radius
-        upper_gap = gap[120:128] - 128
-        lower_gap = gap[0:8] + 128
+        lane8 = iota((8, 128), 1)
+        gap8 = iota((8, 128), 0) - lane8
         zero = jnp.zeros((depth, 128), BF)
         tail = jnp.zeros((120, 128), F32)
         gains = []
@@ -78,37 +83,36 @@
             def lane_taps(shift, sign, v=v):
                 pairs = [(j, shift + sign * j) for j in range(group)]
                 pairs = [(j, tap(v, 0, t)) for j, t in pairs if 0 <= t < taps]
-                return lookup(slot, pairs) if pairs else None
+                return lookup(slot8, pairs) if pairs else None
 
             blocks = {}
-            for i in range(slab):
-                for g in range(ext * depth // 128):
+            for i in range(slab // 2):
+                for g in range(ext // 2 // group + 1):
                     d = group * g - i
                     if d not in blocks:
                         weight = lane_taps(d, 1)
-                        blocks[d] = zero if weight is None else (weight * band_z).astype(BF)
-                    a_ref[pl.ds((v * slab + i) * depth, depth), pl.ds(g * 128, 128)] = blocks[d]
-            blocks = {}
-            for i in range(ext):
-                for g in range(rows // 128):
-                    d = i - group * g
-                    if d not in blocks:
-                        weight = lane_taps(d, -1)
-                        blocks[d] = zero if weight is None else (weight * band_zt).astype(BF)
-                    b_ref[pl.ds(i * depth, depth), pl.ds(v * rows + g * 128, 128)] = blocks[d]
+                        blocks[d] = zero if weight is None else (spread(weight) * band_z).astype(BF)
+                    a_ref[pl.ds((v * slab // 2 + i) * depth, depth), pl.ds(g * 128, 128)] = blocks[d]
+            for e in range(slab // 2 + 2 * radius):
+                block = (spread(lane_taps(e, -1)) * band_zt).astype(BF)
+                b_ref[pl.ds(e * depth, depth), pl.ds(v * 128, 128)] = block
 
             for flip, band_ref in ((False, t_ref), (True, tt_ref)):
                 pairs = [(t, tap(v, 2, taps - 1 - t if flip else t)) for t in range(taps)]
-                middle = lookup(gap, pairs).astype(BF)
-                upper = jnp.concatenate([tail, lookup(upper_gap, pairs[:radius])], axis=0).astype(BF)
-                lower = jnp.concatenate([lookup(lower_gap, pairs[radius + 1 :]), tail], axis=0).astype(BF)
+                strip = lookup((gap8 + radius) & 127, pairs)
+                strips = [strip] + [pltpu.roll(strip, 8 * n, 1) for n in range(1, 16)]
+                first_strip = jnp.where(lane8 < 64, strips[0], 0.0)
+                last_strip = jnp.where(lane8 >= 64, strips[15], 0.0)
+                middle = jnp.concatenate([first_strip] + strips[1:15] + [last_strip], axis=0).astype(BF)
+                upper = jnp.concatenate([tail, strips[15] - last_strip], axis=0).astype(BF)
+                lower = jnp.concatenate([strips[0] - first_strip, tail], axis=0).astype(BF)
                 for at, block in ((0, middle), (1, upper), (2, lower), (3, middle)):
                     at_rows, at_cols = pl.ds(at // 2 * 128, 128), pl.ds(at % 2 * 128, 128)
                     band_ref[v, at_rows, at_cols] = block
 
             mid = depth // 2
             sum_xz = jnp.sum(
-                a_ref[pl.ds(v * rows, depth), :].astype(F32)[mid : mid + 1], axis=1, keepdims=True
+                a_ref[pl.ds(v * rows // 2, depth), :].astype(F32)[mid : mid + 1], axis=1, keepdims=True
             )
             sum_y = jnp.sum(t_ref[v, 0:128, :].astype(F32)[64:65], axis=1, keepdims=True)
             gains.append(1.0 / (sum_xz * sum_y))
@@ -144,10 +148,7 @@
             row_ref[v, 0] = ones(v, 2, y_row, lateral, False)
             row_ref[v, 1] = jnp.broadcast_to(gains[v], (8, lateral))
             edges.append((ones(v, 0, x_ext, rows_total, True) * scale, ones(v, 2, y_row, lateral, True)))
-        for n, back, one_ref, low, high in (
-            (0, back0, one0_ref, 0, ext),
-            (1, back1, one1_ref, radius, radius + slab),
-        ):
+        for back, one_ref, low, high in ((back0, one0_ref, 0, ext), (back1, one1_ref, radius, radius + slab)):
             for e in range(low, high):
                 terms = [back[v] * edges[v][0][e : e + 1] for v in range(views)]
                 for j in range(lateral // 128):
@@ -179,6 +180,65 @@
     )
 
 
+def level_of(x):
+    total = jnp.sum(jnp.sum(x, axis=0, keepdims=True), axis=1, keepdims=True)
+    return (total * (1.0 / x.size)).astype(BF).astype(F32)
+
+
+def across(x, lateral):
+    return jnp.concatenate([x] * (lateral // 128), axis=1)
+
+
+def blur_back(n, h, views, slab, rows, level, data_ref, ext, mats, held):
+    a_ref, b_ref, t_ref, tt_ref, base_ref, off_ref, row_ref = mats
+    lateral = ext.shape[1]
+    half = rows // 2
+    seen = a_ref.shape[1]
+    held[0] = dot(a_ref[...], ext[:seen]).astype(BF)
+    held[1] = dot(a_ref[...], ext[half:]).astype(BF)
+    for v in range(views):
+        at = pl.ds(v * half, half)
+        part = jnp.concatenate([held[0, at, :], held[1, at, :]], axis=0)
+        base = across(base_ref[n, pl.ds(v * rows, rows), :], lateral) * (row_ref[v, 0, 0:1, :] * level)
+        predicted = y_blur(part, t_ref[v]) + base
+        scaled = data_ref[h, v].astype(F32) * row_ref[v, 1, 0:1, :]
+        offset = across(jnp.concatenate([off_ref[n, v]] * slab, axis=0), lateral)
+        quotient = (scaled / predicted - offset).astype(BF)
+        back = y_blur(quotient, tt_ref[v]).astype(BF)
+        held[0, at, :] = back[:half]
+        held[1, at, :] = back[half:]
+    low = dot(b_ref[...], held[0])
+    high = dot(b_ref[...], held[1])
+    return jnp.concatenate([low[:half], low[half:] + high[: seen - half], high[seen - half :]], axis=0)
+
+
+def pick(even, from_pair, from_other, h=0):
+    pair = from_pair[h].astype(F32)
+    other = from_other[0].astype(F32)
+    return jnp.where(even, other, pair), jnp.where(even, pair, other)
+
+
+def put(even, low, high, to_pair, to_other, h=0, g=0):
+    @pl.when(even)
+    def _():
+        to_pair[h] = high
+        to_other[g] = low
+
+    @pl.when(jnp.logical_not(even))
+    def _():
+        to_pair[h] = low
+        to_other[g] = high
+
+
+def is_even():
+    return (lax.axis_index("tile") & 1) == 0
+
+
+def has_sides():
+    index = lax.axis_index("tile")
+    return jnp.where(index > 0, 1.0, 0.0), jnp.where(index + 1 < lax.axis_size("tile"), 1.0, 0.0)
+
+
 def mean_views(h, data_ref, views):
     total = data_ref[h, 0].astype(F32)
     for v in range(1, views):
@@ -186,87 +246,34 @@
     return total * (1.0 / views)
 
 
-def level_of(x):
-    total = jnp.sum(jnp.sum(x, axis=0, keepdims=True), axis=1, keepdims=True)
-    return (total * (1.0 / x.size)).astype(BF).astype(F32)
-
-
-def across(x, lateral):
-    return jnp.concatenate([x] * (lateral // 128), axis=1)
-
-
-def blur_back(n, h, views, slab, rows, level, data_ref, ext, mats, held):
-    a_ref, b_ref, t_ref, tt_ref, base_ref, off_ref, row_ref = mats
-    lateral = ext.shape[1]
-    held[...] = dot(a_ref[...], ext).astype(BF)
-    for v in range(views):
-        part = held[pl.ds(v * rows, rows), :]
-        base = across(base_ref[n, pl.ds(v * rows, rows), :], lateral) * (row_ref[v, 0, 0:1, :] * level)
-        predicted = y_blur(part, t_ref[v]) + base
-        scaled = data_ref[h, v].astype(F32) * row_ref[v, 1, 0:1, :]
-        offset = across(jnp.concatenate([off_ref[n, v]] * slab, axis=0), lateral)
-        quotient = (scaled / predicted - offset).astype(BF)
-        held[pl.ds(v * rows, rows), :] = y_blur(quotient, tt_ref[v]).astype(BF)
-    return dot(b_ref[...], held[...])
-
-
-def pick(even, from_pair, from_other, h=0):
-    pair = from_pair[h].astype(F32)
-    other = from_other[h].astype(F32)
-    return jnp.where(even, other, pair), jnp.where(even, pair, other)
-
-
-def put(even, low, high, to_pair, to_other, h=0):
-    @pl.when(even)
-    def _():
-        to_pair[h] = high
-        to_other[h] = low
-
-    @pl.when(jnp.logical_not(even))
-    def _():
-        to_pair[h] = low
-        to_other[h] = high
-
-
-def is_even():
-    return (lax.axis_index("tile") & 1) == 0
-
-
-def has_sides():
-    index = lax.axis_index("tile")
-    return jnp.where(index > 0, 1.0, 0.0), jnp.where(index + 1 < lax.axis_size("tile"), 1.0, 0.0)
-
-
 def edge_kernel(views, rows, edge):
-    def kernel(data_hbm, data_ref, to_pair, to_other, sems):
-        copies = {}
+    def kernel(data_ref, *outs):
+        even = is_even()
+        to_pair = outs[-1]
         for h in range(2):
-            for v in range(views):
-                copies[h, v] = pltpu.make_async_copy(
-                    data_hbm.at[h, v], data_ref.at[h, v], sems.at[h * views + v]
-                )
-                copies[h, v].start()
-        even = is_even()
-        for h in range(2):
-            for v in range(views):
-                copies[h, v].wait()
-            start = mean_views(h, data_ref, views).astype(BF)
-            put(even, start[:edge], start[rows - edge :], to_pair, to_other, h)
+            est_ref, ext_ref, level_ref, to_other = outs[4 * h : 4 * h + 4]
+            est = mean_views(h, data_ref, views)
+            est_ref[...] = est
+            put(even, est[:edge].astype(BF), est[rows - edge :].astype(BF), to_pair, to_other, h, 0)
+            level = level_of(est)
+            ext_ref[...] = (est - level).astype(BF)
+            level_ref[...] = jnp.broadcast_to(level, level_ref.shape)
 
     return kernel
 
 
 def first_kernel(h, views, slab, rows, edge):
-    def kernel(data_ref, pair_ref, other_ref, *refs):
+    def kernel(data_ref, own_ext, level_ref, pair_ref, other_ref, *refs):
         mats, (own_ref, to_pair, to_other, held) = refs[:7], refs[7:]
         even = is_even()
         lo, hi = pick(even, pair_ref, other_ref, h)
         has_lo, has_hi = has_sides()
-        estimate = mean_views(h, data_ref, views)
-        level = level_of(estimate)
-        ext = jnp.concatenate([lo - level * has_lo, estimate - level, hi - level * has_hi], axis=0)
-        part = blur_back(0, h, views, slab, rows, level, data_ref, ext.astype(BF), mats, held)
-        own_ref[0] = part[edge : edge + rows]
+        level = level_ref[0:1, 0:1]
+        lo = (lo - level * has_lo).astype(BF)
+        hi = (hi - level * has_hi).astype(BF)
+        ext = jnp.concatenate([lo, own_ext[...], hi], axis=0)
+        part = blur_back(0, h, views, slab, rows, level, data_ref, ext, mats, held)
+        own_ref[...] = part[edge : edge + rows]
         put(even, part[0 : 2 * edge].astype(BF), part[rows:].astype(BF), to_pair, to_other)
 
     return kernel
@@ -276,7 +283,7 @@
     scale = 1.0 / views
 
     def kernel(
-        data_ref, pair0_ref, other0_ref, own_ref, sent_pair, sent_other, pair_ref, other_ref, w_ref, one_ref, *refs
+        data_ref, start_ref, level_ref, pair0_ref, other0_ref, own_ref, sent_pair, sent_other, pair_ref, other_ref, w_ref, one_ref, *refs
     ):
         mats, (est_ref, part_ref, to_pair, to_other, held) = refs[:7], refs[7:]
         even = is_even()
@@ -287,10 +294,9 @@
         lo = lo * (one_ref[0:edge] + scale * (sent_lo[0:edge] + got_lo[0:edge]))
         hi = hi * (one_ref[edge + rows :] + scale * (sent_hi[edge:] + got_hi[edge:]))
         got = jnp.concatenate([got_lo[edge:], got_hi[0:edge]], axis=0)
-        before = mean_views(h, data_ref, views)
-        level = level_of(before)
-        estimate = before * (one_ref[pl.ds(edge, rows)] + scale * (own_ref[0] + got))
-        est_ref[0] = estimate
+        level = level_ref[0:1, 0:1]
+        estimate = start_ref[...] * (one_ref[pl.ds(edge, rows)] + scale * (own_ref[...] + got))
+        est_ref[...] = estimate
         shape = across(w_ref[...], lateral) * level
         shapes = jnp.concatenate([shape] * (edge // shape.shape[0]), axis=0)
         ext = jnp.concatenate(
@@ -302,7 +308,7 @@
             axis=0,
         )
         part = blur_back(1, h, views, slab, rows, level, data_ref, ext.astype(BF), mats, held)
-        part_ref[0] = part[edge : edge + rows]
+        part_ref[...] = part[edge : edge + rows]
         put(even, part[0:edge].astype(BF), part[edge + rows :].astype(BF), to_pair, to_other)
 
     return kernel
@@ -313,48 +319,40 @@
 
     def kernel(quarter_ref, wave_ref, _, waves_ref, back_ref, high_ref, low_ref):
         steps = [jnp.broadcast_to(quarter_ref[0:1, :], (8, 128)), jnp.broadcast_to(quarter_ref[1:2, :], (8, 128))]
+        row8 = iota((8, 128), 0)
+        odd_row = (iota((16, 128), 0) & 1) == 1
+        odd_lane = (iota((16, 128), 1) & 1) == 1
         for j in range(half // 128):
             lane = iota((8, 128), 1) + j * 128
-            phase = (iota((8, 128), 0) * lane) & (lateral - 1)
-            for i in range(lateral // 16):
+            phase = (row8 * lane) & (lateral - 1)
+            for i in range(half // 16):
                 pair = []
                 for _ in range(2):
                     near, turn = phase & 127, phase // 128
                     g0 = jnp.take_along_axis(steps[0], near, axis=1)
                     g1 = jnp.take_along_axis(steps[1], near, axis=1)
                     odd = (turn & 1) == 1
-                    cos = jnp.where(odd, g1, g0) * jnp.where(turn >= 2, -1.0, 1.0)
-                    sin = jnp.where(odd, g0, g1) * jnp.where((turn == 0) | (turn == 3), -1.0, 1.0)
-                    if j == 0:
-                        flip = jnp.where((iota((8, 128), 0) & 1) == 1, -1.0, 1.0)
-                        sin = jnp.where(lane == 0, flip, sin)
-                    pair.append((cos, sin))
+                    cos = jnp.where(odd, g1, g0)
+                    sin = jnp.where(odd, g0, g1)
+                    pair.append((jnp.where(turn >= 2, -cos, cos), jnp.where((turn == 0) | (turn == 3), -sin, sin)))
                     phase = (phase + lane * 8) & (lateral - 1)
-                at = pl.ds(i * 16, 16)
-                waves_ref[at, pl.ds(j * 128, 128)] = jnp.concatenate([pair[0][0], pair[1][0]], axis=0).astype(BF)
-                waves_ref[at, pl.ds(half + j * 128, 128)] = jnp.concatenate(
-                    [pair[0][1], pair[1][1]], axis=0
-                ).astype(BF)
-        for j in range(lateral // 128):
-            lane = iota((8, 128), 1) + j * 128
-            phase = (iota((8, 128), 0) * lane) & (lateral - 1)
-            for i in range(half // 16):
-                pair = []
-                for s in range(2):
-                    near, turn = phase & 127, phase // 128
-                    g0 = jnp.take_along_axis(steps[0], near, axis=1)
-                    g1 = jnp.take_along_axis(steps[1], near, axis=1)
-                    odd = (turn & 1) == 1
-                    cos = jnp.where(odd, g1, g0) * jnp.where(turn >= 2, -1.0, 1.0)
-                    sin = jnp.where(odd, g0, g1) * jnp.where((turn == 0) | (turn == 3), 1.0, -1.0)
-                    if i == 0 and s == 0:
-                        flip = jnp.where((lane & 1) == 1, -1.0, 1.0)
-                        sin = jnp.where(iota((8, 128), 0) == 0, flip, sin)
-                    pair.append((cos, sin))
-                    phase = (phase + lane * 8) & (lateral - 1)
-                at = pl.ds(j * 128, 128)
-                back_ref[pl.ds(i * 16, 16), at] = jnp.concatenate([pair[0][0], pair[1][0]], axis=0).astype(BF)
-                back_ref[pl.ds(half + i * 16, 16), at] = jnp.concatenate([pair[0][1], pair[1][1]], axis=0).astype(BF)
+                cos = jnp.concatenate([pair[0][0], pair[1][0]], axis=0)
+                sin = jnp.concatenate([pair[0][1], pair[1][1]], axis=0)
+                ahead, behind = sin, -sin
+                if j == 0:
+                    ahead = jnp.where(iota((16, 128), 1) == 0, jnp.where(odd_row, -1.0, 1.0), sin)
+                if i == 0:
+                    behind = jnp.where(iota((16, 128), 0) == 0, jnp.where(odd_lane, -1.0, 1.0), behind)
+                here, there = pl.ds(i * 16, 16), pl.ds(half + i * 16, 16)
+                left, right = pl.ds(j * 128, 128), pl.ds(half + j * 128, 128)
+                waves_ref[here, left] = cos.astype(BF)
+                waves_ref[here, right] = ahead.astype(BF)
+                waves_ref[there, left] = jnp.where(odd_lane, -cos, cos).astype(BF)
+                waves_ref[there, right] = jnp.where(odd_lane, -ahead, ahead).astype(BF)
+                back_ref[here, left] = cos.astype(BF)
+                back_ref[here, right] = jnp.where(odd_row, -cos, cos).astype(BF)
+                back_ref[there, left] = behind.astype(BF)
+                back_ref[there, right] = jnp.where(odd_row, -behind, behind).astype(BF)
         slot = iota((depth, 128), 1) // depth
         group = 128 // depth
         for kind in range(2):
@@ -379,7 +377,7 @@
 def spectrum(even, scale, rows, half, est_ref, part_ref, pair_ref, other_ref, one_ref, waves_ref, high_ref, low_ref):
     got_lo, got_hi = pick(even, pair_ref, other_ref)
     got = jnp.concatenate([got_lo, got_hi], axis=0)
-    estimate = est_ref[0] * (one_ref[...] + scale * (part_ref[0] + got))
+    estimate = est_ref[...] * (one_ref[...] + scale * (part_ref[...] + got))
     row = dot(estimate.astype(BF), waves_ref[...])
     from_cos = split_dot(high_ref[...], low_ref[...], row[:, :half])
     from_sin = split_dot(high_ref[...], low_ref[...], row[:, half:])
@@ -407,12 +405,16 @@
 
 
 def cycle_kernel(depth, half):
-    def kernel(map_ref, cycle_ref):
+    def kernel(map_ref, _, cycle_ref):
         columns = jnp.transpose(map_ref[0, :, 0:half].astype(F32))
-        cycle = iota((half, CYCLES), 1).astype(F32)
+        cycle = iota((128, CYCLES), 1).astype(F32)
+        zero = jnp.zeros((128, 128), BF)
         for k in range(depth // 2 + 1):
-            here = columns[:, k : k + 1] == cycle
-            cycle_ref[pl.ds(k * half, half), :] = jnp.where(here, 1.0, 0.0).astype(BF)
+            low = columns[:128, k : k + 1] == cycle
+            high = columns[128:, k : k + 1] == cycle[:, 128:]
+            cycle_ref[pl.ds(k * half, 128), :] = jnp.where(low, 1.0, 0.0).astype(BF)
+            cycle_ref[pl.ds(k * half + 128, 128), 0:128] = zero
+            cycle_ref[pl.ds(k * half + 128, 128), 128:256] = jnp.where(high, 1.0, 0.0).astype(BF)
 
     return kernel
 
@@ -540,14 +542,20 @@
     others = [(i, i + 1) for i in range(1, count - 1, 2)]
     others = others + [(b, a) for a, b in others]
 
-    def exchange(to_pair, to_other):
-        other = lax.ppermute(to_other, "tile", others)
-        return lax.ppermute(to_pair, "tile", pairs), other
+    def to_other(array):
+        return lax.ppermute(array, "tile", others)
+
+    def to_pair(array):
+        return lax.ppermute(array, "tile", pairs)
+
+    def exchange(for_pair, for_other):
+        other = to_other(for_other)
+        return to_pair(for_pair), other
 
     vmem = pl.BlockSpec(memory_space=pltpu.VMEM)
     scalars = pl.BlockSpec(memory_space=pltpu.SMEM)
 
-    def call(kernel, inputs, outputs, name, scratch=(), flops=0):
+    def call(kernel, inputs, outputs, scratch=(), flops=0):
         bytes_moved = sum(int(np.prod(s.shape)) * s.dtype.itemsize for s in outputs)
         return pl.pallas_call(
             kernel,
@@ -557,36 +565,34 @@
             scratch_shapes=list(scratch),
             cost_estimate=pl.CostEstimate(flops=flops, bytes_accessed=2 * bytes_moved, transcendentals=0),
             compiler_params=pltpu.CompilerParams(vmem_limit_bytes=VMEM_LIMIT),
-            name=name,
         )(*[x[0] if isinstance(x, tuple) else x for x in inputs])
 
     def shaped(*shape, dtype=F32):
         return jax.ShapeDtypeStruct(shape, dtype)
 
     data = data_halves.reshape(2, views, rows, lateral)
-    data, to_pair, to_other = pl.pallas_call(
+    side = shaped(1, edge, lateral, dtype=BF)
+    plane = shaped(rows, lateral)
+    begun = call(
         edge_kernel(views, rows, edge),
-        in_specs=[pl.BlockSpec(memory_space=pltpu.HBM)],
-        out_specs=(vmem, vmem, vmem),
-        out_shape=(
-            shaped(2, views, rows, lateral, dtype=BF),
-            shaped(2, edge, lateral, dtype=BF),
-            shaped(2, edge, lateral, dtype=BF),
-        ),
-        scratch_shapes=[pltpu.SemaphoreType.DMA((2 * views,))],
-        compiler_params=pltpu.CompilerParams(vmem_limit_bytes=VMEM_LIMIT),
-        name="edges",
-    )(data)
-    pair0, other0 = exchange(to_pair, to_other)
+        [data],
+        [plane, shaped(rows, lateral, dtype=BF), shaped(8, 128), side] * 2
+        + [shaped(2, edge, lateral, dtype=BF)],
+        flops=10**9,
+    )
+    means, own_exts, levels = begun[0:8:4], begun[1:8:4], begun[2:8:4]
+    others0 = [to_other(begun[3]), to_other(begun[7])]
+    pair0 = to_pair(begun[8])
+    starts = [(pair0, other) for other in others0]
 
     kernels = psf_taps / jnp.sum(psf_taps, axis=-1, keepdims=True)
     band = shaped(views, 256, 256, dtype=BF)
     *mats, shape, one0, one1 = call(
         prep_kernel(views, taps, slab, depth, lateral),
-        [(kernels.reshape(-1),)],
+        [kernels.reshape(3 * views, taps)],
         [
-            shaped(views * rows, ext_rows, dtype=BF),
-            shaped(ext_rows, views * rows, dtype=BF),
+            shaped(views * rows // 2, rows // 2 + 2 * edge, dtype=BF),
+            shaped(rows // 2 + 2 * edge, views * rows // 2, dtype=BF),
             band,
             band,
             shaped(2, views * rows, 128),
@@ -596,30 +602,20 @@
             shaped(ext_rows, lateral),
             shaped(rows, lateral),
         ],
-        "prep",
         flops=4 * 10**9,
     )
 
-    (cycles,) = call(
-        cycle_kernel(depth, half),
-        [cycle_map],
-        [shaped((depth // 2 + 1) * half, CYCLES, dtype=BF)],
-        "cycles",
-        flops=10**9,
-    )
-
-    held = [pltpu.VMEM((views * rows, lateral), BF)]
+    held = [pltpu.VMEM((2, views * rows // 2, lateral), BF)]
     firsts = []
     for h in range(2):
-        own, to_pair, to_other = call(
+        own, for_pair, for_other = call(
             first_kernel(h, views, slab, rows, edge),
-            [data, pair0, other0] + mats,
-            [shaped(1, rows, lateral)] + [shaped(1, 2 * edge, lateral, dtype=BF)] * 2,
-            f"first{h}",
+            [data, own_exts[h], levels[h], *starts[h]] + mats,
+            [shaped(rows, lateral)] + [shaped(1, 2 * edge, lateral, dtype=BF)] * 2,
             held,
             flops=4 * 10**9,
         )
-        firsts.append((own, to_pair, to_other) + exchange(to_pair, to_other))
+        firsts.append((own, for_pair, for_other) + exchange(for_pair, for_other))
 
     angle = 2.0 * np.pi / lateral * np.arange(256)
     quarter = jnp.asarray(np.cos(angle).astype(np.float32).reshape(2, 128))
@@ -627,43 +623,42 @@
     wave = np.stack([np.cos(grid_z), np.sin(grid_z)]).astype(np.float32)
     wave = jnp.asarray(np.tile(wave, (1, 1, 128 // depth)))
     table = shaped(2 * rows, rows, dtype=BF)
-    waves, back, table_hi, table_lo = call(
-        table_kernel(slab, depth, lateral),
-        [quarter, wave, firsts[1][0]],
-        [shaped(lateral, lateral, dtype=BF), shaped(lateral, lateral, dtype=BF), table, table],
-        "tables",
-        flops=2 * 10**9,
-    )
-
     seconds = []
     for h in range(2):
-        own, to_pair, to_other, pair, other = firsts[h]
-        est, part, to_pair, to_other = call(
+        est, part, for_pair, for_other = call(
             second_kernel(h, views, slab, rows, edge, lateral),
-            [data, pair0, other0]
-            + [own, to_pair, to_other, pair, other, shape, one0]
+            [data, means[h], levels[h], *starts[h]]
+            + [*firsts[h], shape, one0]
             + mats,
-            [shaped(1, rows, lateral)] * 2 + [shaped(1, edge, lateral, dtype=BF)] * 2,
-            f"second{h}",
+            [shaped(rows, lateral)] * 2 + [shaped(1, edge, lateral, dtype=BF)] * 2,
             held,
             flops=4 * 10**9,
         )
-        seconds.append((est, part) + exchange(to_pair, to_other))
+        seconds.append((est, part) + exchange(for_pair, for_other))
+
+    waves, back, table_hi, table_lo = call(
+        table_kernel(slab, depth, lateral),
+        [quarter, wave, seconds[1][0]],
+        [shaped(lateral, lateral, dtype=BF), shaped(lateral, lateral, dtype=BF), table, table],
+        flops=2 * 10**9,
+    )
+
+    (cycles,) = call(
+        cycle_kernel(depth, half),
+        [cycle_map, seconds[1][0]],
+        [shaped((depth // 2 + 1) * half, CYCLES, dtype=BF)],
+        flops=10**9,
+    )
 
     plane, top = shaped(rows, half), shaped(rows, 128)
     tables = [one1, waves, table_hi, table_lo]
     spectra = call(
-        spectrum_kernel(views, slab, depth, lateral),
-        [*seconds[0]] + tables,
-        [plane, plane, top, top],
-        "spectrum0",
-        flops=10**9,
+        spectrum_kernel(views, slab, depth, lateral), [*seconds[0]] + tables, [plane, plane, top, top], flops=10**9
     )
     *mixed, sums = call(
         power_kernel(views, slab, depth, lateral, count),
         [*seconds[1]] + tables + [cycles, *spectra],
         [plane, plane, top, top, shaped(count, 3, CYCLES)],
-        "spectrum1",
         flops=2 * 10**9,
     )
     sums = lax.all_to_all(sums, "tile", 0, 0)
@@ -671,7 +666,6 @@
         inverse_kernel(slab, depth, lateral, count),
         [(cutoff,), sums, cycle_map, *mixed, back, table_hi, table_lo],
         [shaped(rows, lateral)],
-        "inverse",
         flops=10**9,
     )
     return joined.reshape(slab, depth, lateral)
@@ -685,4 +679,5 @@
         P("groups"),
     )
     out_specs = P(("groups", "tile"), None, None)
+
     return jax.shard_map(body, mesh=mesh, in_specs=in_specs, out_specs=out_specs, check_vma=False)

time: 62.2 us -> 58.1 us (0.934)
  Pallas kernels: 21.3 us -> 18.5 us
  starting transfers between devices: 31.5 us -> 29.8 us
    pallas_call x10 -> x11, Pallas kernels: 20.6 us -> 18.5 us  [call(): pl.pallas_call(kernel, in_specs=[scalars if isinstance(x, tuple) else vme...]
    all_to_all x1, starting transfers between devices: 10.4 us -> 8.55 us  [body(): sums = lax.all_to_all(sums, 'tile', 0, 0)]
    pallas_call x1 -> x0, Pallas kernels: 0.7 us -> none  [body(): pl.pallas_call(edge_kernel(views, rows, edge), in_specs=[pl.BlockSpec(mem...]
    unnamed x10 -> x12, local copies, waits for them, and re-layouts: 1.61 us -> 2.07 us
    ppermute x10 -> x11, starting transfers between devices: 21.2 us -> 21.2 us  [the longest x5 17.1 us: to_pair(): return lax.ppermute(array, 'tile', pairs)]
  transfers between devices with their start and end apart: 11 -> 12, of which waited for: 1 -> 1; matrix products, arithmetic and copies ran while one was open for 0% -> 0% of each run, Pallas kernels for 22% -> 23%
where the time goes in v2:
time: 58.1 us; the launch traced here: 57.7 us
  starting transfers between devices  29.8 us (51%)
  Pallas kernels  18.5 us (32%)
  waiting for transfers between devices  6.28 us (11%)
  local copies, waits for them, and re-layouts  2.09 us (4%)
  between operations  0.9 us (2%)
    pallas_call x11, Pallas kernels, call(): pl.pallas_call(kernel, in_specs=[scalars if isinstance(x, tuple) else vme...  18.5 us
    ppermute x5, starting transfers between devices, to_pair(): return lax.ppermute(array, 'tile', pairs)  17.1 us
    all_to_all x1, starting transfers between devices, body(): sums = lax.all_to_all(sums, 'tile', 0, 0)  8.55 us
    all_to_all x1, waiting for transfers between devices, body(): sums = lax.all_to_all(sums, 'tile', 0, 0)  6.25 us
    ppermute x6, starting transfers between devices, to_other(): return lax.ppermute(array, 'tile', others)  4.16 us
    unnamed x12, local copies, waits for them, and re-layouts  2.07 us
  transfers between devices with their start and end apart: 12, of which 1 were waited for; matrix products, arithmetic and copies ran while one was open for 0% of the time, Pallas kernels for 23%

profile of v2, /device:TPU:0, one launch (start us, length us, event | category | flops | bytes accessed | tf_op | source)
XLA Modules:
  0.0 57.7 jit_solution(10814149395145307045)
XLA Ops:
  0.0 1.6 %copy-done = bf16[2,4,8,32,512]{4,3,2,1,0:T(8,128)(2,1)S(1)} copy-done((bf16[2,4,8,32,512]{4,3,2,1,0:T(8,128)(2,1)S(1)}, bf16[2,4,8,32,512]{4,3,2,1,0:T(8,128)(2,1)}, u32[]{:S(2)}) %copy-start) | copy-done | bytes 2097176
  1.6 0.7 %shard_map.64 = (f32[256,512]{1,0:T(8,128)S(1)}, bf16[256,512]{1,0:T(8,128)(2,1)S(1)}, f32[8,128]{1,0:T(8,128)S(1)}, bf16[1,128,512]{2,1,0:T(8,128)(2,1)S(1)}, f...) custom-call(bf16[2,4,256,512]{3,2,1,0:T(8,128)(2,1)S(1)} %bitcast.2), custom_call_target="tpu_custom_call" | custom-call | flops 1000000000 | bytes 4210688 | tf_op jit(solution)/shard_map/pallas_call | solution.py:560
  2.3 0.6 collective-permute-start
  2.9 0.7 %collective-permute-start.6 = (bf16[1,128,512]{2,1,0:T(8,128)(2,1)S(1)}, bf16[1,128,512]{2,1,0:T(8,128)(2,1)S(1)}, u32[]{:S(2)}, u32[]{:S(2)}) collective-permute-start(bf16[1,128,512]{2,1,0:T(8,128)(2,1)S(1)} %get-tuple-element.78), channel_id=1, source_target_pairs={{1,2},{3,4},{5,6},{7,8},{9,10},{11,12},{13,14},{2,1},{4,3},{6,5},{... | collective-permute-start | bytes 393224 | tf_op jit(solution)/shard_map/ppermute | solution.py:546
  3.6 0.7 %collective-permute-start.1 = (bf16[1,128,512]{2,1,0:T(8,128)(2,1)S(1)}, bf16[1,128,512]{2,1,0:T(8,128)(2,1)S(1)}, u32[]{:S(2)}, u32[]{:S(2)}) collective-permute-start(bf16[1,128,512]{2,1,0:T(8,128)(2,1)S(1)} %get-tuple-element.54), channel_id=1, source_target_pairs={{1,2},{3,4},{5,6},{7,8},{9,10},{11,12},{13,14},{2,1},{4,3},{6,5},{... | collective-permute-start | bytes 393224 | tf_op jit(solution)/shard_map/ppermute | solution.py:546
  4.2 0.1 reduce_sum.9
  4.3 0.1 broadcast_divide_fusion
  4.4 1.4 %shard_map.65 = (bf16[512,384]{1,0:T(8,128)(2,1)S(1)}, bf16[384,512]{1,0:T(8,128)(2,1)S(1)}, bf16[4,256,256]{2,1,0:T(8,128)(2,1)S(1)}, bf16[4,256,256]{2,1,0:T(8...) custom-call(f32[12,9]{1,0:T(8,128)S(1)} %reshape.11.kern), custom_call_target="tpu_custom_call" | custom-call | flops 4000000000 | bytes 9469952 | tf_op jit(solution)/shard_map/pallas_call | solution.py:560
  5.8 0.0 collective-permute-done.6.other_ref.other0_ref
  5.9 0.2 copy-done.1
  6.0 2.3 %shard_map.70 = (f32[256,512]{1,0:T(8,128)S(1)}, bf16[1,256,512]{2,1,0:T(8,128)(2,1)S(1)}, bf16[1,256,512]{2,1,0:T(8,128)(2,1)S(1)}) custom-call(bf16[2,4,256,512]{3,2,1,0:T(8,128)(2,1)S(1)} %bitcast.3, bf16[256,512]{1,0:T(8,128)(2,1)S(1)} %get-tuple-element.79.own_ext, f32[8,128]{1,0:T(8,128)S(1)} %get-tuple-element.77.level_ref, ...), custom_call_target="tpu_custom_call" | custom-call | flops 4000000000 | bytes 2097152 | tf_op jit(solution)/shard_map/pallas_call | solution.py:560
  8.4 5.2 %collective-permute-start.7 = (bf16[1,256,512]{2,1,0:T(8,128)(2,1)S(1)}, bf16[1,256,512]{2,1,0:T(8,128)(2,1)S(1)}, u32[]{:S(2)}, u32[]{:S(2)}) collective-permute-start(bf16[1,256,512]{2,1,0:T(8,128)(2,1)S(1)} %get-tuple-element.81.sent_pair), channel_id=1, source_target_pairs={{0,1},{1,0},{2,3},{3,2},{4,5},{5,4},{6,7},{7,6},{8,9},{9,8},{10,11... | collective-permute-start | bytes 786440 | tf_op jit(solution)/shard_map/ppermute | solution.py:549
  13.6 0.7 %collective-permute-start.8 = (bf16[1,256,512]{2,1,0:T(8,128)(2,1)S(1)}, bf16[1,256,512]{2,1,0:T(8,128)(2,1)S(1)}, u32[]{:S(2)}, u32[]{:S(2)}) collective-permute-start(bf16[1,256,512]{2,1,0:T(8,128)(2,1)S(1)} %get-tuple-element.82.sent_other), channel_id=1, source_target_pairs={{1,2},{3,4},{5,6},{7,8},{9,10},{11,12},{13,14},{2,1},{4,3},{6,5},{... | collective-permute-start | bytes 786440 | tf_op jit(solution)/shard_map/ppermute | solution.py:546
  14.2 2.3 %shard_map.66 = (f32[256,512]{1,0:T(8,128)S(1)}, bf16[1,256,512]{2,1,0:T(8,128)(2,1)S(1)}, bf16[1,256,512]{2,1,0:T(8,128)(2,1)S(1)}) custom-call(bf16[2,4,256,512]{3,2,1,0:T(8,128)(2,1)S(1)} %bitcast.4, bf16[256,512]{1,0:T(8,128)(2,1)S(1)} %get-tuple-element.55.own_ext, f32[8,128]{1,0:T(8,128)S(1)} %get-tuple-element.52.level_ref, ...), custom_call_target="tpu_custom_call" | custom-call | flops 4000000000 | bytes 2097152 | tf_op jit(solution)/shard_map/pallas_call | solution.py:560
  16.6 4.4 %collective-permute-start.2 = (bf16[1,256,512]{2,1,0:T(8,128)(2,1)S(1)}, bf16[1,256,512]{2,1,0:T(8,128)(2,1)S(1)}, u32[]{:S(2)}, u32[]{:S(2)}) collective-permute-start(bf16[1,256,512]{2,1,0:T(8,128)(2,1)S(1)} %get-tuple-element.64.sent_pair), channel_id=1, source_target_pairs={{0,1},{1,0},{2,3},{3,2},{4,5},{5,4},{6,7},{7,6},{8,9},{9,8},{10,11... | collective-permute-start | bytes 786440 | tf_op jit(solution)/shard_map/ppermute | solution.py:549
  21.0 0.7 %collective-permute-start.3 = (bf16[1,256,512]{2,1,0:T(8,128)(2,1)S(1)}, bf16[1,256,512]{2,1,0:T(8,128)(2,1)S(1)}, u32[]{:S(2)}, u32[]{:S(2)}) collective-permute-start(bf16[1,256,512]{2,1,0:T(8,128)(2,1)S(1)} %get-tuple-element.65.sent_other), channel_id=1, source_target_pairs={{1,2},{3,4},{5,6},{7,8},{9,10},{11,12},{13,14},{2,1},{4,3},{6,5},{... | collective-permute-start | bytes 786440 | tf_op jit(solution)/shard_map/ppermute | solution.py:546
  21.7 2.5 %shard_map.71 = (f32[256,512]{1,0:T(8,128)S(1)}, f32[256,512]{1,0:T(8,128)S(1)}, bf16[1,128,512]{2,1,0:T(8,128)(2,1)S(1)}, bf16[1,128,512]{2,1,0:T(8,128)(2,1)S(1)}) custom-call(bf16[2,4,256,512]{3,2,1,0:T(8,128)(2,1)S(1)} %bitcast.5, f32[256,512]{1,0:T(8,128)S(1)} %get-tuple-element.76.start_ref, f32[8,128]{1,0:T(8,128)S(1)} %get-tuple-element.77.level_ref, ...), custom_call_target="tpu_custom_call" | custom-call | flops 4000000000 | bytes 2621440 | tf_op jit(solution)/shard_map/pallas_call | solution.py:560
  24.2 0.7 %collective-permute-start.10 = (bf16[1,128,512]{2,1,0:T(8,128)(2,1)S(1)}, bf16[1,128,512]{2,1,0:T(8,128)(2,1)S(1)}, u32[]{:S(2)}, u32[]{:S(2)}) collective-permute-start(bf16[1,128,512]{2,1,0:T(8,128)(2,1)S(1)} %get-tuple-element.86), channel_id=1, source_target_pairs={{1,2},{3,4},{5,6},{7,8},{9,10},{11,12},{13,14},{2,1},{4,3},{6,5},{... | collective-permute-start | bytes 393224 | tf_op jit(solution)/shard_map/ppermute | solution.py:546
  24.9 6.8 %collective-permute-start.9 = (bf16[1,128,512]{2,1,0:T(8,128)(2,1)S(1)}, bf16[1,128,512]{2,1,0:T(8,128)(2,1)S(1)}, u32[]{:S(2)}, u32[]{:S(2)}) collective-permute-start(bf16[1,128,512]{2,1,0:T(8,128)(2,1)S(1)} %get-tuple-element.85), channel_id=1, source_target_pairs={{0,1},{1,0},{2,3},{3,2},{4,5},{5,4},{6,7},{7,6},{8,9},{9,8},{10,11... | collective-permute-start | bytes 393224 | tf_op jit(solution)/shard_map/ppermute | solution.py:549
  31.7 0.0 copy-start.4
  31.7 2.5 %shard_map.67 = (f32[256,512]{1,0:T(8,128)S(1)}, f32[256,512]{1,0:T(8,128)S(1)}, bf16[1,128,512]{2,1,0:T(8,128)(2,1)S(1)}, bf16[1,128,512]{2,1,0:T(8,128)(2,1)S(1)}) custom-call(bf16[2,4,256,512]{3,2,1,0:T(8,128)(2,1)S(1)} %bitcast.6, f32[256,512]{1,0:T(8,128)S(1)} %get-tuple-element.51.start_ref, f32[8,128]{1,0:T(8,128)S(1)} %get-tuple-element.52.level_ref, ...), custom_call_target="tpu_custom_call" | custom-call | flops 4000000000 | bytes 2621440 | tf_op jit(solution)/shard_map/pallas_call | solution.py:560
  34.2 0.1 collective-permute-start.4
  34.3 0.8 %collective-permute-start.5 = (bf16[1,128,512]{2,1,0:T(8,128)(2,1)S(1)}, bf16[1,128,512]{2,1,0:T(8,128)(2,1)S(1)}, u32[]{:S(2)}, u32[]{:S(2)}) collective-permute-start(bf16[1,128,512]{2,1,0:T(8,128)(2,1)S(1)} %get-tuple-element.71), channel_id=1, source_target_pairs={{1,2},{3,4},{5,6},{7,8},{9,10},{11,12},{13,14},{2,1},{4,3},{6,5},{... | collective-permute-start | bytes 393224 | tf_op jit(solution)/shard_map/ppermute | solution.py:546
  35.2 0.0 copy-start.2
  35.2 0.5 shard_map.68
  35.8 0.3 copy-done.2
  36.1 0.8 %shard_map.69.cycle_ref = bf16[4352,256]{1,0:T(8,128)(2,1)S(1)} custom-call(s32[1,32,512]{2,1,0:T(8,128)S(1)} %copy-done.2, f32[256,512]{1,0:T(8,128)S(1)} %get-tuple-element.68._.est_ref), custom_call_target="tpu_custom_call" | custom-call | flops 1000000000 | bytes 4456448 | tf_op jit(solution)/shard_map/pallas_call | solution.py:560
  36.8 0.9 %shard_map.72 = (f32[256,256]{1,0:T(8,128)S(1)}, f32[256,256]{1,0:T(8,128)S(1)}, f32[256,128]{1,0:T(8,128)S(1)}, f32[256,128]{1,0:T(8,128)S(1)}) custom-call(f32[256,512]{1,0:T(8,128)S(1)} %get-tuple-element.83.est_ref, f32[256,512]{1,0:T(8,128)S(1)} %get-tuple-element.84.part_ref, bf16[1,128,512]{2,1,0:T(8,128)(2,1)S(1)} %collective-permute-done.9.pair_ref, ...), custom_call_target="tpu_custom_call" | custom-call | flops 1000000000 | bytes 1572864 | tf_op jit(solution)/shard_map/pallas_call | solution.py:560
  37.7 2.6 %shard_map.73 = (f32[256,256]{1,0:T(8,128)S(1)}, f32[256,256]{1,0:T(8,128)S(1)}, f32[256,128]{1,0:T(8,128)S(1)}, f32[256,128]{1,0:T(8,128)S(1)}, f32[16,3,256]{2,1,0:T(4,128)}) custom-call(f32[256,512]{1,0:T(8,128)S(1)} %get-tuple-element.68._.est_ref, f32[256,512]{1,0:T(8,128)S(1)} %get-tuple-element.69.part_ref, ...), custom_call_target="tpu_custom_call" | custom-call | flops 2000000000 | bytes 1671168 | tf_op jit(solution)/shard_map/pallas_call | solution.py:560
  40.3 8.6 %all-to-all-start = ((f32[16,3,256]{2,1,0:T(4,128)}), f32[16,3,256]{2,1,0:T(4,128)S(1)}, u32[]{:S(2)}, u32[]{:S(2)}) async-start(f32[16,3,256]{2,1,0:T(4,128)} %get-tuple-element.91), calls=%async_computation | async-start | bytes 131072 | tf_op jit(solution)/shard_map/all_to_all | solution.py:664
  49.5 6.2 %all-to-all-done.sum_ref = f32[16,3,256]{2,1,0:T(4,128)S(1)} async-done(((f32[16,3,256]{2,1,0:T(4,128)}), f32[16,3,256]{2,1,0:T(4,128)S(1)}, u32[]{:S(2)}, u32[]{:S(2)}) %all-to-all-start) | async-done | bytes 49184 | tf_op jit(solution)/shard_map/all_to_all | solution.py:664
  55.8 1.9 %shard_map.74 = f32[256,512]{1,0:T(8,128)} custom-call(s32[1]{0:T(128)S(6)} %copy.9.cut_ref, f32[16,3,256]{2,1,0:T(4,128)S(1)} %all-to-all-done.sum_ref, s32[1,32,512]{2,1,0:T(8,128)S(1)} %copy-done.2, f32[256,256]{1,0:T(8,128)S(1)} %get-tuple-element.92.mre_ref, f32[256,256]{1,0:T(8,128)S(1)} %get-tuple-element.93.mim_ref, ...), custom_call_target="tpu_custom_call" | custom-call | flops 1000000000 | bytes 1048576 | tf_op jit(solution)/shard_map/pallas_call | solution.py:560
  (19 shorter events, 0.1 us)
Async XLA Ops:
  0.0 1.6 %copy-start = (bf16[2,4,8,32,512]{4,3,2,1,0:T(8,128)(2,1)S(1)}, bf16[2,4,8,32,512]{4,3,2,1,0:T(8,128)(2,1)}, u32[]{:S(2)}) copy-start(bf16[2,4,8,32,512]{4,3,2,1,0:T(8,128)(2,1)} %param.6) | copy-start | bytes 6291460
  1.6 2.6 %copy-start.5 = (f32[4,3,9]{2,0,1:T(4,128)S(1)}, f32[4,3,9]{2,0,1:T(4,128)}, u32[]{:S(2)}) copy-start(f32[4,3,9]{2,0,1:T(4,128)} %param.7) | copy-start | bytes 1300
  2.3 3.5 %collective-permute-start = (bf16[2,128,512]{2,1,0:T(8,128)(2,1)S(1)}, bf16[2,128,512]{2,1,0:T(8,128)(2,1)S(1)}, u32[]{:S(2)}, u32[]{:S(2)}) collective-permute-start(bf16[2,128,512]{2,1,0:T(8,128)(2,1)S(1)} %get-tuple-element.53), channel_id=1, source_target_pairs={{0,1},{1,0},{2,3},{3,2},{4,5},{5,4},{6,7},{7,6},{8,9},{9,8},{10,11... | collective-permute-start | bytes 786440 | tf_op jit(solution)/shard_map/ppermute | solution.py:549
  2.9 2.9 %collective-permute-start.6 = (bf16[1,128,512]{2,1,0:T(8,128)(2,1)S(1)}, bf16[1,128,512]{2,1,0:T(8,128)(2,1)S(1)}, u32[]{:S(2)}, u32[]{:S(2)}) collective-permute-start(bf16[1,128,512]{2,1,0:T(8,128)(2,1)S(1)} %get-tuple-element.78), channel_id=1, source_target_pairs={{1,2},{3,4},{5,6},{7,8},{9,10},{11,12},{13,14},{2,1},{4,3},{6,5},{... | collective-permute-start | bytes 393224 | tf_op jit(solution)/shard_map/ppermute | solution.py:546
  3.6 10.7 %collective-permute-start.1 = (bf16[1,128,512]{2,1,0:T(8,128)(2,1)S(1)}, bf16[1,128,512]{2,1,0:T(8,128)(2,1)S(1)}, u32[]{:S(2)}, u32[]{:S(2)}) collective-permute-start(bf16[1,128,512]{2,1,0:T(8,128)(2,1)S(1)} %get-tuple-element.54), channel_id=1, source_target_pairs={{1,2},{3,4},{5,6},{7,8},{9,10},{11,12},{13,14},{2,1},{4,3},{6,5},{... | collective-permute-start | bytes 393224 | tf_op jit(solution)/shard_map/ppermute | solution.py:546
  4.4 1.6 %copy-start.1 = (bf16[2,4,8,32,512]{4,3,2,1,0:T(8,128)(2,1)S(1)}, bf16[2,4,8,32,512]{4,3,2,1,0:T(8,128)(2,1)}, u32[]{:S(2)}) copy-start(bf16[2,4,8,32,512]{4,3,2,1,0:T(8,128)(2,1)} %param.6) | copy-start | bytes 6291460
  8.4 13.3 %collective-permute-start.7 = (bf16[1,256,512]{2,1,0:T(8,128)(2,1)S(1)}, bf16[1,256,512]{2,1,0:T(8,128)(2,1)S(1)}, u32[]{:S(2)}, u32[]{:S(2)}) collective-permute-start(bf16[1,256,512]{2,1,0:T(8,128)(2,1)S(1)} %get-tuple-element.81.sent_pair), channel_id=1, source_target_pairs={{0,1},{1,0},{2,3},{3,2},{4,5},{5,4},{6,7},{7,6},{8,9},{9,8},{10,11... | collective-permute-start | bytes 786440 | tf_op jit(solution)/shard_map/ppermute | solution.py:549
  13.6 8.1 %collective-permute-start.8 = (bf16[1,256,512]{2,1,0:T(8,128)(2,1)S(1)}, bf16[1,256,512]{2,1,0:T(8,128)(2,1)S(1)}, u32[]{:S(2)}, u32[]{:S(2)}) collective-permute-start(bf16[1,256,512]{2,1,0:T(8,128)(2,1)S(1)} %get-tuple-element.82.sent_other), channel_id=1, source_target_pairs={{1,2},{3,4},{5,6},{7,8},{9,10},{11,12},{13,14},{2,1},{4,3},{6,5},{... | collective-permute-start | bytes 786440 | tf_op jit(solution)/shard_map/ppermute | solution.py:546
  16.6 15.1 %collective-permute-start.2 = (bf16[1,256,512]{2,1,0:T(8,128)(2,1)S(1)}, bf16[1,256,512]{2,1,0:T(8,128)(2,1)S(1)}, u32[]{:S(2)}, u32[]{:S(2)}) collective-permute-start(bf16[1,256,512]{2,1,0:T(8,128)(2,1)S(1)} %get-tuple-element.64.sent_pair), channel_id=1, source_target_pairs={{0,1},{1,0},{2,3},{3,2},{4,5},{5,4},{6,7},{7,6},{8,9},{9,8},{10,11... | collective-permute-start | bytes 786440 | tf_op jit(solution)/shard_map/ppermute | solution.py:549
  21.0 10.7 %collective-permute-start.3 = (bf16[1,256,512]{2,1,0:T(8,128)(2,1)S(1)}, bf16[1,256,512]{2,1,0:T(8,128)(2,1)S(1)}, u32[]{:S(2)}, u32[]{:S(2)}) collective-permute-start(bf16[1,256,512]{2,1,0:T(8,128)(2,1)S(1)} %get-tuple-element.65.sent_other), channel_id=1, source_target_pairs={{1,2},{3,4},{5,6},{7,8},{9,10},{11,12},{13,14},{2,1},{4,3},{6,5},{... | collective-permute-start | bytes 786440 | tf_op jit(solution)/shard_map/ppermute | solution.py:546
  24.2 12.6 %collective-permute-start.10 = (bf16[1,128,512]{2,1,0:T(8,128)(2,1)S(1)}, bf16[1,128,512]{2,1,0:T(8,128)(2,1)S(1)}, u32[]{:S(2)}, u32[]{:S(2)}) collective-permute-start(bf16[1,128,512]{2,1,0:T(8,128)(2,1)S(1)} %get-tuple-element.86), channel_id=1, source_target_pairs={{1,2},{3,4},{5,6},{7,8},{9,10},{11,12},{13,14},{2,1},{4,3},{6,5},{... | collective-permute-start | bytes 393224 | tf_op jit(solution)/shard_map/ppermute | solution.py:546
  24.9 11.9 %collective-permute-start.9 = (bf16[1,128,512]{2,1,0:T(8,128)(2,1)S(1)}, bf16[1,128,512]{2,1,0:T(8,128)(2,1)S(1)}, u32[]{:S(2)}, u32[]{:S(2)}) collective-permute-start(bf16[1,128,512]{2,1,0:T(8,128)(2,1)S(1)} %get-tuple-element.85), channel_id=1, source_target_pairs={{0,1},{1,0},{2,3},{3,2},{4,5},{5,4},{6,7},{7,6},{8,9},{9,8},{10,11... | collective-permute-start | bytes 393224 | tf_op jit(solution)/shard_map/ppermute | solution.py:549
  31.7 3.5 %copy-start.3 = (f32[2,32,128]{2,1,0:T(8,128)S(1)}, f32[2,32,128]{2,1,0:T(8,128)}, u32[]{:S(2)}) copy-start(f32[2,32,128]{2,1,0:T(8,128)} %constant.7.clone.wave_ref) | copy-start | bytes 98308
  31.7 3.5 %copy-start.4 = (f32[2,128]{1,0:T(2,128)S(1)}, f32[2,128]{1,0:T(2,128)}, u32[]{:S(2)}) copy-start(f32[2,128]{1,0:T(2,128)} %constant.6.clone.quarter_ref) | copy-start | bytes 3076
  34.2 3.5 %collective-permute-start.4 = (bf16[1,128,512]{2,1,0:T(8,128)(2,1)S(1)}, bf16[1,128,512]{2,1,0:T(8,128)(2,1)S(1)}, u32[]{:S(2)}, u32[]{:S(2)}) collective-permute-start(bf16[1,128,512]{2,1,0:T(8,128)(2,1)S(1)} %get-tuple-element.70), channel_id=1, source_target_pairs={{0,1},{1,0},{2,3},{3,2},{4,5},{5,4},{6,7},{7,6},{8,9},{9,8},{10,11... | collective-permute-start | bytes 393224 | tf_op jit(solution)/shard_map/ppermute | solution.py:549
  34.3 3.4 %collective-permute-start.5 = (bf16[1,128,512]{2,1,0:T(8,128)(2,1)S(1)}, bf16[1,128,512]{2,1,0:T(8,128)(2,1)S(1)}, u32[]{:S(2)}, u32[]{:S(2)}) collective-permute-start(bf16[1,128,512]{2,1,0:T(8,128)(2,1)S(1)} %get-tuple-element.71), channel_id=1, source_target_pairs={{1,2},{3,4},{5,6},{7,8},{9,10},{11,12},{13,14},{2,1},{4,3},{6,5},{... | collective-permute-start | bytes 393224 | tf_op jit(solution)/shard_map/ppermute | solution.py:546
  35.2 0.8 %copy-start.2 = (s32[1,32,512]{2,1,0:T(8,128)S(1)}, s32[1,32,512]{2,1,0:T(8,128)}, u32[]{:S(2)}) copy-start(s32[1,32,512]{2,1,0:T(8,128)} %map_ref.3) | copy-start | bytes 196612
  40.3 15.5 %all-to-all-start = ((f32[16,3,256]{2,1,0:T(4,128)}), f32[16,3,256]{2,1,0:T(4,128)S(1)}, u32[]{:S(2)}, u32[]{:S(2)}) async-start(f32[16,3,256]{2,1,0:T(4,128)} %get-tuple-element.91), calls=%async_computation | async-start | bytes 131072 | tf_op jit(solution)/shard_map/all_to_all | solution.py:664

commit v3 on v2

--- a/solution.py
+++ b/solution.py
@@ -49,10 +49,10 @@
         first = lax.axis_index("tile") * slab
         rows_total = lax.axis_size("tile") * slab
 
-        all_taps = kern[...]
+        all_taps = [kern[axis] / jnp.sum(kern[axis], axis=1, keepdims=True) for axis in range(3)]
 
         def tap(v, axis, t):
-            return all_taps[v * 3 + axis : v * 3 + axis + 1, t : t + 1]
+            return all_taps[axis][v : v + 1, t : t + 1]
 
         def spread(x):
             return jnp.concatenate([x] * (depth // 8), axis=0)
@@ -219,15 +219,8 @@
 
 
 def put(even, low, high, to_pair, to_other, h=0, g=0):
-    @pl.when(even)
-    def _():
-        to_pair[h] = high
-        to_other[g] = low
-
-    @pl.when(jnp.logical_not(even))
-    def _():
-        to_pair[h] = low
-        to_other[g] = high
+    to_pair[h] = jnp.where(even, high, low).astype(BF)
+    to_other[g] = jnp.where(even, low, high).astype(BF)
 
 
 def is_even():
@@ -254,7 +247,7 @@
             est_ref, ext_ref, level_ref, to_other = outs[4 * h : 4 * h + 4]
             est = mean_views(h, data_ref, views)
             est_ref[...] = est
-            put(even, est[:edge].astype(BF), est[rows - edge :].astype(BF), to_pair, to_other, h, 0)
+            put(even, est[:edge], est[rows - edge :], to_pair, to_other, h, 0)
             level = level_of(est)
             ext_ref[...] = (est - level).astype(BF)
             level_ref[...] = jnp.broadcast_to(level, level_ref.shape)
@@ -274,7 +267,7 @@
         ext = jnp.concatenate([lo, own_ext[...], hi], axis=0)
         part = blur_back(0, h, views, slab, rows, level, data_ref, ext, mats, held)
         own_ref[...] = part[edge : edge + rows]
-        put(even, part[0 : 2 * edge].astype(BF), part[rows:].astype(BF), to_pair, to_other)
+        put(even, part[0 : 2 * edge], part[rows:], to_pair, to_other)
 
     return kernel
 
@@ -309,12 +302,12 @@
         )
         part = blur_back(1, h, views, slab, rows, level, data_ref, ext.astype(BF), mats, held)
         part_ref[...] = part[edge : edge + rows]
-        put(even, part[0:edge].astype(BF), part[edge + rows :].astype(BF), to_pair, to_other)
-
-    return kernel
-
-
-def table_kernel(slab, depth, lateral):
+        put(even, part[0:edge], part[edge + rows :], to_pair, to_other)
+
+    return kernel
+
+
+def table_kernel(depth, lateral):
     half = lateral // 2
 
     def kernel(quarter_ref, wave_ref, _, waves_ref, back_ref, high_ref, low_ref):
@@ -358,20 +351,25 @@
         for kind in range(2):
             wave = wave_ref[kind]
             high = wave.astype(BF).astype(F32)
-            for i in range(slab):
-                for g in range(slab * depth // 128):
-                    at = (pl.ds((kind * slab + i) * depth, depth), pl.ds(g * 128, 128))
-                    here = slot == i - group * g
-                    high_ref[at] = jnp.where(here, high, 0.0).astype(BF)
-                    low_ref[at] = jnp.where(here, wave - high, 0.0).astype(BF)
-
-    return kernel
-
-
-def split_dot(table_hi, table_lo, x):
-    x_hi = x.astype(BF)
-    x_lo = (x - x_hi.astype(F32)).astype(BF)
-    return dot(table_hi, x_hi) + dot(table_hi, x_lo) + dot(table_lo, x_hi)
+            for i in range(group):
+                at = pl.ds((kind * group + i) * depth, depth)
+                here = slot == i
+                high_ref[at, :] = jnp.where(here, high, 0.0).astype(BF)
+                low_ref[at, :] = jnp.where(here, wave - high, 0.0).astype(BF)
+
+    return kernel
+
+
+def z_waves(table_hi, table_lo, x):
+    cosines, sines = [], []
+    for at in range(0, x.shape[0], 128):
+        part = x[at : at + 128]
+        high = part.astype(BF)
+        low = (part - high.astype(F32)).astype(BF)
+        total = dot(table_hi, high) + dot(table_hi, low) + dot(table_lo, high)
+        cosines.append(total[:128])
+        sines.append(total[128:])
+    return jnp.concatenate(cosines, axis=0), jnp.concatenate(sines, axis=0)
 
 
 def spectrum(even, scale, rows, half, est_ref, part_ref, pair_ref, other_ref, one_ref, waves_ref, high_ref, low_ref):
@@ -379,13 +377,11 @@
     got = jnp.concatenate([got_lo, got_hi], axis=0)
     estimate = est_ref[...] * (one_ref[...] + scale * (part_ref[...] + got))
     row = dot(estimate.astype(BF), waves_ref[...])
-    from_cos = split_dot(high_ref[...], low_ref[...], row[:, :half])
-    from_sin = split_dot(high_ref[...], low_ref[...], row[:, half:])
+    cos_cos, cos_sin = z_waves(high_ref[...], low_ref[...], row[:, :half])
+    sin_cos, sin_sin = z_waves(high_ref[...], low_ref[...], row[:, half:])
     first = iota((rows, half), 1) == 0
-    sin_cos = from_sin[:rows]
-    sin_sin = from_sin[rows:]
-    real = from_cos[:rows] - jnp.where(first, 0.0, sin_sin)
-    imag = -from_cos[rows:] - jnp.where(first, 0.0, sin_cos)
+    real = cos_cos - jnp.where(first, 0.0, sin_sin)
+    imag = -cos_sin - jnp.where(first, 0.0, sin_cos)
     top = iota((rows, 128), 1) == 0
     top_real = jnp.where(top, sin_cos[:, :128], 0.0)
     top_imag = jnp.where(top, -sin_sin[:, :128], 0.0)
@@ -491,9 +487,9 @@
 
 
 def inverse_kernel(slab, depth, lateral, count):
-    rows, half = slab * depth, lateral // 2
-
-    def kernel(cut_ref, sum_ref, map_ref, mre_ref, mim_ref, mtre_ref, mtim_ref, back_ref, high_ref, low_ref, out_ref):
+    half = lateral // 2
+
+    def kernel(cut_ref, sum_ref, map_ref, mre_ref, mim_ref, mtre_ref, mtim_ref, back_ref, high_ref, low_ref, out_ref, held, sems):
         total = sum_ref[0]
         for i in range(1, count):
             total = total + sum_ref[i]
@@ -520,12 +516,19 @@
         im = mim_ref[...] * cells
         re = jnp.concatenate([re[:, :128] - mtim_ref[...] * last, re[:, 128:]], axis=1)
         im = jnp.concatenate([im[:, :128] + mtre_ref[...] * last, im[:, 128:]], axis=1)
-        from_re = split_dot(high_ref[...], low_ref[...], re)
-        from_im = split_dot(high_ref[...], low_ref[...], im)
-        inner_re = (from_re[:rows] - from_im[rows:]).astype(BF)
-        inner_im = (from_re[rows:] + from_im[:rows]).astype(BF)
-        joined = dot(inner_re, back_ref[0:half]) + dot(inner_im, back_ref[half:lateral])
-        out_ref[...] = joined * (1.0 / (depth * lateral))
+        re_cos, re_sin = z_waves(high_ref[...], low_ref[...], re)
+        im_cos, im_sin = z_waves(high_ref[...], low_ref[...], im)
+        inner_re = (re_cos - im_sin).astype(BF)
+        inner_im = (re_sin + im_cos).astype(BF)
+        copies = []
+        for j in range(2):
+            at = pl.ds(j * half, half)
+            joined = dot(inner_re, back_ref[0:half, at]) + dot(inner_im, back_ref[half:lateral, at])
+            held[j] = joined * (1.0 / (depth * lateral))
+            copies.append(pltpu.make_async_copy(held.at[j], out_ref.at[:, at], sems.at[j]))
+            copies[j].start()
+        for copy in copies:
+            copy.wait()
 
     return kernel
 
@@ -585,11 +588,10 @@
     pair0 = to_pair(begun[8])
     starts = [(pair0, other) for other in others0]
 
-    kernels = psf_taps / jnp.sum(psf_taps, axis=-1, keepdims=True)
     band = shaped(views, 256, 256, dtype=BF)
     *mats, shape, one0, one1 = call(
         prep_kernel(views, taps, slab, depth, lateral),
-        [kernels.reshape(3 * views, taps)],
+        [psf_taps.transpose(1, 0, 2)],
         [
             shaped(views * rows // 2, rows // 2 + 2 * edge, dtype=BF),
             shaped(rows // 2 + 2 * edge, views * rows // 2, dtype=BF),
@@ -622,7 +624,14 @@
     grid_z = np.arange(depth)[:, None] * np.arange(depth)[None, :] % depth * (2.0 * np.pi / depth)
     wave = np.stack([np.cos(grid_z), np.sin(grid_z)]).astype(np.float32)
     wave = jnp.asarray(np.tile(wave, (1, 1, 128 // depth)))
-    table = shaped(2 * rows, rows, dtype=BF)
+    table = shaped(256, 128, dtype=BF)
+    (cycles,) = call(
+        cycle_kernel(depth, half),
+        [cycle_map, firsts[1][0]],
+        [shaped((depth // 2 + 1) * half, CYCLES, dtype=BF)],
+        flops=10**9,
+    )
+
     seconds = []
     for h in range(2):
         est, part, for_pair, for_other = call(
@@ -637,17 +646,10 @@
         seconds.append((est, part) + exchange(for_pair, for_other))
 
     waves, back, table_hi, table_lo = call(
-        table_kernel(slab, depth, lateral),
+        table_kernel(depth, lateral),
         [quarter, wave, seconds[1][0]],
         [shaped(lateral, lateral, dtype=BF), shaped(lateral, lateral, dtype=BF), table, table],
         flops=2 * 10**9,
-    )
-
-    (cycles,) = call(
-        cycle_kernel(depth, half),
-        [cycle_map, seconds[1][0]],
-        [shaped((depth // 2 + 1) * half, CYCLES, dtype=BF)],
-        flops=10**9,
     )
 
     plane, top = shaped(rows, half), shaped(rows, 128)
@@ -662,12 +664,16 @@
         flops=2 * 10**9,
     )
     sums = lax.all_to_all(sums, "tile", 0, 0)
-    (joined,) = call(
+    joined = pl.pallas_call(
         inverse_kernel(slab, depth, lateral, count),
-        [(cutoff,), sums, cycle_map, *mixed, back, table_hi, table_lo],
-        [shaped(rows, lateral)],
-        flops=10**9,
-    )
+        in_specs=[scalars] + [vmem] * 9,
+        out_specs=pl.BlockSpec(memory_space=pl.ANY),
+        out_shape=shaped(rows, lateral),
+        scratch_shapes=[pltpu.VMEM((2, rows, half), F32), pltpu.SemaphoreType.DMA((2,))],
+        cost_estimate=pl.CostEstimate(flops=10**9, bytes_accessed=10**6, transcendentals=0),
+        compiler_params=pltpu.CompilerParams(vmem_limit_bytes=VMEM_LIMIT),
+        name="inverse",
+    )(cutoff, sums, cycle_map, *mixed, back, table_hi, table_lo)
     return joined.reshape(slab, depth, lateral)
 
 

time: 58.1 us -> 57.8 us (level)
    pallas_call x11 -> x10, Pallas kernels: 18.5 us -> 16.4 us  [call(): pl.pallas_call(kernel, in_specs=[scalars if isinstance(x, tuple) else vme...]
    pallas_call x0 -> x1, Pallas kernels: none -> 1.74 us  [body(): pl.pallas_call(inverse_kernel(slab, depth, lateral, count), in_specs=[sca...]
    all_to_all x1, starting transfers between devices: 8.55 us -> 9.89 us  [body(): sums = lax.all_to_all(sums, 'tile', 0, 0)]
    ppermute x5, starting transfers between devices: 17.1 us -> 16.3 us  [to_pair(): return lax.ppermute(array, 'tile', pairs)]
where the time goes in v3:
time: 57.8 us; the launch traced here: 57.5 us
  starting transfers between devices  30.3 us (52%)
  Pallas kernels  18.1 us (31%)
  waiting for transfers between devices  6.28 us (11%)
  local copies, waits for them, and re-layouts  1.7 us (3%)
  between operations  1.06 us (2%)
    pallas_call x10, Pallas kernels, call(): pl.pallas_call(kernel, in_specs=[scalars if isinstance(x, tuple) else vme...  16.4 us
    ppermute x5, starting transfers between devices, to_pair(): return lax.ppermute(array, 'tile', pairs)  16.3 us
    all_to_all x1, starting transfers between devices, body(): sums = lax.all_to_all(sums, 'tile', 0, 0)  9.89 us
    all_to_all x1, waiting for transfers between devices, body(): sums = lax.all_to_all(sums, 'tile', 0, 0)  6.25 us
    ppermute x6, starting transfers between devices, to_other(): return lax.ppermute(array, 'tile', others)  4.15 us
    pallas_call x1, Pallas kernels, body(): pl.pallas_call(inverse_kernel(slab, depth, lateral, count), in_specs=[sca...  1.74 us
    unnamed x12, local copies, waits for them, and re-layouts  1.7 us
  transfers between devices with their start and end apart: 12, of which 1 were waited for; matrix products, arithmetic and copies ran while one was open for 0% of the time, Pallas kernels for 23%

profile of v3, /device:TPU:0, one launch (start us, length us, event | category | flops | bytes accessed | tf_op | source)
XLA Modules:
  0.0 57.5 jit_solution(8171313065727259154)
XLA Ops:
  0.0 1.6 %copy-done = bf16[2,4,8,32,512]{4,3,2,1,0:T(8,128)(2,1)S(1)} copy-done((bf16[2,4,8,32,512]{4,3,2,1,0:T(8,128)(2,1)S(1)}, bf16[2,4,8,32,512]{4,3,2,1,0:T(8,128)(2,1)}, u32[]{:S(2)}) %copy-start) | copy-done | bytes 2097176
  1.6 0.8 %shard_map.64 = (f32[256,512]{1,0:T(8,128)S(1)}, bf16[256,512]{1,0:T(8,128)(2,1)S(1)}, f32[8,128]{1,0:T(8,128)S(1)}, bf16[1,128,512]{2,1,0:T(8,128)(2,1)S(1)}, f...) custom-call(bf16[2,4,256,512]{3,2,1,0:T(8,128)(2,1)S(1)} %bitcast.3), custom_call_target="tpu_custom_call" | custom-call | flops 1000000000 | bytes 4210688 | tf_op jit(solution)/shard_map/pallas_call | solution.py:563
  2.4 0.6 collective-permute-start
  2.9 0.7 %collective-permute-start.6 = (bf16[1,128,512]{2,1,0:T(8,128)(2,1)S(1)}, bf16[1,128,512]{2,1,0:T(8,128)(2,1)S(1)}, u32[]{:S(2)}, u32[]{:S(2)}) collective-permute-start(bf16[1,128,512]{2,1,0:T(8,128)(2,1)S(1)} %get-tuple-element.78), channel_id=1, source_target_pairs={{1,2},{3,4},{5,6},{7,8},{9,10},{11,12},{13,14},{2,1},{4,3},{6,5},{... | collective-permute-start | bytes 393224 | tf_op jit(solution)/shard_map/ppermute | solution.py:549
  3.6 0.7 %collective-permute-start.1 = (bf16[1,128,512]{2,1,0:T(8,128)(2,1)S(1)}, bf16[1,128,512]{2,1,0:T(8,128)(2,1)S(1)}, u32[]{:S(2)}, u32[]{:S(2)}) collective-permute-start(bf16[1,128,512]{2,1,0:T(8,128)(2,1)S(1)} %get-tuple-element.54), channel_id=1, source_target_pairs={{1,2},{3,4},{5,6},{7,8},{9,10},{11,12},{13,14},{2,1},{4,3},{6,5},{... | collective-permute-start | bytes 393224 | tf_op jit(solution)/shard_map/ppermute | solution.py:549
  4.3 0.0 copy-start.1
  4.3 1.5 %shard_map.65 = (bf16[512,384]{1,0:T(8,128)(2,1)S(1)}, bf16[384,512]{1,0:T(8,128)(2,1)S(1)}, bf16[4,256,256]{2,1,0:T(8,128)(2,1)S(1)}, bf16[4,256,256]{2,1,0:T(8...) custom-call(f32[3,4,9]{2,1,0:T(4,128)S(1)} %bitcast.8), custom_call_target="tpu_custom_call" | custom-call | flops 4000000000 | bytes 9469952 | tf_op jit(solution)/shard_map/pallas_call | solution.py:563
  5.8 0.0 collective-permute-done.6.other_ref.other0_ref
  5.8 0.1 copy-done.1
  5.9 2.3 %shard_map.70 = (f32[256,512]{1,0:T(8,128)S(1)}, bf16[1,256,512]{2,1,0:T(8,128)(2,1)S(1)}, bf16[1,256,512]{2,1,0:T(8,128)(2,1)S(1)}) custom-call(bf16[2,4,256,512]{3,2,1,0:T(8,128)(2,1)S(1)} %bitcast.4, bf16[256,512]{1,0:T(8,128)(2,1)S(1)} %get-tuple-element.79.own_ext, f32[8,128]{1,0:T(8,128)S(1)} %get-tuple-element.77.level_ref, ...), custom_call_target="tpu_custom_call" | custom-call | flops 4000000000 | bytes 2097152 | tf_op jit(solution)/shard_map/pallas_call | solution.py:563
  8.2 5.2 %collective-permute-start.7 = (bf16[1,256,512]{2,1,0:T(8,128)(2,1)S(1)}, bf16[1,256,512]{2,1,0:T(8,128)(2,1)S(1)}, u32[]{:S(2)}, u32[]{:S(2)}) collective-permute-start(bf16[1,256,512]{2,1,0:T(8,128)(2,1)S(1)} %get-tuple-element.81.sent_pair), channel_id=1, source_target_pairs={{0,1},{1,0},{2,3},{3,2},{4,5},{5,4},{6,7},{7,6},{8,9},{9,8},{10,11... | collective-permute-start | bytes 786440 | tf_op jit(solution)/shard_map/ppermute | solution.py:552
  13.4 0.7 %collective-permute-start.8 = (bf16[1,256,512]{2,1,0:T(8,128)(2,1)S(1)}, bf16[1,256,512]{2,1,0:T(8,128)(2,1)S(1)}, u32[]{:S(2)}, u32[]{:S(2)}) collective-permute-start(bf16[1,256,512]{2,1,0:T(8,128)(2,1)S(1)} %get-tuple-element.82.sent_other), channel_id=1, source_target_pairs={{1,2},{3,4},{5,6},{7,8},{9,10},{11,12},{13,14},{2,1},{4,3},{6,5},{... | collective-permute-start | bytes 786440 | tf_op jit(solution)/shard_map/ppermute | solution.py:549
  14.1 0.0 collective-permute-done.1.other_ref.other0_ref
  14.1 0.0 copy-start.2
  14.1 2.3 %shard_map.66 = (f32[256,512]{1,0:T(8,128)S(1)}, bf16[1,256,512]{2,1,0:T(8,128)(2,1)S(1)}, bf16[1,256,512]{2,1,0:T(8,128)(2,1)S(1)}) custom-call(bf16[2,4,256,512]{3,2,1,0:T(8,128)(2,1)S(1)} %bitcast.5, bf16[256,512]{1,0:T(8,128)(2,1)S(1)} %get-tuple-element.55.own_ext, f32[8,128]{1,0:T(8,128)S(1)} %get-tuple-element.52.level_ref, ...), custom_call_target="tpu_custom_call" | custom-call | flops 4000000000 | bytes 2097152 | tf_op jit(solution)/shard_map/pallas_call | solution.py:563
  16.4 4.4 %collective-permute-start.2 = (bf16[1,256,512]{2,1,0:T(8,128)(2,1)S(1)}, bf16[1,256,512]{2,1,0:T(8,128)(2,1)S(1)}, u32[]{:S(2)}, u32[]{:S(2)}) collective-permute-start(bf16[1,256,512]{2,1,0:T(8,128)(2,1)S(1)} %get-tuple-element.64.sent_pair), channel_id=1, source_target_pairs={{0,1},{1,0},{2,3},{3,2},{4,5},{5,4},{6,7},{7,6},{8,9},{9,8},{10,11... | collective-permute-start | bytes 786440 | tf_op jit(solution)/shard_map/ppermute | solution.py:552
  20.8 0.7 %collective-permute-start.3 = (bf16[1,256,512]{2,1,0:T(8,128)(2,1)S(1)}, bf16[1,256,512]{2,1,0:T(8,128)(2,1)S(1)}, u32[]{:S(2)}, u32[]{:S(2)}) collective-permute-start(bf16[1,256,512]{2,1,0:T(8,128)(2,1)S(1)} %get-tuple-element.65.sent_other), channel_id=1, source_target_pairs={{1,2},{3,4},{5,6},{7,8},{9,10},{11,12},{13,14},{2,1},{4,3},{6,5},{... | collective-permute-start | bytes 786440 | tf_op jit(solution)/shard_map/ppermute | solution.py:549
  21.5 0.8 %shard_map.69.cycle_ref = bf16[4352,256]{1,0:T(8,128)(2,1)S(1)} custom-call(s32[1,32,512]{2,1,0:T(8,128)S(1)} %copy-done.2, f32[256,512]{1,0:T(8,128)S(1)} %get-tuple-element.63.own_ref._), custom_call_target="tpu_custom_call" | custom-call | flops 1000000000 | bytes 4456448 | tf_op jit(solution)/shard_map/pallas_call | solution.py:563
  22.3 2.5 %shard_map.71 = (f32[256,512]{1,0:T(8,128)S(1)}, f32[256,512]{1,0:T(8,128)S(1)}, bf16[1,128,512]{2,1,0:T(8,128)(2,1)S(1)}, bf16[1,128,512]{2,1,0:T(8,128)(2,1)S(1)}) custom-call(bf16[2,4,256,512]{3,2,1,0:T(8,128)(2,1)S(1)} %bitcast.6, f32[256,512]{1,0:T(8,128)S(1)} %get-tuple-element.76.start_ref, f32[8,128]{1,0:T(8,128)S(1)} %get-tuple-element.77.level_ref, ...), custom_call_target="tpu_custom_call" | custom-call | flops 4000000000 | bytes 2621440 | tf_op jit(solution)/shard_map/pallas_call | solution.py:563
  24.8 0.7 %collective-permute-start.10 = (bf16[1,128,512]{2,1,0:T(8,128)(2,1)S(1)}, bf16[1,128,512]{2,1,0:T(8,128)(2,1)S(1)}, u32[]{:S(2)}, u32[]{:S(2)}) collective-permute-start(bf16[1,128,512]{2,1,0:T(8,128)(2,1)S(1)} %get-tuple-element.86), channel_id=1, source_target_pairs={{1,2},{3,4},{5,6},{7,8},{9,10},{11,12},{13,14},{2,1},{4,3},{6,5},{... | collective-permute-start | bytes 393224 | tf_op jit(solution)/shard_map/ppermute | solution.py:549
  25.5 6.0 %collective-permute-start.9 = (bf16[1,128,512]{2,1,0:T(8,128)(2,1)S(1)}, bf16[1,128,512]{2,1,0:T(8,128)(2,1)S(1)}, u32[]{:S(2)}, u32[]{:S(2)}) collective-permute-start(bf16[1,128,512]{2,1,0:T(8,128)(2,1)S(1)} %get-tuple-element.85), channel_id=1, source_target_pairs={{0,1},{1,0},{2,3},{3,2},{4,5},{5,4},{6,7},{7,6},{8,9},{9,8},{10,11... | collective-permute-start | bytes 393224 | tf_op jit(solution)/shard_map/ppermute | solution.py:552
  31.5 0.0 collective-permute-done.3.other_ref
  31.5 0.0 copy-start.5
  31.5 2.5 %shard_map.67 = (f32[256,512]{1,0:T(8,128)S(1)}, f32[256,512]{1,0:T(8,128)S(1)}, bf16[1,128,512]{2,1,0:T(8,128)(2,1)S(1)}, bf16[1,128,512]{2,1,0:T(8,128)(2,1)S(1)}) custom-call(bf16[2,4,256,512]{3,2,1,0:T(8,128)(2,1)S(1)} %bitcast.7, f32[256,512]{1,0:T(8,128)S(1)} %get-tuple-element.51.start_ref, f32[8,128]{1,0:T(8,128)S(1)} %get-tuple-element.52.level_ref, ...), custom_call_target="tpu_custom_call" | custom-call | flops 4000000000 | bytes 2621440 | tf_op jit(solution)/shard_map/pallas_call | solution.py:563
  34.0 0.1 collective-permute-start.4
  34.1 0.8 %collective-permute-start.5 = (bf16[1,128,512]{2,1,0:T(8,128)(2,1)S(1)}, bf16[1,128,512]{2,1,0:T(8,128)(2,1)S(1)}, u32[]{:S(2)}, u32[]{:S(2)}) collective-permute-start(bf16[1,128,512]{2,1,0:T(8,128)(2,1)S(1)} %get-tuple-element.71), channel_id=1, source_target_pairs={{1,2},{3,4},{5,6},{7,8},{9,10},{11,12},{13,14},{2,1},{4,3},{6,5},{... | collective-permute-start | bytes 393224 | tf_op jit(solution)/shard_map/ppermute | solution.py:549
  35.0 0.5 shard_map.68
  35.5 0.9 %shard_map.72 = (f32[256,256]{1,0:T(8,128)S(1)}, f32[256,256]{1,0:T(8,128)S(1)}, f32[256,128]{1,0:T(8,128)S(1)}, f32[256,128]{1,0:T(8,128)S(1)}) custom-call(f32[256,512]{1,0:T(8,128)S(1)} %get-tuple-element.83.est_ref, f32[256,512]{1,0:T(8,128)S(1)} %get-tuple-element.84.part_ref, bf16[1,128,512]{2,1,0:T(8,128)(2,1)S(1)} %collective-permute-done.9.pair_ref, ...), custom_call_target="tpu_custom_call" | custom-call | flops 1000000000 | bytes 1572864 | tf_op jit(solution)/shard_map/pallas_call | solution.py:563
  36.4 2.4 %shard_map.73 = (f32[256,256]{1,0:T(8,128)S(1)}, f32[256,256]{1,0:T(8,128)S(1)}, f32[256,128]{1,0:T(8,128)S(1)}, f32[256,128]{1,0:T(8,128)S(1)}, f32[16,3,256]{2,1,0:T(4,128)}) custom-call(f32[256,512]{1,0:T(8,128)S(1)} %get-tuple-element.68._.est_ref, f32[256,512]{1,0:T(8,128)S(1)} %get-tuple-element.69.part_ref, ...), custom_call_target="tpu_custom_call" | custom-call | flops 2000000000 | bytes 1671168 | tf_op jit(solution)/shard_map/pallas_call | solution.py:563
  38.8 9.9 %all-to-all-start = ((f32[16,3,256]{2,1,0:T(4,128)}), f32[16,3,256]{2,1,0:T(4,128)S(1)}, u32[]{:S(2)}, u32[]{:S(2)}) async-start(f32[16,3,256]{2,1,0:T(4,128)} %get-tuple-element.91), calls=%async_computation | async-start | bytes 131072 | tf_op jit(solution)/shard_map/all_to_all | solution.py:666
  49.3 6.2 %all-to-all-done.sum_ref = f32[16,3,256]{2,1,0:T(4,128)S(1)} async-done(((f32[16,3,256]{2,1,0:T(4,128)}), f32[16,3,256]{2,1,0:T(4,128)S(1)}, u32[]{:S(2)}, u32[]{:S(2)}) %all-to-all-start) | async-done | bytes 49184 | tf_op jit(solution)/shard_map/all_to_all | solution.py:666
  55.6 1.7 %inverse.1 = f32[256,512]{1,0:T(8,128)} custom-call(s32[1]{0:T(128)S(6)} %copy.7.cut_ref, f32[16,3,256]{2,1,0:T(4,128)S(1)} %all-to-all-done.sum_ref, s32[1,32,512]{2,1,0:T(8,128)S(1)} %copy-done.2, f32[256,256]{1,0:T(8,128)S(1)} %get-tuple-element.92.mre_ref, f32[256,256]{1,0:T(8,128)S(1)} %get-tuple-element.93.mim_ref, ...), custom_call_target="tpu_custom_call" | custom-call | flops 1000000000 | bytes 1000000 | tf_op jit(solution)/shard_map/inverse/pallas_call | solution.py:667
  (15 shorter events, 0.0 us)
Async XLA Ops:
  0.0 1.6 %copy-start = (bf16[2,4,8,32,512]{4,3,2,1,0:T(8,128)(2,1)S(1)}, bf16[2,4,8,32,512]{4,3,2,1,0:T(8,128)(2,1)}, u32[]{:S(2)}) copy-start(bf16[2,4,8,32,512]{4,3,2,1,0:T(8,128)(2,1)} %param.6) | copy-start | bytes 6291460
  1.6 2.7 %copy-start.3 = (f32[4,3,9]{2,0,1:T(4,128)S(1)}, f32[4,3,9]{2,0,1:T(4,128)}, u32[]{:S(2)}) copy-start(f32[4,3,9]{2,0,1:T(4,128)} %param.7) | copy-start | bytes 1300
  2.4 3.4 %collective-permute-start = (bf16[2,128,512]{2,1,0:T(8,128)(2,1)S(1)}, bf16[2,128,512]{2,1,0:T(8,128)(2,1)S(1)}, u32[]{:S(2)}, u32[]{:S(2)}) collective-permute-start(bf16[2,128,512]{2,1,0:T(8,128)(2,1)S(1)} %get-tuple-element.53), channel_id=1, source_target_pairs={{0,1},{1,0},{2,3},{3,2},{4,5},{5,4},{6,7},{7,6},{8,9},{9,8},{10,11... | collective-permute-start | bytes 786440 | tf_op jit(solution)/shard_map/ppermute | solution.py:552
  2.9 2.8 %collective-permute-start.6 = (bf16[1,128,512]{2,1,0:T(8,128)(2,1)S(1)}, bf16[1,128,512]{2,1,0:T(8,128)(2,1)S(1)}, u32[]{:S(2)}, u32[]{:S(2)}) collective-permute-start(bf16[1,128,512]{2,1,0:T(8,128)(2,1)S(1)} %get-tuple-element.78), channel_id=1, source_target_pairs={{1,2},{3,4},{5,6},{7,8},{9,10},{11,12},{13,14},{2,1},{4,3},{6,5},{... | collective-permute-start | bytes 393224 | tf_op jit(solution)/shard_map/ppermute | solution.py:549
  3.6 10.5 %collective-permute-start.1 = (bf16[1,128,512]{2,1,0:T(8,128)(2,1)S(1)}, bf16[1,128,512]{2,1,0:T(8,128)(2,1)S(1)}, u32[]{:S(2)}, u32[]{:S(2)}) collective-permute-start(bf16[1,128,512]{2,1,0:T(8,128)(2,1)S(1)} %get-tuple-element.54), channel_id=1, source_target_pairs={{1,2},{3,4},{5,6},{7,8},{9,10},{11,12},{13,14},{2,1},{4,3},{6,5},{... | collective-permute-start | bytes 393224 | tf_op jit(solution)/shard_map/ppermute | solution.py:549
  4.3 1.6 %copy-start.1 = (bf16[2,4,8,32,512]{4,3,2,1,0:T(8,128)(2,1)S(1)}, bf16[2,4,8,32,512]{4,3,2,1,0:T(8,128)(2,1)}, u32[]{:S(2)}) copy-start(bf16[2,4,8,32,512]{4,3,2,1,0:T(8,128)(2,1)} %param.6) | copy-start | bytes 6291460
  8.2 14.1 %collective-permute-start.7 = (bf16[1,256,512]{2,1,0:T(8,128)(2,1)S(1)}, bf16[1,256,512]{2,1,0:T(8,128)(2,1)S(1)}, u32[]{:S(2)}, u32[]{:S(2)}) collective-permute-start(bf16[1,256,512]{2,1,0:T(8,128)(2,1)S(1)} %get-tuple-element.81.sent_pair), channel_id=1, source_target_pairs={{0,1},{1,0},{2,3},{3,2},{4,5},{5,4},{6,7},{7,6},{8,9},{9,8},{10,11... | collective-permute-start | bytes 786440 | tf_op jit(solution)/shard_map/ppermute | solution.py:552
  13.4 8.9 %collective-permute-start.8 = (bf16[1,256,512]{2,1,0:T(8,128)(2,1)S(1)}, bf16[1,256,512]{2,1,0:T(8,128)(2,1)S(1)}, u32[]{:S(2)}, u32[]{:S(2)}) collective-permute-start(bf16[1,256,512]{2,1,0:T(8,128)(2,1)S(1)} %get-tuple-element.82.sent_other), channel_id=1, source_target_pairs={{1,2},{3,4},{5,6},{7,8},{9,10},{11,12},{13,14},{2,1},{4,3},{6,5},{... | collective-permute-start | bytes 786440 | tf_op jit(solution)/shard_map/ppermute | solution.py:549
  14.1 7.4 %copy-start.2 = (s32[1,32,512]{2,1,0:T(8,128)S(1)}, s32[1,32,512]{2,1,0:T(8,128)}, u32[]{:S(2)}) copy-start(s32[1,32,512]{2,1,0:T(8,128)} %map_ref.3) | copy-start | bytes 196612
  16.4 15.1 %collective-permute-start.2 = (bf16[1,256,512]{2,1,0:T(8,128)(2,1)S(1)}, bf16[1,256,512]{2,1,0:T(8,128)(2,1)S(1)}, u32[]{:S(2)}, u32[]{:S(2)}) collective-permute-start(bf16[1,256,512]{2,1,0:T(8,128)(2,1)S(1)} %get-tuple-element.64.sent_pair), channel_id=1, source_target_pairs={{0,1},{1,0},{2,3},{3,2},{4,5},{5,4},{6,7},{7,6},{8,9},{9,8},{10,11... | collective-permute-start | bytes 786440 | tf_op jit(solution)/shard_map/ppermute | solution.py:552
  20.8 10.7 %collective-permute-start.3 = (bf16[1,256,512]{2,1,0:T(8,128)(2,1)S(1)}, bf16[1,256,512]{2,1,0:T(8,128)(2,1)S(1)}, u32[]{:S(2)}, u32[]{:S(2)}) collective-permute-start(bf16[1,256,512]{2,1,0:T(8,128)(2,1)S(1)} %get-tuple-element.65.sent_other), channel_id=1, source_target_pairs={{1,2},{3,4},{5,6},{7,8},{9,10},{11,12},{13,14},{2,1},{4,3},{6,5},{... | collective-permute-start | bytes 786440 | tf_op jit(solution)/shard_map/ppermute | solution.py:549
  24.8 10.7 %collective-permute-start.10 = (bf16[1,128,512]{2,1,0:T(8,128)(2,1)S(1)}, bf16[1,128,512]{2,1,0:T(8,128)(2,1)S(1)}, u32[]{:S(2)}, u32[]{:S(2)}) collective-permute-start(bf16[1,128,512]{2,1,0:T(8,128)(2,1)S(1)} %get-tuple-element.86), channel_id=1, source_target_pairs={{1,2},{3,4},{5,6},{7,8},{9,10},{11,12},{13,14},{2,1},{4,3},{6,5},{... | collective-permute-start | bytes 393224 | tf_op jit(solution)/shard_map/ppermute | solution.py:549
  25.5 10.0 %collective-permute-start.9 = (bf16[1,128,512]{2,1,0:T(8,128)(2,1)S(1)}, bf16[1,128,512]{2,1,0:T(8,128)(2,1)S(1)}, u32[]{:S(2)}, u32[]{:S(2)}) collective-permute-start(bf16[1,128,512]{2,1,0:T(8,128)(2,1)S(1)} %get-tuple-element.85), channel_id=1, source_target_pairs={{0,1},{1,0},{2,3},{3,2},{4,5},{5,4},{6,7},{7,6},{8,9},{9,8},{10,11... | collective-permute-start | bytes 393224 | tf_op jit(solution)/shard_map/ppermute | solution.py:552
  31.5 3.5 %copy-start.4 = (f32[2,32,128]{2,1,0:T(8,128)S(1)}, f32[2,32,128]{2,1,0:T(8,128)}, u32[]{:S(2)}) copy-start(f32[2,32,128]{2,1,0:T(8,128)} %constant.5.clone.wave_ref) | copy-start | bytes 98308
  31.5 3.5 %copy-start.5 = (f32[2,128]{1,0:T(2,128)S(1)}, f32[2,128]{1,0:T(2,128)}, u32[]{:S(2)}) copy-start(f32[2,128]{1,0:T(2,128)} %constant.4.clone.quarter_ref) | copy-start | bytes 3076
  34.0 2.3 %collective-permute-start.4 = (bf16[1,128,512]{2,1,0:T(8,128)(2,1)S(1)}, bf16[1,128,512]{2,1,0:T(8,128)(2,1)S(1)}, u32[]{:S(2)}, u32[]{:S(2)}) collective-permute-start(bf16[1,128,512]{2,1,0:T(8,128)(2,1)S(1)} %get-tuple-element.70), channel_id=1, source_target_pairs={{0,1},{1,0},{2,3},{3,2},{4,5},{5,4},{6,7},{7,6},{8,9},{9,8},{10,11... | collective-permute-start | bytes 393224 | tf_op jit(solution)/shard_map/ppermute | solution.py:552
  34.1 2.3 %collective-permute-start.5 = (bf16[1,128,512]{2,1,0:T(8,128)(2,1)S(1)}, bf16[1,128,512]{2,1,0:T(8,128)(2,1)S(1)}, u32[]{:S(2)}, u32[]{:S(2)}) collective-permute-start(bf16[1,128,512]{2,1,0:T(8,128)(2,1)S(1)} %get-tuple-element.71), channel_id=1, source_target_pairs={{1,2},{3,4},{5,6},{7,8},{9,10},{11,12},{13,14},{2,1},{4,3},{6,5},{... | collective-permute-start | bytes 393224 | tf_op jit(solution)/shard_map/ppermute | solution.py:549
  38.8 16.8 %all-to-all-start = ((f32[16,3,256]{2,1,0:T(4,128)}), f32[16,3,256]{2,1,0:T(4,128)S(1)}, u32[]{:S(2)}, u32[]{:S(2)}) async-start(f32[16,3,256]{2,1,0:T(4,128)} %get-tuple-element.91), calls=%async_computation | async-start | bytes 131072 | tf_op jit(solution)/shard_map/all_to_all | solution.py:666

commit v4 on v3

--- a/solution.py
+++ b/solution.py
@@ -38,14 +38,26 @@
     return jnp.concatenate([pad, x[: count + by]], axis=0)
 
 
-def prep_kernel(views, taps, slab, depth, lateral):
+def prep_kernel(later, views, taps, slab, depth, lateral):
     radius = taps // 2
     group = 128 // depth
     ext = slab + 2 * radius
     rows = slab * depth
     scale = 1.0 / views
 
-    def kernel(kern, a_ref, b_ref, t_ref, tt_ref, base_ref, off_ref, row_ref, w_ref, one0_ref, one1_ref):
+    def kernel(psf_hbm, *refs):
+        kern = psf_hbm
+        if not later:
+            *refs, kern, sem = refs
+            copy = pltpu.make_async_copy(psf_hbm, kern, sem)
+            copy.start()
+            copy.wait()
+            *refs, kept = refs
+            kept[...] = kern[...]
+        if later:
+            held_ref, base_ref, off_ref, w_ref, one0_ref, one1_ref = refs
+        else:
+            a_ref, b_ref, t_ref, tt_ref, base_ref, off_ref, row_ref = refs
         first = lax.axis_index("tile") * slab
         rows_total = lax.axis_size("tile") * slab
 
@@ -76,7 +88,7 @@
         zero = jnp.zeros((depth, 128), BF)
         tail = jnp.zeros((120, 128), F32)
         gains = []
-        for v in range(views):
+        for v in range(0 if later else views):
             band_z = lookup(gap_z, [(t, tap(v, 1, t)) for t in range(taps)])
             band_zt = lookup(gap_zt, [(t, tap(v, 1, t)) for t in range(taps)])
 
@@ -125,14 +137,17 @@
             return total
 
         field0 = [ones(v, 1, row, depth, False) for v in range(views)]
-        back0 = [blur_z(v, 1.0 / field0[v], True) for v in range(views)]
-        shape = back0[0]
-        for v in range(1, views):
-            shape = shape + back0[v]
-        shape = shape * scale
-        w_ref[...] = shape
-        field1 = [blur_z(v, shape, False) for v in range(views)]
-        back1 = [blur_z(v, 1.0 / field1[v], True) for v in range(views)]
+        fields = field0
+        if later:
+            back0 = [blur_z(v, 1.0 / field0[v], True) for v in range(views)]
+            shape = back0[0]
+            for v in range(1, views):
+                shape = shape + back0[v]
+            shape = shape * scale
+            w_ref[...] = shape
+            fields = [blur_z(v, shape, False) for v in range(views)]
+            back1 = [blur_z(v, 1.0 / fields[v], True) for v in range(views)]
+            gains = [held_ref[v, 1, 0:1, 0:1] for v in range(views)]
 
         x_out = iota((slab, 128), 0) + first
         x_ext = iota((ext, 128), 0) + (first - radius)
@@ -140,15 +155,20 @@
         edges = []
         for v in range(views):
             part_x = ones(v, 0, x_out, rows_total, False)
-            for n, field in enumerate((field0, field1)):
-                for i in range(slab):
-                    at = pl.ds((v * slab + i) * depth, depth)
-                    base_ref[n, at, :] = field[v] * part_x[i : i + 1]
-                off_ref[n, v] = gains[v] / field[v]
-            row_ref[v, 0] = ones(v, 2, y_row, lateral, False)
-            row_ref[v, 1] = jnp.broadcast_to(gains[v], (8, lateral))
+            for i in range(slab):
+                base_ref[pl.ds((v * slab + i) * depth, depth), :] = fields[v] * part_x[i : i + 1]
+            off_ref[v] = gains[v] / fields[v]
+            if not later:
+                row_ref[v, 0] = ones(v, 2, y_row, lateral, False)
+                row_ref[v, 1] = jnp.broadcast_to(gains[v], (8, lateral))
+                continue
             edges.append((ones(v, 0, x_ext, rows_total, True) * scale, ones(v, 2, y_row, lateral, True)))
-        for back, one_ref, low, high in ((back0, one0_ref, 0, ext), (back1, one1_ref, radius, radius + slab)):
+        if not later:
+            return
+        for back, one_ref, low, high in (
+            (back0, one0_ref, 0, ext),
+            (back1, one1_ref, radius, radius + slab),
+        ):
             for e in range(low, high):
                 terms = [back[v] * edges[v][0][e : e + 1] for v in range(views)]
                 for j in range(lateral // 128):
@@ -189,7 +209,7 @@
     return jnp.concatenate([x] * (lateral // 128), axis=1)
 
 
-def blur_back(n, h, views, slab, rows, level, data_ref, ext, mats, held):
+def blur_back(views, slab, rows, level, data_ref, ext, mats, held):
     a_ref, b_ref, t_ref, tt_ref, base_ref, off_ref, row_ref = mats
     lateral = ext.shape[1]
     half = rows // 2
@@ -199,10 +219,10 @@
     for v in range(views):
         at = pl.ds(v * half, half)
         part = jnp.concatenate([held[0, at, :], held[1, at, :]], axis=0)
-        base = across(base_ref[n, pl.ds(v * rows, rows), :], lateral) * (row_ref[v, 0, 0:1, :] * level)
+        base = across(base_ref[pl.ds(v * rows, rows), :], lateral) * (row_ref[v, 0, 0:1, :] * level)
         predicted = y_blur(part, t_ref[v]) + base
-        scaled = data_ref[h, v].astype(F32) * row_ref[v, 1, 0:1, :]
-        offset = across(jnp.concatenate([off_ref[n, v]] * slab, axis=0), lateral)
+        scaled = data_ref[v].astype(F32) * row_ref[v, 1, 0:1, :]
+        offset = across(jnp.concatenate([off_ref[v]] * slab, axis=0), lateral)
         quotient = (scaled / predicted - offset).astype(BF)
         back = y_blur(quotient, tt_ref[v]).astype(BF)
         held[0, at, :] = back[:half]
@@ -265,7 +285,7 @@
         lo = (lo - level * has_lo).astype(BF)
         hi = (hi - level * has_hi).astype(BF)
         ext = jnp.concatenate([lo, own_ext[...], hi], axis=0)
-        part = blur_back(0, h, views, slab, rows, level, data_ref, ext, mats, held)
+        part = blur_back(views, slab, rows, level, data_ref.at[h], ext, mats, held)
         own_ref[...] = part[edge : edge + rows]
         put(even, part[0 : 2 * edge], part[rows:], to_pair, to_other)
 
@@ -300,7 +320,7 @@
             ],
             axis=0,
         )
-        part = blur_back(1, h, views, slab, rows, level, data_ref, ext.astype(BF), mats, held)
+        part = blur_back(views, slab, rows, level, data_ref.at[h], ext.astype(BF), mats, held)
         part_ref[...] = part[edge : edge + rows]
         put(even, part[0:edge], part[edge + rows :], to_pair, to_other)
 
@@ -562,7 +582,7 @@
         bytes_moved = sum(int(np.prod(s.shape)) * s.dtype.itemsize for s in outputs)
         return pl.pallas_call(
             kernel,
-            in_specs=[scalars if isinstance(x, tuple) else vmem for x in inputs],
+            in_specs=[x[1] if isinstance(x, tuple) else vmem for x in inputs],
             out_specs=tuple(vmem for _ in outputs),
             out_shape=tuple(outputs),
             scratch_shapes=list(scratch),
@@ -589,30 +609,40 @@
     starts = [(pair0, other) for other in others0]
 
     band = shaped(views, 256, 256, dtype=BF)
-    *mats, shape, one0, one1 = call(
-        prep_kernel(views, taps, slab, depth, lateral),
-        [psf_taps.transpose(1, 0, 2)],
+    base, offset = shaped(views * rows, 128), shaped(views, depth, 128)
+    psf = pltpu.with_memory_space_constraint(psf_taps.transpose(1, 0, 2), pltpu.HBM)
+    psf = (psf, pl.BlockSpec(memory_space=pltpu.HBM))
+    taps_here = [pltpu.VMEM((3, views, taps), F32), pltpu.SemaphoreType.DMA]
+    *mats, kept = call(
+        prep_kernel(False, views, taps, slab, depth, lateral),
+        [psf],
         [
             shaped(views * rows // 2, rows // 2 + 2 * edge, dtype=BF),
             shaped(rows // 2 + 2 * edge, views * rows // 2, dtype=BF),
             band,
             band,
-            shaped(2, views * rows, 128),
-            shaped(2, views, depth, 128),
+            base,
+            offset,
             shaped(views, 2, 8, lateral),
-            shaped(depth, 128),
-            shaped(ext_rows, lateral),
-            shaped(rows, lateral),
+            shaped(3, views, taps),
         ],
+        taps_here,
         flops=4 * 10**9,
     )
+    base1, offset1, shape, one0, one1 = call(
+        prep_kernel(True, views, taps, slab, depth, lateral),
+        [kept, mats[6]],
+        [base, offset, shaped(depth, 128), shaped(ext_rows, lateral), shaped(rows, lateral)],
+        flops=10**9,
+    )
+    mats1 = [*mats[:4], base1, offset1, mats[6]]
 
     held = [pltpu.VMEM((2, views * rows // 2, lateral), BF)]
     firsts = []
     for h in range(2):
         own, for_pair, for_other = call(
             first_kernel(h, views, slab, rows, edge),
-            [data, own_exts[h], levels[h], *starts[h]] + mats,
+            [data, own_exts[h], levels[h], *starts[h], *mats],
             [shaped(rows, lateral)] + [shaped(1, 2 * edge, lateral, dtype=BF)] * 2,
             held,
             flops=4 * 10**9,
@@ -625,20 +655,13 @@
     wave = np.stack([np.cos(grid_z), np.sin(grid_z)]).astype(np.float32)
     wave = jnp.asarray(np.tile(wave, (1, 1, 128 // depth)))
     table = shaped(256, 128, dtype=BF)
-    (cycles,) = call(
-        cycle_kernel(depth, half),
-        [cycle_map, firsts[1][0]],
-        [shaped((depth // 2 + 1) * half, CYCLES, dtype=BF)],
-        flops=10**9,
-    )
-
     seconds = []
     for h in range(2):
         est, part, for_pair, for_other = call(
             second_kernel(h, views, slab, rows, edge, lateral),
             [data, means[h], levels[h], *starts[h]]
             + [*firsts[h], shape, one0]
-            + mats,
+            + mats1,
             [shaped(rows, lateral)] * 2 + [shaped(1, edge, lateral, dtype=BF)] * 2,
             held,
             flops=4 * 10**9,
@@ -650,6 +673,13 @@
         [quarter, wave, seconds[1][0]],
         [shaped(lateral, lateral, dtype=BF), shaped(lateral, lateral, dtype=BF), table, table],
         flops=2 * 10**9,
+    )
+
+    (cycles,) = call(
+        cycle_kernel(depth, half),
+        [cycle_map, seconds[1][0]],
+        [shaped((depth // 2 + 1) * half, CYCLES, dtype=BF)],
+        flops=10**9,
     )
 
     plane, top = shaped(rows, half), shaped(rows, 128)

time: 57.8 us -> 59.1 us (1.022)
  Pallas kernels: 18.1 us -> 19 us
  local copies, waits for them, and re-layouts: 1.7 us -> 2.54 us
    all_to_all x1, starting transfers between devices: 9.89 us -> 8.56 us  [body(): sums = lax.all_to_all(sums, 'tile', 0, 0)]
    pallas_call x10 -> x11, Pallas kernels: 16.4 us -> 17.3 us  [call(): pl.pallas_call(kernel, in_specs=[x[1] if isinstance(x, tuple) else vmem f...]
    unnamed x12 -> x10, local copies, waits for them, and re-layouts: 1.7 us -> 2.54 us
    ppermute x5, starting transfers between devices: 16.3 us -> 17.1 us  [to_pair(): return lax.ppermute(array, 'tile', pairs)]
  transfers between devices with their start and end apart: 12 -> 12, of which waited for: 1 -> 1; matrix products, arithmetic and copies ran while one was open for 0% -> 0% of each run, Pallas kernels for 23% -> 24%
where the time goes in v4:
time: 59.1 us; the launch traced here: 58.7 us
  starting transfers between devices  29.8 us (50%)
  Pallas kernels  19 us (32%)
  waiting for transfers between devices  6.28 us (11%)
  local copies, waits for them, and re-layouts  2.54 us (4%)
  between operations  1.05 us (2%)
    pallas_call x11, Pallas kernels, call(): pl.pallas_call(kernel, in_specs=[x[1] if isinstance(x, tuple) else vmem f...  17.3 us
    ppermute x5, starting transfers between devices, to_pair(): return lax.ppermute(array, 'tile', pairs)  17.1 us
    all_to_all x1, starting transfers between devices, body(): sums = lax.all_to_all(sums, 'tile', 0, 0)  8.56 us
    all_to_all x1, waiting for transfers between devices, body(): sums = lax.all_to_all(sums, 'tile', 0, 0)  6.25 us
    ppermute x6, starting transfers between devices, to_other(): return lax.ppermute(array, 'tile', others)  4.16 us
    unnamed x10, local copies, waits for them, and re-layouts  2.54 us
    pallas_call x1, Pallas kernels, body(): pl.pallas_call(inverse_kernel(slab, depth, lateral, count), in_specs=[sca...  1.73 us
  transfers between devices with their start and end apart: 12, of which 1 were waited for; matrix products, arithmetic and copies ran while one was open for 0% of the time, Pallas kernels for 24%

profile of v4, /device:TPU:0, one launch (start us, length us, event | category | flops | bytes accessed | tf_op | source)
XLA Modules:
  0.0 58.7 jit_solution(12152225539904588763)
XLA Ops:
  0.0 1.6 %copy-done = bf16[2,4,8,32,512]{4,3,2,1,0:T(8,128)(2,1)S(1)} copy-done((bf16[2,4,8,32,512]{4,3,2,1,0:T(8,128)(2,1)S(1)}, bf16[2,4,8,32,512]{4,3,2,1,0:T(8,128)(2,1)}, u32[]{:S(2)}) %copy-start) | copy-done | bytes 2097176
  1.6 0.8 %shard_map.64 = (f32[256,512]{1,0:T(8,128)S(1)}, bf16[256,512]{1,0:T(8,128)(2,1)S(1)}, f32[8,128]{1,0:T(8,128)S(1)}, bf16[1,128,512]{2,1,0:T(8,128)(2,1)S(1)}, f...) custom-call(bf16[2,4,256,512]{3,2,1,0:T(8,128)(2,1)S(1)} %bitcast.3), custom_call_target="tpu_custom_call" | custom-call | flops 1000000000 | bytes 4210688 | tf_op jit(solution)/shard_map/pallas_call | solution.py:583
  2.4 0.6 collective-permute-start
  2.9 0.7 %collective-permute-start.6 = (bf16[1,128,512]{2,1,0:T(8,128)(2,1)S(1)}, bf16[1,128,512]{2,1,0:T(8,128)(2,1)S(1)}, u32[]{:S(2)}, u32[]{:S(2)}) collective-permute-start(bf16[1,128,512]{2,1,0:T(8,128)(2,1)S(1)} %get-tuple-element.84), channel_id=1, source_target_pairs={{1,2},{3,4},{5,6},{7,8},{9,10},{11,12},{13,14},{2,1},{4,3},{6,5},{... | collective-permute-start | bytes 393224 | tf_op jit(solution)/shard_map/ppermute | solution.py:569
  3.6 0.7 %collective-permute-start.1 = (bf16[1,128,512]{2,1,0:T(8,128)(2,1)S(1)}, bf16[1,128,512]{2,1,0:T(8,128)(2,1)S(1)}, u32[]{:S(2)}, u32[]{:S(2)}) collective-permute-start(bf16[1,128,512]{2,1,0:T(8,128)(2,1)S(1)} %get-tuple-element.57), channel_id=1, source_target_pairs={{1,2},{3,4},{5,6},{7,8},{9,10},{11,12},{13,14},{2,1},{4,3},{6,5},{... | collective-permute-start | bytes 393224 | tf_op jit(solution)/shard_map/ppermute | solution.py:569
  4.3 1.5 %shard_map.65 = (bf16[512,384]{1,0:T(8,128)(2,1)S(1)}, bf16[384,512]{1,0:T(8,128)(2,1)S(1)}, bf16[4,256,256]{2,1,0:T(8,128)(2,1)S(1)}, bf16[4,256,256]{2,1,0:T(8...) custom-call(f32[3,4,9]{2,1,0:T(4,128)} %bitcast.8), custom_call_target="tpu_custom_call" | custom-call | flops 4000000000 | bytes 5112672 | tf_op jit(solution)/shard_map/pallas_call | solution.py:583
  5.7 0.0 copy-start.1
  5.7 1.0 %shard_map.67 = (f32[1024,128]{1,0:T(8,128)S(1)}, f32[4,32,128]{2,1,0:T(8,128)S(1)}, f32[32,128]{1,0:T(8,128)S(1)}, f32[512,512]{1,0:T(8,128)S(1)}, f32[256,512]{1,0:T(8,128)S(1)}) custom-call(f32[3,4,9]{2,1,0:T(4,128)S(1)} %get-tuple-element.69.psf_hbm, f32[4,2,8,512]{3,2,1,0:T(8,128)S(1)} %get-tuple-element.65.refs_6_.refs_0_), custom_call_target="tpu_custom_call" | custom-call | flops 1000000000 | bytes 4358144 | tf_op jit(solution)/shard_map/pallas_call | solution.py:583
  6.8 0.6 copy-done.1
  7.3 2.3 %shard_map.71 = (f32[256,512]{1,0:T(8,128)S(1)}, bf16[1,256,512]{2,1,0:T(8,128)(2,1)S(1)}, bf16[1,256,512]{2,1,0:T(8,128)(2,1)S(1)}) custom-call(bf16[2,4,256,512]{3,2,1,0:T(8,128)(2,1)S(1)} %bitcast.4, bf16[256,512]{1,0:T(8,128)(2,1)S(1)} %get-tuple-element.85.own_ext, f32[8,128]{1,0:T(8,128)S(1)} %get-tuple-element.83.level_ref, ...), custom_call_target="tpu_custom_call" | custom-call | flops 4000000000 | bytes 2097152 | tf_op jit(solution)/shard_map/pallas_call | solution.py:583
  9.6 5.2 %collective-permute-start.7 = (bf16[1,256,512]{2,1,0:T(8,128)(2,1)S(1)}, bf16[1,256,512]{2,1,0:T(8,128)(2,1)S(1)}, u32[]{:S(2)}, u32[]{:S(2)}) collective-permute-start(bf16[1,256,512]{2,1,0:T(8,128)(2,1)S(1)} %get-tuple-element.87.sent_pair), channel_id=1, source_target_pairs={{0,1},{1,0},{2,3},{3,2},{4,5},{5,4},{6,7},{7,6},{8,9},{9,8},{10,11... | collective-permute-start | bytes 786440 | tf_op jit(solution)/shard_map/ppermute | solution.py:572
  14.8 0.7 %collective-permute-start.8 = (bf16[1,256,512]{2,1,0:T(8,128)(2,1)S(1)}, bf16[1,256,512]{2,1,0:T(8,128)(2,1)S(1)}, u32[]{:S(2)}, u32[]{:S(2)}) collective-permute-start(bf16[1,256,512]{2,1,0:T(8,128)(2,1)S(1)} %get-tuple-element.88.sent_other), channel_id=1, source_target_pairs={{1,2},{3,4},{5,6},{7,8},{9,10},{11,12},{13,14},{2,1},{4,3},{6,5},{... | collective-permute-start | bytes 786440 | tf_op jit(solution)/shard_map/ppermute | solution.py:569
  15.5 0.0 collective-permute-done.1.other_ref.other0_ref
  15.5 2.3 %shard_map.66 = (f32[256,512]{1,0:T(8,128)S(1)}, bf16[1,256,512]{2,1,0:T(8,128)(2,1)S(1)}, bf16[1,256,512]{2,1,0:T(8,128)(2,1)S(1)}) custom-call(bf16[2,4,256,512]{3,2,1,0:T(8,128)(2,1)S(1)} %bitcast.5, bf16[256,512]{1,0:T(8,128)(2,1)S(1)} %get-tuple-element.58.own_ext, f32[8,128]{1,0:T(8,128)S(1)} %get-tuple-element.55.level_ref, ...), custom_call_target="tpu_custom_call" | custom-call | flops 4000000000 | bytes 2097152 | tf_op jit(solution)/shard_map/pallas_call | solution.py:583
  17.8 4.4 %collective-permute-start.2 = (bf16[1,256,512]{2,1,0:T(8,128)(2,1)S(1)}, bf16[1,256,512]{2,1,0:T(8,128)(2,1)S(1)}, u32[]{:S(2)}, u32[]{:S(2)}) collective-permute-start(bf16[1,256,512]{2,1,0:T(8,128)(2,1)S(1)} %get-tuple-element.67.sent_pair), channel_id=1, source_target_pairs={{0,1},{1,0},{2,3},{3,2},{4,5},{5,4},{6,7},{7,6},{8,9},{9,8},{10,11... | collective-permute-start | bytes 786440 | tf_op jit(solution)/shard_map/ppermute | solution.py:572
  22.2 0.7 %collective-permute-start.3 = (bf16[1,256,512]{2,1,0:T(8,128)(2,1)S(1)}, bf16[1,256,512]{2,1,0:T(8,128)(2,1)S(1)}, u32[]{:S(2)}, u32[]{:S(2)}) collective-permute-start(bf16[1,256,512]{2,1,0:T(8,128)(2,1)S(1)} %get-tuple-element.68.sent_other), channel_id=1, source_target_pairs={{1,2},{3,4},{5,6},{7,8},{9,10},{11,12},{13,14},{2,1},{4,3},{6,5},{... | collective-permute-start | bytes 786440 | tf_op jit(solution)/shard_map/ppermute | solution.py:569
  22.9 2.5 %shard_map.72 = (f32[256,512]{1,0:T(8,128)S(1)}, f32[256,512]{1,0:T(8,128)S(1)}, bf16[1,128,512]{2,1,0:T(8,128)(2,1)S(1)}, bf16[1,128,512]{2,1,0:T(8,128)(2,1)S(1)}) custom-call(bf16[2,4,256,512]{3,2,1,0:T(8,128)(2,1)S(1)} %bitcast.6, f32[256,512]{1,0:T(8,128)S(1)} %get-tuple-element.82.start_ref, f32[8,128]{1,0:T(8,128)S(1)} %get-tuple-element.83.level_ref, ...), custom_call_target="tpu_custom_call" | custom-call | flops 4000000000 | bytes 2621440 | tf_op jit(solution)/shard_map/pallas_call | solution.py:583
  25.4 0.7 %collective-permute-start.10 = (bf16[1,128,512]{2,1,0:T(8,128)(2,1)S(1)}, bf16[1,128,512]{2,1,0:T(8,128)(2,1)S(1)}, u32[]{:S(2)}, u32[]{:S(2)}) collective-permute-start(bf16[1,128,512]{2,1,0:T(8,128)(2,1)S(1)} %get-tuple-element.92), channel_id=1, source_target_pairs={{1,2},{3,4},{5,6},{7,8},{9,10},{11,12},{13,14},{2,1},{4,3},{6,5},{... | collective-permute-start | bytes 393224 | tf_op jit(solution)/shard_map/ppermute | solution.py:569
  26.1 6.8 %collective-permute-start.9 = (bf16[1,128,512]{2,1,0:T(8,128)(2,1)S(1)}, bf16[1,128,512]{2,1,0:T(8,128)(2,1)S(1)}, u32[]{:S(2)}, u32[]{:S(2)}) collective-permute-start(bf16[1,128,512]{2,1,0:T(8,128)(2,1)S(1)} %get-tuple-element.91), channel_id=1, source_target_pairs={{0,1},{1,0},{2,3},{3,2},{4,5},{5,4},{6,7},{7,6},{8,9},{9,8},{10,11... | collective-permute-start | bytes 393224 | tf_op jit(solution)/shard_map/ppermute | solution.py:572
  32.9 0.0 copy-start.4
  32.9 2.5 %shard_map.68 = (f32[256,512]{1,0:T(8,128)S(1)}, f32[256,512]{1,0:T(8,128)S(1)}, bf16[1,128,512]{2,1,0:T(8,128)(2,1)S(1)}, bf16[1,128,512]{2,1,0:T(8,128)(2,1)S(1)}) custom-call(bf16[2,4,256,512]{3,2,1,0:T(8,128)(2,1)S(1)} %bitcast.7, f32[256,512]{1,0:T(8,128)S(1)} %get-tuple-element.54.start_ref, f32[8,128]{1,0:T(8,128)S(1)} %get-tuple-element.55.level_ref, ...), custom_call_target="tpu_custom_call" | custom-call | flops 4000000000 | bytes 2621440 | tf_op jit(solution)/shard_map/pallas_call | solution.py:583
  35.4 0.1 collective-permute-start.4
  35.5 0.8 %collective-permute-start.5 = (bf16[1,128,512]{2,1,0:T(8,128)(2,1)S(1)}, bf16[1,128,512]{2,1,0:T(8,128)(2,1)S(1)}, u32[]{:S(2)}, u32[]{:S(2)}) collective-permute-start(bf16[1,128,512]{2,1,0:T(8,128)(2,1)S(1)} %get-tuple-element.77), channel_id=1, source_target_pairs={{1,2},{3,4},{5,6},{7,8},{9,10},{11,12},{13,14},{2,1},{4,3},{6,5},{... | collective-permute-start | bytes 393224 | tf_op jit(solution)/shard_map/ppermute | solution.py:569
  36.4 0.0 copy-start.2
  36.4 0.5 shard_map.69
  36.9 0.4 copy-done.2
  37.2 0.8 %shard_map.70.cycle_ref = bf16[4352,256]{1,0:T(8,128)(2,1)S(1)} custom-call(s32[1,32,512]{2,1,0:T(8,128)S(1)} %copy-done.2, f32[256,512]{1,0:T(8,128)S(1)} %get-tuple-element.74._.est_ref), custom_call_target="tpu_custom_call" | custom-call | flops 1000000000 | bytes 4456448 | tf_op jit(solution)/shard_map/pallas_call | solution.py:583
  38.0 0.9 %shard_map.73 = (f32[256,256]{1,0:T(8,128)S(1)}, f32[256,256]{1,0:T(8,128)S(1)}, f32[256,128]{1,0:T(8,128)S(1)}, f32[256,128]{1,0:T(8,128)S(1)}) custom-call(f32[256,512]{1,0:T(8,128)S(1)} %get-tuple-element.89.est_ref, f32[256,512]{1,0:T(8,128)S(1)} %get-tuple-element.90.part_ref, bf16[1,128,512]{2,1,0:T(8,128)(2,1)S(1)} %collective-permute-done.9.pair_ref, ...), custom_call_target="tpu_custom_call" | custom-call | flops 1000000000 | bytes 1572864 | tf_op jit(solution)/shard_map/pallas_call | solution.py:583
  38.9 2.4 %shard_map.74 = (f32[256,256]{1,0:T(8,128)S(1)}, f32[256,256]{1,0:T(8,128)S(1)}, f32[256,128]{1,0:T(8,128)S(1)}, f32[256,128]{1,0:T(8,128)S(1)}, f32[16,3,256]{2,1,0:T(4,128)}) custom-call(f32[256,512]{1,0:T(8,128)S(1)} %get-tuple-element.74._.est_ref, f32[256,512]{1,0:T(8,128)S(1)} %get-tuple-element.75.part_ref, ...), custom_call_target="tpu_custom_call" | custom-call | flops 2000000000 | bytes 1671168 | tf_op jit(solution)/shard_map/pallas_call | solution.py:583
  41.3 8.6 %all-to-all-start = ((f32[16,3,256]{2,1,0:T(4,128)}), f32[16,3,256]{2,1,0:T(4,128)S(1)}, u32[]{:S(2)}, u32[]{:S(2)}) async-start(f32[16,3,256]{2,1,0:T(4,128)} %get-tuple-element.97), calls=%async_computation | async-start | bytes 131072 | tf_op jit(solution)/shard_map/all_to_all | solution.py:696
  50.5 6.2 %all-to-all-done.sum_ref = f32[16,3,256]{2,1,0:T(4,128)S(1)} async-done(((f32[16,3,256]{2,1,0:T(4,128)}), f32[16,3,256]{2,1,0:T(4,128)S(1)}, u32[]{:S(2)}, u32[]{:S(2)}) %all-to-all-start) | async-done | bytes 49184 | tf_op jit(solution)/shard_map/all_to_all | solution.py:696
  56.8 1.7 %inverse.1 = f32[256,512]{1,0:T(8,128)} custom-call(s32[1]{0:T(128)S(6)} %copy.7.cut_ref, f32[16,3,256]{2,1,0:T(4,128)S(1)} %all-to-all-done.sum_ref, s32[1,32,512]{2,1,0:T(8,128)S(1)} %copy-done.2, f32[256,256]{1,0:T(8,128)S(1)} %get-tuple-element.98.mre_ref, f32[256,256]{1,0:T(8,128)S(1)} %get-tuple-element.99.mim_ref, ...), custom_call_target="tpu_custom_call" | custom-call | flops 1000000000 | bytes 1000000 | tf_op jit(solution)/shard_map/inverse/pallas_call | solution.py:697
  (14 shorter events, 0.0 us)
Async XLA Ops:
  0.0 1.6 %copy-start = (bf16[2,4,8,32,512]{4,3,2,1,0:T(8,128)(2,1)S(1)}, bf16[2,4,8,32,512]{4,3,2,1,0:T(8,128)(2,1)}, u32[]{:S(2)}) copy-start(bf16[2,4,8,32,512]{4,3,2,1,0:T(8,128)(2,1)} %param.6) | copy-start | bytes 6291460
  2.4 4.4 %collective-permute-start = (bf16[2,128,512]{2,1,0:T(8,128)(2,1)S(1)}, bf16[2,128,512]{2,1,0:T(8,128)(2,1)S(1)}, u32[]{:S(2)}, u32[]{:S(2)}) collective-permute-start(bf16[2,128,512]{2,1,0:T(8,128)(2,1)S(1)} %get-tuple-element.56), channel_id=1, source_target_pairs={{0,1},{1,0},{2,3},{3,2},{4,5},{5,4},{6,7},{7,6},{8,9},{9,8},{10,11... | collective-permute-start | bytes 786440 | tf_op jit(solution)/shard_map/ppermute | solution.py:572
  2.9 3.8 %collective-permute-start.6 = (bf16[1,128,512]{2,1,0:T(8,128)(2,1)S(1)}, bf16[1,128,512]{2,1,0:T(8,128)(2,1)S(1)}, u32[]{:S(2)}, u32[]{:S(2)}) collective-permute-start(bf16[1,128,512]{2,1,0:T(8,128)(2,1)S(1)} %get-tuple-element.84), channel_id=1, source_target_pairs={{1,2},{3,4},{5,6},{7,8},{9,10},{11,12},{13,14},{2,1},{4,3},{6,5},{... | collective-permute-start | bytes 393224 | tf_op jit(solution)/shard_map/ppermute | solution.py:569
  3.6 11.9 %collective-permute-start.1 = (bf16[1,128,512]{2,1,0:T(8,128)(2,1)S(1)}, bf16[1,128,512]{2,1,0:T(8,128)(2,1)S(1)}, u32[]{:S(2)}, u32[]{:S(2)}) collective-permute-start(bf16[1,128,512]{2,1,0:T(8,128)(2,1)S(1)} %get-tuple-element.57), channel_id=1, source_target_pairs={{1,2},{3,4},{5,6},{7,8},{9,10},{11,12},{13,14},{2,1},{4,3},{6,5},{... | collective-permute-start | bytes 393224 | tf_op jit(solution)/shard_map/ppermute | solution.py:569
  5.7 1.6 %copy-start.1 = (bf16[2,4,8,32,512]{4,3,2,1,0:T(8,128)(2,1)S(1)}, bf16[2,4,8,32,512]{4,3,2,1,0:T(8,128)(2,1)}, u32[]{:S(2)}) copy-start(bf16[2,4,8,32,512]{4,3,2,1,0:T(8,128)(2,1)} %param.6) | copy-start | bytes 6291460
  9.6 13.3 %collective-permute-start.7 = (bf16[1,256,512]{2,1,0:T(8,128)(2,1)S(1)}, bf16[1,256,512]{2,1,0:T(8,128)(2,1)S(1)}, u32[]{:S(2)}, u32[]{:S(2)}) collective-permute-start(bf16[1,256,512]{2,1,0:T(8,128)(2,1)S(1)} %get-tuple-element.87.sent_pair), channel_id=1, source_target_pairs={{0,1},{1,0},{2,3},{3,2},{4,5},{5,4},{6,7},{7,6},{8,9},{9,8},{10,11... | collective-permute-start | bytes 786440 | tf_op jit(solution)/shard_map/ppermute | solution.py:572
  14.8 8.1 %collective-permute-start.8 = (bf16[1,256,512]{2,1,0:T(8,128)(2,1)S(1)}, bf16[1,256,512]{2,1,0:T(8,128)(2,1)S(1)}, u32[]{:S(2)}, u32[]{:S(2)}) collective-permute-start(bf16[1,256,512]{2,1,0:T(8,128)(2,1)S(1)} %get-tuple-element.88.sent_other), channel_id=1, source_target_pairs={{1,2},{3,4},{5,6},{7,8},{9,10},{11,12},{13,14},{2,1},{4,3},{6,5},{... | collective-permute-start | bytes 786440 | tf_op jit(solution)/shard_map/ppermute | solution.py:569
  17.8 15.1 %collective-permute-start.2 = (bf16[1,256,512]{2,1,0:T(8,128)(2,1)S(1)}, bf16[1,256,512]{2,1,0:T(8,128)(2,1)S(1)}, u32[]{:S(2)}, u32[]{:S(2)}) collective-permute-start(bf16[1,256,512]{2,1,0:T(8,128)(2,1)S(1)} %get-tuple-element.67.sent_pair), channel_id=1, source_target_pairs={{0,1},{1,0},{2,3},{3,2},{4,5},{5,4},{6,7},{7,6},{8,9},{9,8},{10,11... | collective-permute-start | bytes 786440 | tf_op jit(solution)/shard_map/ppermute | solution.py:572
  22.2 10.7 %collective-permute-start.3 = (bf16[1,256,512]{2,1,0:T(8,128)(2,1)S(1)}, bf16[1,256,512]{2,1,0:T(8,128)(2,1)S(1)}, u32[]{:S(2)}, u32[]{:S(2)}) collective-permute-start(bf16[1,256,512]{2,1,0:T(8,128)(2,1)S(1)} %get-tuple-element.68.sent_other), channel_id=1, source_target_pairs={{1,2},{3,4},{5,6},{7,8},{9,10},{11,12},{13,14},{2,1},{4,3},{6,5},{... | collective-permute-start | bytes 786440 | tf_op jit(solution)/shard_map/ppermute | solution.py:569
  25.4 12.6 %collective-permute-start.10 = (bf16[1,128,512]{2,1,0:T(8,128)(2,1)S(1)}, bf16[1,128,512]{2,1,0:T(8,128)(2,1)S(1)}, u32[]{:S(2)}, u32[]{:S(2)}) collective-permute-start(bf16[1,128,512]{2,1,0:T(8,128)(2,1)S(1)} %get-tuple-element.92), channel_id=1, source_target_pairs={{1,2},{3,4},{5,6},{7,8},{9,10},{11,12},{13,14},{2,1},{4,3},{6,5},{... | collective-permute-start | bytes 393224 | tf_op jit(solution)/shard_map/ppermute | solution.py:569
  26.1 11.9 %collective-permute-start.9 = (bf16[1,128,512]{2,1,0:T(8,128)(2,1)S(1)}, bf16[1,128,512]{2,1,0:T(8,128)(2,1)S(1)}, u32[]{:S(2)}, u32[]{:S(2)}) collective-permute-start(bf16[1,128,512]{2,1,0:T(8,128)(2,1)S(1)} %get-tuple-element.91), channel_id=1, source_target_pairs={{0,1},{1,0},{2,3},{3,2},{4,5},{5,4},{6,7},{7,6},{8,9},{9,8},{10,11... | collective-permute-start | bytes 393224 | tf_op jit(solution)/shard_map/ppermute | solution.py:572
  32.9 3.5 %copy-start.3 = (f32[2,32,128]{2,1,0:T(8,128)S(1)}, f32[2,32,128]{2,1,0:T(8,128)}, u32[]{:S(2)}) copy-start(f32[2,32,128]{2,1,0:T(8,128)} %constant.5.clone.wave_ref) | copy-start | bytes 98308
  32.9 3.5 %copy-start.4 = (f32[2,128]{1,0:T(2,128)S(1)}, f32[2,128]{1,0:T(2,128)}, u32[]{:S(2)}) copy-start(f32[2,128]{1,0:T(2,128)} %constant.4.clone.quarter_ref) | copy-start | bytes 3076
  35.4 3.5 %collective-permute-start.4 = (bf16[1,128,512]{2,1,0:T(8,128)(2,1)S(1)}, bf16[1,128,512]{2,1,0:T(8,128)(2,1)S(1)}, u32[]{:S(2)}, u32[]{:S(2)}) collective-permute-start(bf16[1,128,512]{2,1,0:T(8,128)(2,1)S(1)} %get-tuple-element.76), channel_id=1, source_target_pairs={{0,1},{1,0},{2,3},{3,2},{4,5},{5,4},{6,7},{7,6},{8,9},{9,8},{10,11... | collective-permute-start | bytes 393224 | tf_op jit(solution)/shard_map/ppermute | solution.py:572
  35.5 3.4 %collective-permute-start.5 = (bf16[1,128,512]{2,1,0:T(8,128)(2,1)S(1)}, bf16[1,128,512]{2,1,0:T(8,128)(2,1)S(1)}, u32[]{:S(2)}, u32[]{:S(2)}) collective-permute-start(bf16[1,128,512]{2,1,0:T(8,128)(2,1)S(1)} %get-tuple-element.77), channel_id=1, source_target_pairs={{1,2},{3,4},{5,6},{7,8},{9,10},{11,12},{13,14},{2,1},{4,3},{6,5},{... | collective-permute-start | bytes 393224 | tf_op jit(solution)/shard_map/ppermute | solution.py:569
  36.4 0.8 %copy-start.2 = (s32[1,32,512]{2,1,0:T(8,128)S(1)}, s32[1,32,512]{2,1,0:T(8,128)}, u32[]{:S(2)}) copy-start(s32[1,32,512]{2,1,0:T(8,128)} %map_ref.3) | copy-start | bytes 196612
  41.3 15.5 %all-to-all-start = ((f32[16,3,256]{2,1,0:T(4,128)}), f32[16,3,256]{2,1,0:T(4,128)S(1)}, u32[]{:S(2)}, u32[]{:S(2)}) async-start(f32[16,3,256]{2,1,0:T(4,128)} %get-tuple-element.97), calls=%async_computation | async-start | bytes 131072 | tf_op jit(solution)/shard_map/all_to_all | solution.py:696

commit v5 on v4

--- a/solution.py
+++ b/solution.py
@@ -414,8 +414,14 @@
     def kernel(est_ref, part_ref, pair_ref, other_ref, one_ref, waves_ref, high_ref, low_ref, *outs):
         even = is_even()
         args = (est_ref, part_ref, pair_ref, other_ref, one_ref, waves_ref, high_ref, low_ref)
-        for ref, value in zip(outs, spectrum(even, 1.0 / views, rows, half, *args)):
+        values = spectrum(even, 1.0 / views, rows, half, *args)
+        for ref, value in zip(outs, values):
             ref[...] = value
+        power = values[0] * values[0] + values[1] * values[1]
+        total = power[0:depth]
+        for s in range(1, slab):
+            total = total + power[s * depth : (s + 1) * depth]
+        outs[4][...] = total * jnp.where(iota((depth, half), 1) == 0, 1.0, 2.0)
 
     return kernel
 
@@ -452,6 +458,7 @@
         im_ref,
         tre_ref,
         tim_ref,
+        power_ref,
         mre_ref,
         mim_ref,
         mtre_ref,
@@ -477,10 +484,10 @@
         powers, tops = [], []
         for a, b, c, d in (
             (re0, re1, im0, im1),
-            (re0, re0, im0, im0),
             (re1, re1, im1, im1),
         ):
             powers.append(over_slab(a * b + c * d) * twice)
+        powers.insert(1, power_ref[...])
         for a, b, c, d in (
             (tre0, tre1, tim0, tim1),
             (tre0, tre0, tim0, tim0),
@@ -685,7 +692,10 @@
     plane, top = shaped(rows, half), shaped(rows, 128)
     tables = [one1, waves, table_hi, table_lo]
     spectra = call(
-        spectrum_kernel(views, slab, depth, lateral), [*seconds[0]] + tables, [plane, plane, top, top], flops=10**9
+        spectrum_kernel(views, slab, depth, lateral),
+        [*seconds[0]] + tables,
+        [plane, plane, top, top, shaped(depth, half)],
+        flops=10**9,
     )
     *mixed, sums = call(
         power_kernel(views, slab, depth, lateral, count),

time: 59.1 us -> 59.1 us (level)
  no operation moved by 1% of the time
where the time goes in v5:
time: 59.1 us; the launch traced here: 58.7 us
  starting transfers between devices  29.8 us (50%)
  Pallas kernels  19 us (32%)
  waiting for transfers between devices  6.28 us (11%)
  local copies, waits for them, and re-layouts  2.54 us (4%)
  between operations  1.05 us (2%)
    pallas_call x11, Pallas kernels, call(): pl.pallas_call(kernel, in_specs=[x[1] if isinstance(x, tuple) else vmem f...  17.3 us
    ppermute x5, starting transfers between devices, to_pair(): return lax.ppermute(array, 'tile', pairs)  17.1 us
    all_to_all x1, starting transfers between devices, body(): sums = lax.all_to_all(sums, 'tile', 0, 0)  8.55 us
    all_to_all x1, waiting for transfers between devices, body(): sums = lax.all_to_all(sums, 'tile', 0, 0)  6.25 us
    ppermute x6, starting transfers between devices, to_other(): return lax.ppermute(array, 'tile', others)  4.16 us
    unnamed x10, local copies, waits for them, and re-layouts  2.54 us
    pallas_call x1, Pallas kernels, body(): pl.pallas_call(inverse_kernel(slab, depth, lateral, count), in_specs=[sca...  1.73 us
  transfers between devices with their start and end apart: 12, of which 1 were waited for; matrix products, arithmetic and copies ran while one was open for 0% of the time, Pallas kernels for 24%

profile of v5, /device:TPU:0, one launch (start us, length us, event | category | flops | bytes accessed | tf_op | source)
XLA Modules:
  0.0 58.7 jit_solution(14073604145125158964)
XLA Ops:
  0.0 1.6 %copy-done = bf16[2,4,8,32,512]{4,3,2,1,0:T(8,128)(2,1)S(1)} copy-done((bf16[2,4,8,32,512]{4,3,2,1,0:T(8,128)(2,1)S(1)}, bf16[2,4,8,32,512]{4,3,2,1,0:T(8,128)(2,1)}, u32[]{:S(2)}) %copy-start) | copy-done | bytes 2097176
  1.6 0.8 %shard_map.64 = (f32[256,512]{1,0:T(8,128)S(1)}, bf16[256,512]{1,0:T(8,128)(2,1)S(1)}, f32[8,128]{1,0:T(8,128)S(1)}, bf16[1,128,512]{2,1,0:T(8,128)(2,1)S(1)}, f...) custom-call(bf16[2,4,256,512]{3,2,1,0:T(8,128)(2,1)S(1)} %bitcast.3), custom_call_target="tpu_custom_call" | custom-call | flops 1000000000 | bytes 4210688 | tf_op jit(solution)/shard_map/pallas_call | solution.py:590
  2.4 0.6 collective-permute-start
  2.9 0.7 %collective-permute-start.6 = (bf16[1,128,512]{2,1,0:T(8,128)(2,1)S(1)}, bf16[1,128,512]{2,1,0:T(8,128)(2,1)S(1)}, u32[]{:S(2)}, u32[]{:S(2)}) collective-permute-start(bf16[1,128,512]{2,1,0:T(8,128)(2,1)S(1)} %get-tuple-element.85), channel_id=1, source_target_pairs={{1,2},{3,4},{5,6},{7,8},{9,10},{11,12},{13,14},{2,1},{4,3},{6,5},{... | collective-permute-start | bytes 393224 | tf_op jit(solution)/shard_map/ppermute | solution.py:576
  3.6 0.7 %collective-permute-start.1 = (bf16[1,128,512]{2,1,0:T(8,128)(2,1)S(1)}, bf16[1,128,512]{2,1,0:T(8,128)(2,1)S(1)}, u32[]{:S(2)}, u32[]{:S(2)}) collective-permute-start(bf16[1,128,512]{2,1,0:T(8,128)(2,1)S(1)} %get-tuple-element.58), channel_id=1, source_target_pairs={{1,2},{3,4},{5,6},{7,8},{9,10},{11,12},{13,14},{2,1},{4,3},{6,5},{... | collective-permute-start | bytes 393224 | tf_op jit(solution)/shard_map/ppermute | solution.py:576
  4.3 1.5 %shard_map.65 = (bf16[512,384]{1,0:T(8,128)(2,1)S(1)}, bf16[384,512]{1,0:T(8,128)(2,1)S(1)}, bf16[4,256,256]{2,1,0:T(8,128)(2,1)S(1)}, bf16[4,256,256]{2,1,0:T(8...) custom-call(f32[3,4,9]{2,1,0:T(4,128)} %bitcast.8), custom_call_target="tpu_custom_call" | custom-call | flops 4000000000 | bytes 5112672 | tf_op jit(solution)/shard_map/pallas_call | solution.py:590
  5.7 0.0 copy-start.1
  5.7 1.0 %shard_map.67 = (f32[1024,128]{1,0:T(8,128)S(1)}, f32[4,32,128]{2,1,0:T(8,128)S(1)}, f32[32,128]{1,0:T(8,128)S(1)}, f32[512,512]{1,0:T(8,128)S(1)}, f32[256,512]{1,0:T(8,128)S(1)}) custom-call(f32[3,4,9]{2,1,0:T(4,128)S(1)} %get-tuple-element.70.psf_hbm, f32[4,2,8,512]{3,2,1,0:T(8,128)S(1)} %get-tuple-element.66.refs_6_.refs_0_), custom_call_target="tpu_custom_call" | custom-call | flops 1000000000 | bytes 4358144 | tf_op jit(solution)/shard_map/pallas_call | solution.py:590
  6.8 0.6 copy-done.1
  7.3 2.3 %shard_map.71 = (f32[256,512]{1,0:T(8,128)S(1)}, bf16[1,256,512]{2,1,0:T(8,128)(2,1)S(1)}, bf16[1,256,512]{2,1,0:T(8,128)(2,1)S(1)}) custom-call(bf16[2,4,256,512]{3,2,1,0:T(8,128)(2,1)S(1)} %bitcast.4, bf16[256,512]{1,0:T(8,128)(2,1)S(1)} %get-tuple-element.86.own_ext, f32[8,128]{1,0:T(8,128)S(1)} %get-tuple-element.84.level_ref, ...), custom_call_target="tpu_custom_call" | custom-call | flops 4000000000 | bytes 2097152 | tf_op jit(solution)/shard_map/pallas_call | solution.py:590
  9.6 5.2 %collective-permute-start.7 = (bf16[1,256,512]{2,1,0:T(8,128)(2,1)S(1)}, bf16[1,256,512]{2,1,0:T(8,128)(2,1)S(1)}, u32[]{:S(2)}, u32[]{:S(2)}) collective-permute-start(bf16[1,256,512]{2,1,0:T(8,128)(2,1)S(1)} %get-tuple-element.88.sent_pair), channel_id=1, source_target_pairs={{0,1},{1,0},{2,3},{3,2},{4,5},{5,4},{6,7},{7,6},{8,9},{9,8},{10,11... | collective-permute-start | bytes 786440 | tf_op jit(solution)/shard_map/ppermute | solution.py:579
  14.8 0.7 %collective-permute-start.8 = (bf16[1,256,512]{2,1,0:T(8,128)(2,1)S(1)}, bf16[1,256,512]{2,1,0:T(8,128)(2,1)S(1)}, u32[]{:S(2)}, u32[]{:S(2)}) collective-permute-start(bf16[1,256,512]{2,1,0:T(8,128)(2,1)S(1)} %get-tuple-element.89.sent_other), channel_id=1, source_target_pairs={{1,2},{3,4},{5,6},{7,8},{9,10},{11,12},{13,14},{2,1},{4,3},{6,5},{... | collective-permute-start | bytes 786440 | tf_op jit(solution)/shard_map/ppermute | solution.py:576
  15.5 0.0 collective-permute-done.1.other_ref.other0_ref
  15.5 2.3 %shard_map.66 = (f32[256,512]{1,0:T(8,128)S(1)}, bf16[1,256,512]{2,1,0:T(8,128)(2,1)S(1)}, bf16[1,256,512]{2,1,0:T(8,128)(2,1)S(1)}) custom-call(bf16[2,4,256,512]{3,2,1,0:T(8,128)(2,1)S(1)} %bitcast.5, bf16[256,512]{1,0:T(8,128)(2,1)S(1)} %get-tuple-element.59.own_ext, f32[8,128]{1,0:T(8,128)S(1)} %get-tuple-element.56.level_ref, ...), custom_call_target="tpu_custom_call" | custom-call | flops 4000000000 | bytes 2097152 | tf_op jit(solution)/shard_map/pallas_call | solution.py:590
  17.8 4.4 %collective-permute-start.2 = (bf16[1,256,512]{2,1,0:T(8,128)(2,1)S(1)}, bf16[1,256,512]{2,1,0:T(8,128)(2,1)S(1)}, u32[]{:S(2)}, u32[]{:S(2)}) collective-permute-start(bf16[1,256,512]{2,1,0:T(8,128)(2,1)S(1)} %get-tuple-element.68.sent_pair), channel_id=1, source_target_pairs={{0,1},{1,0},{2,3},{3,2},{4,5},{5,4},{6,7},{7,6},{8,9},{9,8},{10,11... | collective-permute-start | bytes 786440 | tf_op jit(solution)/shard_map/ppermute | solution.py:579
  22.2 0.7 %collective-permute-start.3 = (bf16[1,256,512]{2,1,0:T(8,128)(2,1)S(1)}, bf16[1,256,512]{2,1,0:T(8,128)(2,1)S(1)}, u32[]{:S(2)}, u32[]{:S(2)}) collective-permute-start(bf16[1,256,512]{2,1,0:T(8,128)(2,1)S(1)} %get-tuple-element.69.sent_other), channel_id=1, source_target_pairs={{1,2},{3,4},{5,6},{7,8},{9,10},{11,12},{13,14},{2,1},{4,3},{6,5},{... | collective-permute-start | bytes 786440 | tf_op jit(solution)/shard_map/ppermute | solution.py:576
  22.9 2.5 %shard_map.72 = (f32[256,512]{1,0:T(8,128)S(1)}, f32[256,512]{1,0:T(8,128)S(1)}, bf16[1,128,512]{2,1,0:T(8,128)(2,1)S(1)}, bf16[1,128,512]{2,1,0:T(8,128)(2,1)S(1)}) custom-call(bf16[2,4,256,512]{3,2,1,0:T(8,128)(2,1)S(1)} %bitcast.6, f32[256,512]{1,0:T(8,128)S(1)} %get-tuple-element.83.start_ref, f32[8,128]{1,0:T(8,128)S(1)} %get-tuple-element.84.level_ref, ...), custom_call_target="tpu_custom_call" | custom-call | flops 4000000000 | bytes 2621440 | tf_op jit(solution)/shard_map/pallas_call | solution.py:590
  25.4 0.7 %collective-permute-start.10 = (bf16[1,128,512]{2,1,0:T(8,128)(2,1)S(1)}, bf16[1,128,512]{2,1,0:T(8,128)(2,1)S(1)}, u32[]{:S(2)}, u32[]{:S(2)}) collective-permute-start(bf16[1,128,512]{2,1,0:T(8,128)(2,1)S(1)} %get-tuple-element.93), channel_id=1, source_target_pairs={{1,2},{3,4},{5,6},{7,8},{9,10},{11,12},{13,14},{2,1},{4,3},{6,5},{... | collective-permute-start | bytes 393224 | tf_op jit(solution)/shard_map/ppermute | solution.py:576
  26.1 6.8 %collective-permute-start.9 = (bf16[1,128,512]{2,1,0:T(8,128)(2,1)S(1)}, bf16[1,128,512]{2,1,0:T(8,128)(2,1)S(1)}, u32[]{:S(2)}, u32[]{:S(2)}) collective-permute-start(bf16[1,128,512]{2,1,0:T(8,128)(2,1)S(1)} %get-tuple-element.92), channel_id=1, source_target_pairs={{0,1},{1,0},{2,3},{3,2},{4,5},{5,4},{6,7},{7,6},{8,9},{9,8},{10,11... | collective-permute-start | bytes 393224 | tf_op jit(solution)/shard_map/ppermute | solution.py:579
  32.9 0.0 copy-start.4
  32.9 2.5 %shard_map.68 = (f32[256,512]{1,0:T(8,128)S(1)}, f32[256,512]{1,0:T(8,128)S(1)}, bf16[1,128,512]{2,1,0:T(8,128)(2,1)S(1)}, bf16[1,128,512]{2,1,0:T(8,128)(2,1)S(1)}) custom-call(bf16[2,4,256,512]{3,2,1,0:T(8,128)(2,1)S(1)} %bitcast.7, f32[256,512]{1,0:T(8,128)S(1)} %get-tuple-element.55.start_ref, f32[8,128]{1,0:T(8,128)S(1)} %get-tuple-element.56.level_ref, ...), custom_call_target="tpu_custom_call" | custom-call | flops 4000000000 | bytes 2621440 | tf_op jit(solution)/shard_map/pallas_call | solution.py:590
  35.4 0.1 collective-permute-start.4
  35.5 0.8 %collective-permute-start.5 = (bf16[1,128,512]{2,1,0:T(8,128)(2,1)S(1)}, bf16[1,128,512]{2,1,0:T(8,128)(2,1)S(1)}, u32[]{:S(2)}, u32[]{:S(2)}) collective-permute-start(bf16[1,128,512]{2,1,0:T(8,128)(2,1)S(1)} %get-tuple-element.78), channel_id=1, source_target_pairs={{1,2},{3,4},{5,6},{7,8},{9,10},{11,12},{13,14},{2,1},{4,3},{6,5},{... | collective-permute-start | bytes 393224 | tf_op jit(solution)/shard_map/ppermute | solution.py:576
  36.4 0.0 copy-start.2
  36.4 0.5 shard_map.69
  36.9 0.4 copy-done.2
  37.2 0.8 %shard_map.70.cycle_ref = bf16[4352,256]{1,0:T(8,128)(2,1)S(1)} custom-call(s32[1,32,512]{2,1,0:T(8,128)S(1)} %copy-done.2, f32[256,512]{1,0:T(8,128)S(1)} %get-tuple-element.75._.est_ref), custom_call_target="tpu_custom_call" | custom-call | flops 1000000000 | bytes 4456448 | tf_op jit(solution)/shard_map/pallas_call | solution.py:590
  38.0 0.9 %shard_map.73 = (f32[256,256]{1,0:T(8,128)S(1)}, f32[256,256]{1,0:T(8,128)S(1)}, f32[256,128]{1,0:T(8,128)S(1)}, f32[256,128]{1,0:T(8,128)S(1)}, f32[32,256]{1,0:T(8,128)S(1)}) custom-call(f32[256,512]{1,0:T(8,128)S(1)} %get-tuple-element.90.est_ref, f32[256,512]{1,0:T(8,128)S(1)} %get-tuple-element.91.part_ref, ...), custom_call_target="tpu_custom_call" | custom-call | flops 1000000000 | bytes 1638400 | tf_op jit(solution)/shard_map/pallas_call | solution.py:590
  38.9 2.4 %shard_map.74 = (f32[256,256]{1,0:T(8,128)S(1)}, f32[256,256]{1,0:T(8,128)S(1)}, f32[256,128]{1,0:T(8,128)S(1)}, f32[256,128]{1,0:T(8,128)S(1)}, f32[16,3,256]{2,1,0:T(4,128)}) custom-call(f32[256,512]{1,0:T(8,128)S(1)} %get-tuple-element.75._.est_ref, f32[256,512]{1,0:T(8,128)S(1)} %get-tuple-element.76.part_ref, ...), custom_call_target="tpu_custom_call" | custom-call | flops 2000000000 | bytes 1671168 | tf_op jit(solution)/shard_map/pallas_call | solution.py:590
  41.3 8.6 %all-to-all-start = ((f32[16,3,256]{2,1,0:T(4,128)}), f32[16,3,256]{2,1,0:T(4,128)S(1)}, u32[]{:S(2)}, u32[]{:S(2)}) async-start(f32[16,3,256]{2,1,0:T(4,128)} %get-tuple-element.99), calls=%async_computation | async-start | bytes 131072 | tf_op jit(solution)/shard_map/all_to_all | solution.py:706
  50.5 6.2 %all-to-all-done.sum_ref = f32[16,3,256]{2,1,0:T(4,128)S(1)} async-done(((f32[16,3,256]{2,1,0:T(4,128)}), f32[16,3,256]{2,1,0:T(4,128)S(1)}, u32[]{:S(2)}, u32[]{:S(2)}) %all-to-all-start) | async-done | bytes 49184 | tf_op jit(solution)/shard_map/all_to_all | solution.py:706
  56.8 1.7 %inverse.1 = f32[256,512]{1,0:T(8,128)} custom-call(s32[1]{0:T(128)S(6)} %copy.7.cut_ref, f32[16,3,256]{2,1,0:T(4,128)S(1)} %all-to-all-done.sum_ref, s32[1,32,512]{2,1,0:T(8,128)S(1)} %copy-done.2, f32[256,256]{1,0:T(8,128)S(1)} %get-tuple-element.100.mre_ref, f32[256,256]{1,0:T(8,128)S(1)} %get-tuple-element.101.mim_ref, ...), custom_call_target="tpu_custom_call" | custom-call | flops 1000000000 | bytes 1000000 | tf_op jit(solution)/shard_map/inverse/pallas_call | solution.py:707
  (14 shorter events, 0.0 us)
Async XLA Ops:
  0.0 1.6 %copy-start = (bf16[2,4,8,32,512]{4,3,2,1,0:T(8,128)(2,1)S(1)}, bf16[2,4,8,32,512]{4,3,2,1,0:T(8,128)(2,1)}, u32[]{:S(2)}) copy-start(bf16[2,4,8,32,512]{4,3,2,1,0:T(8,128)(2,1)} %param.6) | copy-start | bytes 6291460
  2.4 4.4 %collective-permute-start = (bf16[2,128,512]{2,1,0:T(8,128)(2,1)S(1)}, bf16[2,128,512]{2,1,0:T(8,128)(2,1)S(1)}, u32[]{:S(2)}, u32[]{:S(2)}) collective-permute-start(bf16[2,128,512]{2,1,0:T(8,128)(2,1)S(1)} %get-tuple-element.57), channel_id=1, source_target_pairs={{0,1},{1,0},{2,3},{3,2},{4,5},{5,4},{6,7},{7,6},{8,9},{9,8},{10,11... | collective-permute-start | bytes 786440 | tf_op jit(solution)/shard_map/ppermute | solution.py:579
  2.9 3.8 %collective-permute-start.6 = (bf16[1,128,512]{2,1,0:T(8,128)(2,1)S(1)}, bf16[1,128,512]{2,1,0:T(8,128)(2,1)S(1)}, u32[]{:S(2)}, u32[]{:S(2)}) collective-permute-start(bf16[1,128,512]{2,1,0:T(8,128)(2,1)S(1)} %get-tuple-element.85), channel_id=1, source_target_pairs={{1,2},{3,4},{5,6},{7,8},{9,10},{11,12},{13,14},{2,1},{4,3},{6,5},{... | collective-permute-start | bytes 393224 | tf_op jit(solution)/shard_map/ppermute | solution.py:576
  3.6 11.9 %collective-permute-start.1 = (bf16[1,128,512]{2,1,0:T(8,128)(2,1)S(1)}, bf16[1,128,512]{2,1,0:T(8,128)(2,1)S(1)}, u32[]{:S(2)}, u32[]{:S(2)}) collective-permute-start(bf16[1,128,512]{2,1,0:T(8,128)(2,1)S(1)} %get-tuple-element.58), channel_id=1, source_target_pairs={{1,2},{3,4},{5,6},{7,8},{9,10},{11,12},{13,14},{2,1},{4,3},{6,5},{... | collective-permute-start | bytes 393224 | tf_op jit(solution)/shard_map/ppermute | solution.py:576
  5.7 1.6 %copy-start.1 = (bf16[2,4,8,32,512]{4,3,2,1,0:T(8,128)(2,1)S(1)}, bf16[2,4,8,32,512]{4,3,2,1,0:T(8,128)(2,1)}, u32[]{:S(2)}) copy-start(bf16[2,4,8,32,512]{4,3,2,1,0:T(8,128)(2,1)} %param.6) | copy-start | bytes 6291460
  9.6 13.3 %collective-permute-start.7 = (bf16[1,256,512]{2,1,0:T(8,128)(2,1)S(1)}, bf16[1,256,512]{2,1,0:T(8,128)(2,1)S(1)}, u32[]{:S(2)}, u32[]{:S(2)}) collective-permute-start(bf16[1,256,512]{2,1,0:T(8,128)(2,1)S(1)} %get-tuple-element.88.sent_pair), channel_id=1, source_target_pairs={{0,1},{1,0},{2,3},{3,2},{4,5},{5,4},{6,7},{7,6},{8,9},{9,8},{10,11... | collective-permute-start | bytes 786440 | tf_op jit(solution)/shard_map/ppermute | solution.py:579
  14.8 8.1 %collective-permute-start.8 = (bf16[1,256,512]{2,1,0:T(8,128)(2,1)S(1)}, bf16[1,256,512]{2,1,0:T(8,128)(2,1)S(1)}, u32[]{:S(2)}, u32[]{:S(2)}) collective-permute-start(bf16[1,256,512]{2,1,0:T(8,128)(2,1)S(1)} %get-tuple-element.89.sent_other), channel_id=1, source_target_pairs={{1,2},{3,4},{5,6},{7,8},{9,10},{11,12},{13,14},{2,1},{4,3},{6,5},{... | collective-permute-start | bytes 786440 | tf_op jit(solution)/shard_map/ppermute | solution.py:576
  17.8 15.1 %collective-permute-start.2 = (bf16[1,256,512]{2,1,0:T(8,128)(2,1)S(1)}, bf16[1,256,512]{2,1,0:T(8,128)(2,1)S(1)}, u32[]{:S(2)}, u32[]{:S(2)}) collective-permute-start(bf16[1,256,512]{2,1,0:T(8,128)(2,1)S(1)} %get-tuple-element.68.sent_pair), channel_id=1, source_target_pairs={{0,1},{1,0},{2,3},{3,2},{4,5},{5,4},{6,7},{7,6},{8,9},{9,8},{10,11... | collective-permute-start | bytes 786440 | tf_op jit(solution)/shard_map/ppermute | solution.py:579
  22.2 10.7 %collective-permute-start.3 = (bf16[1,256,512]{2,1,0:T(8,128)(2,1)S(1)}, bf16[1,256,512]{2,1,0:T(8,128)(2,1)S(1)}, u32[]{:S(2)}, u32[]{:S(2)}) collective-permute-start(bf16[1,256,512]{2,1,0:T(8,128)(2,1)S(1)} %get-tuple-element.69.sent_other), channel_id=1, source_target_pairs={{1,2},{3,4},{5,6},{7,8},{9,10},{11,12},{13,14},{2,1},{4,3},{6,5},{... | collective-permute-start | bytes 786440 | tf_op jit(solution)/shard_map/ppermute | solution.py:576
  25.4 12.6 %collective-permute-start.10 = (bf16[1,128,512]{2,1,0:T(8,128)(2,1)S(1)}, bf16[1,128,512]{2,1,0:T(8,128)(2,1)S(1)}, u32[]{:S(2)}, u32[]{:S(2)}) collective-permute-start(bf16[1,128,512]{2,1,0:T(8,128)(2,1)S(1)} %get-tuple-element.93), channel_id=1, source_target_pairs={{1,2},{3,4},{5,6},{7,8},{9,10},{11,12},{13,14},{2,1},{4,3},{6,5},{... | collective-permute-start | bytes 393224 | tf_op jit(solution)/shard_map/ppermute | solution.py:576
  26.1 11.9 %collective-permute-start.9 = (bf16[1,128,512]{2,1,0:T(8,128)(2,1)S(1)}, bf16[1,128,512]{2,1,0:T(8,128)(2,1)S(1)}, u32[]{:S(2)}, u32[]{:S(2)}) collective-permute-start(bf16[1,128,512]{2,1,0:T(8,128)(2,1)S(1)} %get-tuple-element.92), channel_id=1, source_target_pairs={{0,1},{1,0},{2,3},{3,2},{4,5},{5,4},{6,7},{7,6},{8,9},{9,8},{10,11... | collective-permute-start | bytes 393224 | tf_op jit(solution)/shard_map/ppermute | solution.py:579
  32.9 3.5 %copy-start.3 = (f32[2,32,128]{2,1,0:T(8,128)S(1)}, f32[2,32,128]{2,1,0:T(8,128)}, u32[]{:S(2)}) copy-start(f32[2,32,128]{2,1,0:T(8,128)} %constant.5.clone.wave_ref) | copy-start | bytes 98308
  32.9 3.5 %copy-start.4 = (f32[2,128]{1,0:T(2,128)S(1)}, f32[2,128]{1,0:T(2,128)}, u32[]{:S(2)}) copy-start(f32[2,128]{1,0:T(2,128)} %constant.4.clone.quarter_ref) | copy-start | bytes 3076
  35.4 3.5 %collective-permute-start.4 = (bf16[1,128,512]{2,1,0:T(8,128)(2,1)S(1)}, bf16[1,128,512]{2,1,0:T(8,128)(2,1)S(1)}, u32[]{:S(2)}, u32[]{:S(2)}) collective-permute-start(bf16[1,128,512]{2,1,0:T(8,128)(2,1)S(1)} %get-tuple-element.77), channel_id=1, source_target_pairs={{0,1},{1,0},{2,3},{3,2},{4,5},{5,4},{6,7},{7,6},{8,9},{9,8},{10,11... | collective-permute-start | bytes 393224 | tf_op jit(solution)/shard_map/ppermute | solution.py:579
  35.5 3.4 %collective-permute-start.5 = (bf16[1,128,512]{2,1,0:T(8,128)(2,1)S(1)}, bf16[1,128,512]{2,1,0:T(8,128)(2,1)S(1)}, u32[]{:S(2)}, u32[]{:S(2)}) collective-permute-start(bf16[1,128,512]{2,1,0:T(8,128)(2,1)S(1)} %get-tuple-element.78), channel_id=1, source_target_pairs={{1,2},{3,4},{5,6},{7,8},{9,10},{11,12},{13,14},{2,1},{4,3},{6,5},{... | collective-permute-start | bytes 393224 | tf_op jit(solution)/shard_map/ppermute | solution.py:576
  36.4 0.8 %copy-start.2 = (s32[1,32,512]{2,1,0:T(8,128)S(1)}, s32[1,32,512]{2,1,0:T(8,128)}, u32[]{:S(2)}) copy-start(s32[1,32,512]{2,1,0:T(8,128)} %map_ref.3) | copy-start | bytes 196612
  41.3 15.5 %all-to-all-start = ((f32[16,3,256]{2,1,0:T(4,128)}), f32[16,3,256]{2,1,0:T(4,128)S(1)}, u32[]{:S(2)}, u32[]{:S(2)}) async-start(f32[16,3,256]{2,1,0:T(4,128)} %get-tuple-element.99), calls=%async_computation | async-start | bytes 131072 | tf_op jit(solution)/shard_map/all_to_all | solution.py:706
